TPU v7x, 128 devices: a whole 4x4x4 slice. The times are simulated.
128 devices in a mesh: expert: 16 (over x, y), head: 8 (over z, core).
Axes of the slice: x: 4, y: 4, z: 4, core: 2. Of those that a mesh axis runs over, the one named last changes fastest.
Arguments:
- table_cells: bfloat16 [8192, 2, 2048], P(('expert', 'head')), may hold values from -8 to 8
- w_query: bfloat16 [2048, 2048], P(None, 'head')
- w_key: bfloat16 [2048, 2048], P(None, 'head')
- w_value: bfloat16 [2048, 2048], P(None, 'head'), may hold values from -0.125 to 0.125
- w_out: bfloat16 [2048, 2048], P('head'), may hold values from -0.125 to 0.125
- norm_gain: bfloat16 [2048], replicated, may hold values from 0.099609375 to 1.8984375
- w_gate: bfloat16 [128, 704, 2048], P(('expert', 'head')), may hold values from -0.125 to 0.125
- w_up: bfloat16 [128, 704, 2048], P(('expert', 'head')), may hold values from -0.125 to 0.125
- w_down: bfloat16 [128, 704, 2048], P(('expert', 'head')), may hold values from -0.15625 to 0.15625
- lengths: int32 [2], replicated, may hold values from 2048 to 8192, as said below
- expert_of_cell: int32 [8192, 2], P(('expert', 'head')), may hold values from 0 to 63, as said below
- slot_of_cell: int32 [8192, 2], P(('expert', 'head')), may hold values from 0 to 3, as said below
Outputs:
- updated_cells: bfloat16 [8192, 2, 2048], P(('expert', 'head'))
Inputs may be any that keep to these rules, and one draw needn't show every extreme that they name: `lengths`: one table in every draw has all 8192 cells. `expert_of_cell`: within the 128 cells of one device (aligned blocks in row-major order), no expert has more than 4 cells, and in every draw one expert has exactly 4 cells in every device's block. `slot_of_cell`: cells of one device with the same expert have distinct slots.
All inputs are finite; a program needn't handle non-finite values.
Results may differ from a plain program's by a relative error of at most 0.014.
Values may be sent and summed in bfloat16 or wider, within the bound.
A program may use at most 128 MiB of HBM per device.

v0:
```python
import math

import jax
import jax.numpy as jnp
from jax import lax
from jax.sharding import PartitionSpec as P

DH = 128


def expert_half(slot_rows, gate_half, up_half, down_half):
    contract_rows = (((1,), (1,)), ((), ()))
    gate_t = lax.dot_general(
        gate_half, slot_rows, contract_rows, preferred_element_type=jnp.float32
    )
    up_t = lax.dot_general(up_half, slot_rows, contract_rows, preferred_element_type=jnp.float32)
    hidden = (jax.nn.silu(gate_t) * up_t).astype(jnp.bfloat16)
    product = lax.dot_general(
        hidden, down_half, (((0,), (0,)), ((), ())), preferred_element_type=jnp.float32
    )
    return product.astype(jnp.bfloat16)


def shards(
    table_cells,
    w_query,
    w_key,
    w_value,
    w_out,
    norm_gain,
    w_gate,
    w_up,
    w_down,
    lengths,
    expert_of_cell,
    slot_of_cell,
):
    cell_count, tables, model_width = table_cells.shape
    head_width = w_query.shape[1]
    head_count = head_width // DH
    score_scale = 1.0 / math.sqrt(DH)
    joined = jnp.concatenate([w_query, w_key, w_value], axis=1)
    shard_rows = lax.all_gather(table_cells, "head", axis=0, tiled=True)
    rows_here = shard_rows.shape[0]
    mixed_rows = jnp.dot(
        shard_rows.reshape(rows_here * tables, model_width),
        joined,
        preferred_element_type=jnp.float32,
    )
    projected = mixed_rows.astype(jnp.bfloat16).reshape(rows_here, tables, 3 * head_width)
    row_cells = projected.shape[0]
    queries = projected[:, :, :head_width].reshape(row_cells, tables, head_count, DH)
    key_rows = projected[:, :, head_width : 2 * head_width]
    value_rows = projected[:, :, 2 * head_width :]
    offset = lax.axis_index("expert") * row_cells
    own_positions = offset + jnp.arange(row_cells, dtype=jnp.int32)
    start_state = (
        jnp.full((tables, head_count, row_cells), -1e30, jnp.float32),
        jnp.zeros((tables, head_count, row_cells), jnp.float32),
        jnp.zeros((tables, head_count, row_cells, DH), jnp.float32),
    )
    key_piece = lax.all_gather(key_rows, "expert", axis=0, tiled=True)
    value_piece = lax.all_gather(value_rows, "expert", axis=0, tiled=True)
    piece_len = key_piece.shape[0]
    block_len = math.gcd(piece_len, 512)
    block_count = piece_len // block_len
    key_blocks = key_piece.reshape(block_count, block_len, tables, head_count, DH)
    value_blocks = value_piece.reshape(block_count, block_len, tables, head_count, DH)
    block_starts = jnp.arange(block_count, dtype=jnp.int32) * block_len

    def step(carried, block_item):
        running_max, running_sum, accum = carried
        key_block, value_block, block_first = block_item
        scores = (
            jnp.einsum("qshd,kshd->shqk", queries, key_block, preferred_element_type=jnp.float32)
            * score_scale
        )
        key_valid = (block_first + jnp.arange(block_len, dtype=jnp.int32))[None, :] < lengths[
            :, None
        ]
        scores = jnp.where(key_valid[:, None, None, :], scores, -jnp.inf)
        new_max = jnp.maximum(running_max, jnp.max(scores, axis=-1))
        factor = jnp.exp(running_max - new_max)
        exp_scores = jnp.exp(scores - new_max[..., None])
        running_sum = running_sum * factor + jnp.sum(exp_scores, axis=-1)
        accum = accum * factor[..., None] + jnp.einsum(
            "shqk,kshd->shqd",
            exp_scores.astype(jnp.bfloat16),
            value_block,
            preferred_element_type=jnp.float32,
        )
        return ((new_max, running_sum, accum), None)

    finished, _ = lax.scan(step, start_state, (key_blocks, value_blocks, block_starts))
    running_max, running_sum, accum = finished
    normalized = accum / running_sum[..., None]
    live = own_positions[None, :] < lengths[:, None]
    normalized = jnp.where(live[:, None, :, None], normalized, 0.0)
    attended = (
        jnp.transpose(normalized, (2, 0, 1, 3))
        .reshape(row_cells, tables, head_width)
        .astype(jnp.bfloat16)
    )
    count_rows = cell_count * lax.axis_size("head")
    product = jnp.dot(
        attended.reshape(count_rows * tables, head_width), w_out, preferred_element_type=jnp.float32
    )
    summed = lax.psum_scatter(
        product.reshape(count_rows, tables, model_width).astype(jnp.bfloat16),
        "head",
        scatter_dimension=0,
        tiled=True,
    ).astype(jnp.float32)
    residual = table_cells.astype(jnp.float32) + summed
    mean_square = jnp.mean(residual * residual, axis=-1, keepdims=True)
    normed = (residual * lax.rsqrt(mean_square + 1e-06) * norm_gain.astype(jnp.float32)).astype(
        jnp.bfloat16
    )
    rows_dev = cell_count * tables
    normed_rows = normed.reshape(rows_dev, model_width)
    expert_count = lax.axis_size("expert") * lax.axis_size("head") // 2
    slot_cap = 2 * max(1, rows_dev // expert_count)
    target = expert_of_cell.reshape(rows_dev) * slot_cap + slot_of_cell.reshape(rows_dev)
    slot_table = (
        jnp.arange(expert_count * slot_cap, dtype=jnp.int32)[:, None] == target[None, :]
    ).astype(jnp.bfloat16)
    send_rows = jnp.dot(slot_table, normed_rows, preferred_element_type=jnp.float32).astype(
        jnp.bfloat16
    )
    gate_half = w_gate[0]
    up_half = w_up[0]
    down_half = w_down[0]
    doubled = jnp.repeat(send_rows.reshape(expert_count, slot_cap, model_width), 2, axis=0)
    received = lax.all_to_all(doubled, ("expert", "head"), split_axis=0, concat_axis=0, tiled=True)
    sources = received.shape[0]
    item_count = received.shape[1]
    flat_rows = received.reshape(sources * item_count, model_width)
    gathered = lax.all_to_all(
        expert_half(flat_rows, gate_half, up_half, down_half).reshape(
            sources, item_count, model_width
        ),
        ("expert", "head"),
        split_axis=0,
        concat_axis=0,
        tiled=True,
    )
    halves = gathered.reshape(expert_count, 2, slot_cap, model_width).astype(jnp.float32)
    combined = (
        (halves[:, 0] + halves[:, 1])
        .astype(jnp.bfloat16)
        .reshape(expert_count * slot_cap, model_width)
    )
    expert_out = lax.dot_general(
        slot_table, combined, (((0,), (0,)), ((), ())), preferred_element_type=jnp.float32
    )
    updated = (residual.reshape(rows_dev, model_width) + expert_out).astype(jnp.bfloat16)
    return updated.reshape(cell_count, tables, model_width)


def solution(mesh):
    placed = (
        P(("expert", "head"), None, None),
        P(None, "head"),
        P(None, "head"),
        P(None, "head"),
        P("head", None),
        P(),
        P(("expert", "head"), None, None),
        P(("expert", "head"), None, None),
        P(("expert", "head"), None, None),
        P(),
        P(("expert", "head"), None),
        P(("expert", "head"), None),
    )
    return jax.shard_map(
        shards,
        mesh=mesh,
        in_specs=placed,
        out_specs=P(("expert", "head"), None, None),
        check_vma=False,
    )
```

profile of v0, /device:TPU:1, one launch (start us, length us, event | category | flops | bytes accessed | tf_op | source)
XLA Modules:
  0.0 631.7 jit_solution(11269988385761301558)
XLA Ops:
  7.3 37.8 %all-gather.4.cloned.1.call-done = bf16[512,2,2048]{2,1,0:T(2,128)(2,1)} async-done(((bf16[64,2,2048]{2,1,0:T(2,128)(2,1)}), bf16[512,2,2048]{2,1,0:T(2,128)(2,1)}) %all-gather.4.cloned.1.call-update) | async-done | bytes 4194320 | tf_op jit(solution)/shard_map/all_gather | solution.py:43
  45.1 7.2 %reshape.135 = bf16[1024,2048]{1,0:T(8,128)(2,1)} reshape(bf16[512,2,2048]{2,1,0:T(2,128)(2,1)} %all-gather.4.cloned.1.call-done) | data formatting | bytes 8388608 | tf_op jit(solution)/shard_map/reshape | solution.py:46
  52.3 7.8 %fusion.33 = bf16[1024,768]{0,1:T(8,128)(2,1)} fusion(bf16[1024,2048]{1,0:T(8,128)(2,1)} %reshape.135, bf16[2048,256]{1,0:T(8,128)(2,1)} %param.17, bf16[2048,256]{1,0:T(8,128)(2,1)} %param.16, bf16[2048,256]{1,0:T(8,128)(2,1)} %param.15), kind=kOutput, calls=%fused_computation.46 | convolution fusion | flops 3231449088 | bytes 8912896 | tf_op jit(solution)/shard_map/dot_general | solution.py:45
  62.7 4.5 reshape.136
  67.2 3.4 fusion.56
  74.5 66.3 %all-gather.6.cloned.1.call-done = bf16[8192,2,256]{2,1,0:T(2,128)(2,1)} async-done(((bf16[512,2,256]{2,1,0:T(2,128)(2,1)}), bf16[8192,2,256]{2,1,0:T(2,128)(2,1)}) %all-gather.6.cloned.1.call-update) | async-done | bytes 8388624 | tf_op jit(solution)/shard_map/all_gather | solution.py:62
  140.8 21.6 %reshape.149 = bf16[16,512,2,2,128]{4,3,2,1,0:T(2,128)(2,1)} reshape(bf16[8192,2,256]{2,1,0:T(2,128)(2,1)} %all-gather.6.cloned.1.call-done) | data formatting | bytes 16777216 | tf_op jit(solution)/shard_map/reshape | solution.py:67
  162.5 50.9 %all-gather.8.cloned.1.call-done = bf16[8192,2,256]{2,1,0:T(2,128)(2,1)} async-done(((bf16[512,2,256]{2,1,0:T(2,128)(2,1)}), bf16[8192,2,256]{2,1,0:T(2,128)(2,1)}) %all-gather.8.cloned.1.call-update) | async-done | bytes 8388624 | tf_op jit(solution)/shard_map/all_gather | solution.py:63
  213.3 21.6 %reshape.150 = bf16[16,512,2,2,128]{4,3,2,1,0:T(2,128)(2,1)} reshape(bf16[8192,2,256]{2,1,0:T(2,128)(2,1)} %all-gather.8.cloned.1.call-done) | data formatting | bytes 16777216 | tf_op jit(solution)/shard_map/reshape | solution.py:68
  234.9 227.6 %while.15 = (s32[]{:T(128)}, f32[2,2,512]{2,1,0:T(2,128)S(1)}, f32[2,2,512]{2,1,0:T(2,128)S(1)}, f32[2,2,512,128]{3,2,1,0:T(8,128)}, s32[16]{0:T(128)S(1)}, /*in...) while((s32[]{:T(128)}, f32[2,2,512]{2,1,0:T(2,128)S(1)}, ...), condition=%wide.region_3.4_spmd.clone, body=%wide.region_0.3_spmd.clone.sunk | while | flops 549203456 | bytes 35266736 | solution.py:94
  241.6 3.3 fusion.73
  245.1 3.8 fusion.75
  255.5 3.3 fusion.73
  259.0 4.1 fusion.75
  269.8 3.3 fusion.73
  273.2 4.1 fusion.75
  284.0 3.3 fusion.73
  287.5 4.1 fusion.75
  298.3 3.3 fusion.73
  301.7 4.1 fusion.75
  312.5 3.3 fusion.73
  316.0 4.1 fusion.75
  326.8 3.3 fusion.73
  330.2 4.1 fusion.75
  341.0 3.3 fusion.73
  344.5 4.1 fusion.75
  355.3 3.3 fusion.73
  358.7 4.1 fusion.75
  373.0 4.1 fusion.75
  383.8 3.3 fusion.73
  387.2 4.1 fusion.75
  401.5 4.1 fusion.75
  415.7 4.1 fusion.75
  426.5 3.3 fusion.73
  430.0 4.1 fusion.75
  440.8 3.3 fusion.73
  444.2 4.1 fusion.75
  455.0 3.3 fusion.73
  458.5 4.1 fusion.75
  466.5 4.5 convolution_convert_fusion
  471.9 34.2 %reduce-scatter.2.cloned.1.call-done = bf16[64,2,2048]{2,0,1:T(8,128)(2,1)} async-done(((bf16[512,2,2048]{2,0,1:T(8,128)(2,1)}), bf16[64,2,2048]{2,0,1:T(8,128)(2,1)}) %reduce-scatter.2.cloned.1.call-update) | async-done | bytes 524304 | tf_op jit(solution)/shard_map/reduce_scatter | solution.py:108
  518.5 40.4 %all_to_all.10 = bf16[128,4,2048]{2,1,0:T(4,128)(2,1)} all-to-all(bf16[128,4,2048]{2,1,0:T(4,128)(2,1)S(1)} %bitcast.83), channel_id=1, replica_groups=mesh['expert'=16,'head'=8] {'expert','head'}, dimensions={0} | all-to-all | bytes 4194304 | tf_op jit(solution)/shard_map/all_to_all | solution.py:134
  558.9 4.0 reshape.144
  562.9 5.3 fusion.36
  568.1 7.6 %convolution_convert_fusion.1 = bf16[512,2048]{1,0:T(8,128)(2,1)} fusion(bf16[1,704,2048]{2,1,0:T(8,128)(2,1)S(1)} %copy-done, bf16[512,2048]{1,0:T(8,128)(2,1)} %reshape.144, bf16[1,704,2048]{2,1,0:T(8,128)(2,1)} %param.21, f32[704,512]{1,0:T(8,128)} %fusion.36), kind=kOutput, calls=%fused_computation.34 | convolution fusion | flops 2956001280 | bytes 11403264 | tf_op jit(solution)/shard_map/dot_general | solution.py:18
  575.8 4.1 reshape.145
  579.9 5.7 all-to-all-start.1
  591.5 24.4 %all-to-all-done.1 = bf16[128,4,2048]{2,1,0:T(4,128)(2,1)} async-done(((bf16[128,4,2048]{2,1,0:T(4,128)(2,1)}), bf16[128,4,2048]{2,1,0:T(4,128)(2,1)}, u32[]{:S(2)}, u32[]{:S(2)}) %all-to-all-start.1) | async-done | bytes 2097184 | tf_op jit(solution)/shard_map/all_to_all | solution.py:138
  (213 shorter events, 159.2 us)
Async XLA Ops:
  6.5 561.6 %copy-start = (bf16[1,704,2048]{2,1,0:T(8,128)(2,1)S(1)}, bf16[1,704,2048]{2,1,0:T(8,128)(2,1)}, u32[]{:S(2)}) copy-start(bf16[1,704,2048]{2,1,0:T(8,128)(2,1)} %param.22) | copy-start | bytes 8650756
  6.5 38.5 %all-gather.4.cloned.1.call-start = ((), (), s32[]{:S(2)}) async-start(), calls=%async_computation.3 | async-start | bytes 4718592 | tf_op jit(solution)/shard_map/all_gather | solution.py:43
  7.3 133.5 %all-gather.6.cloned.1.call-start = ((), (), s32[]{:S(2)}) async-start(), calls=%async_computation.4 | async-start | bytes 8912896 | tf_op jit(solution)/shard_map/all_gather | solution.py:62
  62.7 9.0 %copy-start.3 = (s32[2]{0:T(128)S(1)}, s32[2]{0:T(128)}, u32[]{:S(2)}) copy-start(s32[2]{0:T(128)} %param.23) | copy-start | bytes 28
  70.7 142.7 %all-gather.8.cloned.1.call-start = ((), (), s32[]{:S(2)}) async-start(), calls=%async_computation.5 | async-start | bytes 8912896 | tf_op jit(solution)/shard_map/all_gather | solution.py:63
  71.4 434.7 %reduce-scatter.2.cloned.1.call-start = ((), (), s32[]{:S(2)}) async-start(), calls=%async_computation.6 | async-start | bytes 4718592 | tf_op jit(solution)/shard_map/reduce_scatter | solution.py:108
  241.6 3.4 copy-start.1
  255.5 3.4 copy-start.1
  269.8 3.4 copy-start.1
  284.0 3.4 copy-start.1
  298.3 3.4 copy-start.1
  312.5 3.4 copy-start.1
  326.8 3.4 copy-start.1
  341.0 3.4 copy-start.1
  355.3 3.4 copy-start.1
  369.5 3.4 copy-start.1
  383.8 3.4 copy-start.1
  398.0 3.4 copy-start.1
  412.3 3.4 copy-start.1
  426.5 3.4 copy-start.1
  440.8 3.4 copy-start.1
  455.0 3.4 copy-start.1
  471.0 0.7 copy-start.4
  471.0 0.7 copy-start.5
  471.0 0.7 copy-start.6
  471.0 35.2 %copy-start.2 = (bf16[64,2,2048]{2,1,0:T(2,128)(2,1)S(1)}, bf16[64,2,2048]{2,1,0:T(2,128)(2,1)}, u32[]{:S(2)}) copy-start(bf16[64,2,2048]{2,1,0:T(2,128)(2,1)} %param.14) | copy-start | bytes 1572868
  579.9 36.0 %all-to-all-start.1 = ((bf16[128,4,2048]{2,1,0:T(4,128)(2,1)}), bf16[128,4,2048]{2,1,0:T(4,128)(2,1)}, u32[]{:S(2)}, u32[]{:S(2)}) async-start(bf16[128,4,2048]{2,1,0:T(4,128)(2,1)} %reshape.145), calls=%async_computation.2 | async-start | bytes 4194304 | tf_op jit(solution)/shard_map/all_to_all | solution.py:138
Sparse Core Ops, SparseCore 0:
  9.1 35.9 all-gather.3
  70.8 69.9 all-gather.5
  143.0 70.3 all-gather.7
  471.1 34.9 reduce-scatter.1
where the time goes:
time: 635 us; the launch traced here: 632 us
  waiting for transfers between devices  215 us (34%)
  local copies, waits for them, and re-layouts  146 us (23%)
  matrix products  138 us (22%)
  other arithmetic  73.5 us (12%)
  blocking collectives  40.4 us (6%)
  between operations  13.2 us (2%)
    all_gather x1, waiting for transfers between devices, shards(): key_piece = lax.all_gather(key_rows, 'expert', axis=0, tiled=True)  66.3 us
    dot_general x16, matrix products, step(): jnp.einsum('shqk,kshd->shqd', exp_scores.astype(jnp.bfloat16), value_bloc...  65.2 us
    dynamic_slice x32, local copies, waits for them, and re-layouts, shards(): lax.scan(step, start_state, (key_blocks, value_blocks, block_starts))  52.7 us
    reduce_sum x16, other arithmetic, step(): running_sum = running_sum * factor + jnp.sum(exp_scores, axis=-1)  52.1 us
    all_gather x1, waiting for transfers between devices, shards(): value_piece = lax.all_gather(value_rows, 'expert', axis=0, tiled=True)  50.9 us
    dot_general x16, matrix products, step(): jnp.einsum('qshd,kshd->shqk', queries, key_block, preferred_element_type=...  42.8 us
    all_to_all x1, blocking collectives, shards(): lax.all_to_all(doubled, ('expert', 'head'), split_axis=0, concat_axis=0,...  40.4 us
    all_gather x1, waiting for transfers between devices, shards(): shard_rows = lax.all_gather(table_cells, 'head', axis=0, tiled=True)  37.8 us
  transfers between devices with their start and end apart: 5, of which 5 were waited for; matrix products, arithmetic and copies ran while one was open for 5% of the time, Pallas kernels for 0%

commit v1 on v0

--- a/solution.py
+++ b/solution.py
@@ -1,11 +1,106 @@
+import functools
 import math
 
 import jax
 import jax.numpy as jnp
 from jax import lax
+from jax.experimental import pallas as pl
+from jax.experimental.pallas import tpu as pltpu
+
 from jax.sharding import PartitionSpec as P
 
 DH = 128
+KEY_BLOCK = 512
+
+
+def flash_body(scalars, q_ref, k_ref, v_ref, o_ref, m_ref, l_ref, acc_ref, *, scale, key_block):
+    s = pl.program_id(0)
+    j = pl.program_id(2)
+    last = pl.num_programs(2) - 1
+    length = scalars[s]
+    start = j * key_block
+
+    @pl.when(j == 0)
+    def _():
+        m_ref[...] = jnp.full(m_ref.shape, -1e30, jnp.float32)
+        l_ref[...] = jnp.zeros(l_ref.shape, jnp.float32)
+        acc_ref[...] = jnp.zeros(acc_ref.shape, jnp.float32)
+
+    def update(masked):
+        q = q_ref[...]
+        k = k_ref[...]
+        scores = lax.dot_general(
+            q, k, (((1,), (1,)), ((), ())), preferred_element_type=jnp.float32
+        ) * scale
+        if masked:
+            cols = start + lax.broadcasted_iota(jnp.int32, scores.shape, 1)
+            scores = jnp.where(cols < length, scores, -jnp.inf)
+        m_prev = m_ref[...]
+        m_new = jnp.maximum(m_prev, jnp.max(scores, axis=1, keepdims=True))
+        alpha = jnp.exp(m_prev - m_new)
+        p = jnp.exp(scores - m_new[:, :1])
+        l_ref[...] = alpha * l_ref[...] + jnp.sum(p, axis=1, keepdims=True)
+        acc_ref[...] = acc_ref[...] * alpha + jnp.dot(
+            p.astype(jnp.bfloat16), v_ref[...], preferred_element_type=jnp.float32
+        )
+        m_ref[...] = m_new
+
+    @pl.when(start + key_block <= length)
+    def _():
+        update(False)
+
+    @pl.when(jnp.logical_and(start < length, start + key_block > length))
+    def _():
+        update(True)
+
+    @pl.when(j == last)
+    def _():
+        rows = scalars[2] + lax.broadcasted_iota(jnp.int32, acc_ref.shape, 0)
+        out = acc_ref[...] / l_ref[...]
+        o_ref[...] = jnp.where(rows < length, out, 0.0).astype(o_ref.dtype)
+
+
+def flash_attention(scalars, q_all, kv_all, heads, scale):
+    rows = q_all.shape[0]
+    keys = kv_all.shape[0]
+    tables = scalars.shape[0] - 1
+    key_block = KEY_BLOCK
+    nk = keys // key_block
+
+    def clamp(j, sc, s):
+        return jnp.minimum(j, (sc[s] - 1) // key_block)
+
+    grid_spec = pltpu.PrefetchScalarGridSpec(
+        num_scalar_prefetch=1,
+        grid=(tables, heads, nk),
+        in_specs=[
+            pl.BlockSpec((rows, DH), lambda s, h, j, sc: (0, s * heads + h)),
+            pl.BlockSpec((key_block, DH), lambda s, h, j, sc: (clamp(j, sc, s), s * 2 * heads + h)),
+            pl.BlockSpec(
+                (key_block, DH), lambda s, h, j, sc: (clamp(j, sc, s), s * 2 * heads + heads + h)
+            ),
+        ],
+        out_specs=pl.BlockSpec((rows, DH), lambda s, h, j, sc: (0, s * heads + h)),
+        scratch_shapes=[
+            pltpu.VMEM((rows, DH), jnp.float32),
+            pltpu.VMEM((rows, DH), jnp.float32),
+            pltpu.VMEM((rows, DH), jnp.float32),
+        ],
+    )
+    flops = 4 * tables * heads * rows * keys * DH
+    return pl.pallas_call(
+        functools.partial(flash_body, scale=scale, key_block=key_block),
+        grid_spec=grid_spec,
+        out_shape=jax.ShapeDtypeStruct((rows, tables * heads * DH), jnp.bfloat16),
+        compiler_params=pltpu.CompilerParams(
+            dimension_semantics=("arbitrary", "arbitrary", "arbitrary")
+        ),
+        cost_estimate=pl.CostEstimate(
+            flops=flops,
+            transcendentals=tables * heads * rows * keys,
+            bytes_accessed=2 * (q_all.size * 2 + kv_all.size),
+        ),
+    )(scalars, q_all, kv_all, kv_all)
 
 
 def expert_half(slot_rows, gate_half, up_half, down_half):
@@ -39,68 +134,26 @@
     head_width = w_query.shape[1]
     head_count = head_width // DH
     score_scale = 1.0 / math.sqrt(DH)
-    joined = jnp.concatenate([w_query, w_key, w_value], axis=1)
     shard_rows = lax.all_gather(table_cells, "head", axis=0, tiled=True)
-    rows_here = shard_rows.shape[0]
-    mixed_rows = jnp.dot(
-        shard_rows.reshape(rows_here * tables, model_width),
-        joined,
-        preferred_element_type=jnp.float32,
-    )
-    projected = mixed_rows.astype(jnp.bfloat16).reshape(rows_here, tables, 3 * head_width)
-    row_cells = projected.shape[0]
-    queries = projected[:, :, :head_width].reshape(row_cells, tables, head_count, DH)
-    key_rows = projected[:, :, head_width : 2 * head_width]
-    value_rows = projected[:, :, 2 * head_width :]
+    row_cells = shard_rows.shape[0]
+    flat_rows = shard_rows.reshape(row_cells * tables, model_width)
+    q_all = (
+        jnp.dot(flat_rows, w_query, preferred_element_type=jnp.float32)
+        .astype(jnp.bfloat16)
+        .reshape(row_cells, tables * head_width)
+    )
+    kv_weight = jnp.concatenate([w_key, w_value], axis=1)
+    kv_rows = (
+        jnp.dot(flat_rows, kv_weight, preferred_element_type=jnp.float32)
+        .astype(jnp.bfloat16)
+        .reshape(row_cells, tables * 2 * head_width)
+    )
+    kv_all = lax.all_gather(kv_rows, "expert", axis=0, tiled=True)
     offset = lax.axis_index("expert") * row_cells
-    own_positions = offset + jnp.arange(row_cells, dtype=jnp.int32)
-    start_state = (
-        jnp.full((tables, head_count, row_cells), -1e30, jnp.float32),
-        jnp.zeros((tables, head_count, row_cells), jnp.float32),
-        jnp.zeros((tables, head_count, row_cells, DH), jnp.float32),
-    )
-    key_piece = lax.all_gather(key_rows, "expert", axis=0, tiled=True)
-    value_piece = lax.all_gather(value_rows, "expert", axis=0, tiled=True)
-    piece_len = key_piece.shape[0]
-    block_len = math.gcd(piece_len, 512)
-    block_count = piece_len // block_len
-    key_blocks = key_piece.reshape(block_count, block_len, tables, head_count, DH)
-    value_blocks = value_piece.reshape(block_count, block_len, tables, head_count, DH)
-    block_starts = jnp.arange(block_count, dtype=jnp.int32) * block_len
-
-    def step(carried, block_item):
-        running_max, running_sum, accum = carried
-        key_block, value_block, block_first = block_item
-        scores = (
-            jnp.einsum("qshd,kshd->shqk", queries, key_block, preferred_element_type=jnp.float32)
-            * score_scale
-        )
-        key_valid = (block_first + jnp.arange(block_len, dtype=jnp.int32))[None, :] < lengths[
-            :, None
-        ]
-        scores = jnp.where(key_valid[:, None, None, :], scores, -jnp.inf)
-        new_max = jnp.maximum(running_max, jnp.max(scores, axis=-1))
-        factor = jnp.exp(running_max - new_max)
-        exp_scores = jnp.exp(scores - new_max[..., None])
-        running_sum = running_sum * factor + jnp.sum(exp_scores, axis=-1)
-        accum = accum * factor[..., None] + jnp.einsum(
-            "shqk,kshd->shqd",
-            exp_scores.astype(jnp.bfloat16),
-            value_block,
-            preferred_element_type=jnp.float32,
-        )
-        return ((new_max, running_sum, accum), None)
-
-    finished, _ = lax.scan(step, start_state, (key_blocks, value_blocks, block_starts))
-    running_max, running_sum, accum = finished
-    normalized = accum / running_sum[..., None]
-    live = own_positions[None, :] < lengths[:, None]
-    normalized = jnp.where(live[:, None, :, None], normalized, 0.0)
-    attended = (
-        jnp.transpose(normalized, (2, 0, 1, 3))
-        .reshape(row_cells, tables, head_width)
-        .astype(jnp.bfloat16)
-    )
+    scalars = jnp.concatenate(
+        [lengths.astype(jnp.int32), jnp.reshape(offset, (1,)).astype(jnp.int32)]
+    )
+    attended = flash_attention(scalars, q_all, kv_all, head_count, score_scale)
     count_rows = cell_count * lax.axis_size("head")
     product = jnp.dot(
         attended.reshape(count_rows * tables, head_width), w_out, preferred_element_type=jnp.float32

time: 635 us -> 396 us (0.62)
  local copies, waits for them, and re-layouts: 146 us -> 37.1 us
  matrix products: 138 us -> 31.8 us
  other arithmetic: 73.5 us -> 8.47 us
  Pallas kernels: 0 us -> 55.8 us
  waiting for transfers between devices: 215 us -> 202 us
    dot_general x33 -> x2, matrix products: 116 us -> 9.96 us  [the longest x1 6.22 us: shards(): jnp.dot(flat_rows, kv_weight, preferred_element_type=jnp.float32)]
    pallas_call x0 -> x1, Pallas kernels: none -> 55.8 us  [flash_attention(): pl.pallas_call(functools.partial(flash_body, scale=scale, key_block=key_b...]
    dynamic_slice x32 -> x0, local copies, waits for them, and re-layouts: 52.7 us -> none  [shards(): lax.scan(step, start_state, (key_blocks, value_blocks, block_starts))]
    reduce_sum x16 -> x0, other arithmetic: 52.1 us -> none  [step(): running_sum = running_sum * factor + jnp.sum(exp_scores, axis=-1)]
    reshape x4 -> x3, local copies, waits for them, and re-layouts: 55 us -> 10.4 us  [the longest x1 7.19 us: shards(): flat_rows = shard_rows.reshape(row_cells * tables, model_width)]
    all_gather x2 -> x1, waiting for transfers between devices: 117 us -> 105 us  [shards(): kv_all = lax.all_gather(kv_rows, 'expert', axis=0, tiled=True)]
    add x33 -> x0, other arithmetic: 10.8 us -> none  [the longest x16 10.3 us: step(): block_first + jnp.arange(block_len, dtype=jnp.int32)]
  transfers between devices with their start and end apart: 5 -> 4, of which waited for: 5 -> 4; matrix products, arithmetic and copies ran while one was open for 5% -> 3% of each run, Pallas kernels for 0% -> 0%
where the time goes in v1:
time: 396 us; the launch traced here: 395 us
  waiting for transfers between devices  202 us (51%)
  Pallas kernels  55.8 us (14%)
  blocking collectives  40.4 us (10%)
  local copies, waits for them, and re-layouts  37.1 us (9%)
  matrix products  31.8 us (8%)
  between operations  13.2 us (3%)
  other arithmetic  8.47 us (2%)
  starting transfers between devices  5.75 us (1%)
    all_gather x1, waiting for transfers between devices, shards(): kv_all = lax.all_gather(kv_rows, 'expert', axis=0, tiled=True)  105 us
    pallas_call x1, Pallas kernels, flash_attention(): pl.pallas_call(functools.partial(flash_body, scale=scale, key_block=key_b...  55.8 us
    all_to_all x1, blocking collectives, shards(): lax.all_to_all(doubled, ('expert', 'head'), split_axis=0, concat_axis=0,...  40.4 us
    all_gather x1, waiting for transfers between devices, shards(): shard_rows = lax.all_gather(table_cells, 'head', axis=0, tiled=True)  37.8 us
    reduce_scatter x1, waiting for transfers between devices, shards(): lax.psum_scatter(product.reshape(count_rows, tables, model_width).astype(...  34.2 us
    all_to_all x1, waiting for transfers between devices, shards(): lax.all_to_all(expert_half(flat_rows, gate_half, up_half, down_half).resh...  24.4 us
  transfers between devices with their start and end apart: 4, of which 4 were waited for; matrix products, arithmetic and copies ran while one was open for 3% of the time, Pallas kernels for 0%

profile of v1, /device:TPU:1, one launch (start us, length us, event | category | flops | bytes accessed | tf_op | source)
XLA Modules:
  0.0 394.9 jit_solution(18324075434810539000)
XLA Ops:
  6.5 0.0 copy-start
  6.5 0.0 all-gather.3.cloned.1.call-start
  6.5 0.7 all-gather.3.cloned.1.call-update
  7.3 0.0 all-gather.5.cloned.1.call-start
  7.3 37.8 %all-gather.3.cloned.1.call-done = bf16[512,2,2048]{2,1,0:T(2,128)(2,1)} async-done(((bf16[64,2,2048]{2,1,0:T(2,128)(2,1)}), bf16[512,2,2048]{2,1,0:T(2,128)(2,1)}) %all-gather.3.cloned.1.call-update) | async-done | bytes 4194320 | tf_op jit(solution)/shard_map/all_gather | solution.py:137
  45.1 7.2 %reshape.70 = bf16[1024,2048]{1,0:T(8,128)(2,1)} reshape(bf16[512,2,2048]{2,1,0:T(2,128)(2,1)} %all-gather.3.cloned.1.call-done) | data formatting | bytes 8388608 | tf_op jit(solution)/shard_map/reshape | solution.py:139
  52.3 6.2 %fusion.26 = bf16[1024,512]{0,1:T(8,128)(2,1)} fusion(bf16[1024,2048]{1,0:T(8,128)(2,1)} %reshape.70, bf16[2048,256]{1,0:T(8,128)(2,1)} %param.15, bf16[2048,256]{1,0:T(8,128)(2,1)} %param.14), kind=kOutput, calls=%fused_computation.21 | convolution fusion | flops 2152202240 | bytes 7340032 | tf_op jit(solution)/shard_map/dot_general | solution.py:147
  58.5 2.3 copy.24
  60.8 2.2 reshape.72
  63.0 0.0 all-gather.5.cloned.1.call-update
  63.0 0.0 reduce-scatter.2.cloned.1.call-start
  63.1 0.0 copy-done.5
  63.1 0.6 pad_add_fusion.scalars
  63.7 3.7 convolution_convert_fusion.3
  67.4 1.0 reshape.71.q_ref
  68.4 105.3 %all-gather.5.cloned.1.call-done.k_ref.v_ref = bf16[8192,1024]{1,0:T(8,128)(2,1)} async-done(((bf16[512,1024]{1,0:T(8,128)(2,1)}), bf16[8192,1024]{1,0:T(8,128)(2,1)}) %all-gather.5.cloned.1.call-update) | async-done | bytes 16777232 | tf_op jit(solution)/shard_map/all_gather | solution.py:151
  173.7 55.8 %shard_map.118 = bf16[512,512]{1,0:T(8,128)(2,1)} custom-call(s32[3]{0:T(128)} %pad_add_fusion.scalars, bf16[512,512]{1,0:T(8,128)(2,1)} %reshape.71.q_ref, bf16[8192,1024]{1,0:T(8,128)(2,1)} %all-gather.5.cloned.1.call-done.k_ref.v_ref, bf16[8192,1024]{1,0:T(8,128)(2,1)} %all-gather.5.cloned.1.call-done.k_ref.v_ref), custom_call_target="tpu_custom_call" | custom-call | flops 8589934592 | bytes 17825792 | tf_op jit(solution)/shard_map/pallas_call | solution.py:91
  229.5 4.6 %convolution_convert_fusion = bf16[512,2,2048]{2,0,1:T(8,128)(2,1)} fusion(bf16[256,2048]{1,0:T(8,128)(2,1)} %param.16, bf16[64,2,8,256]{3,2,1,0:T(8,128)(2,1)} %bitcast.50), kind=kOutput, calls=%fused_computation | convolution fusion | flops 1075838976 | bytes 5767168 | tf_op jit(solution)/shard_map/dot_general | solution.py:158
  234.2 0.0 reduce-scatter.2.cloned.1.call-update
  234.2 0.6 copy-done.2
  234.8 0.0 copy-done.3
  234.8 0.0 copy-done.4
  234.9 0.1 copy.27
  235.0 0.1 add.40
  235.1 34.2 %reduce-scatter.2.cloned.1.call-done = bf16[64,2,2048]{2,0,1:T(8,128)(2,1)} async-done(((bf16[512,2,2048]{2,0,1:T(8,128)(2,1)}), bf16[64,2,2048]{2,0,1:T(8,128)(2,1)}) %reduce-scatter.2.cloned.1.call-update) | async-done | bytes 524304 | tf_op jit(solution)/shard_map/reduce_scatter | solution.py:161
  269.3 0.0 copy-done.1
  269.3 1.3 multiply_reduce_fusion
  270.6 2.4 multiply_convert_fusion
  273.0 0.5 copy.28
  273.5 1.0 reshape.74
  274.5 2.4 convolution_convert_fusion.2
  277.0 2.3 reshape.75
  279.2 2.5 broadcast_in_dim.2
  281.7 40.4 %all_to_all.10 = bf16[128,4,2048]{2,1,0:T(4,128)(2,1)} all-to-all(bf16[128,4,2048]{2,1,0:T(4,128)(2,1)S(1)} %bitcast.49), channel_id=1, replica_groups=mesh['expert'=16,'head'=8] {'expert','head'}, dimensions={0} | all-to-all | bytes 4194304 | tf_op jit(solution)/shard_map/all_to_all | solution.py:187
  322.1 4.0 %reshape.77 = bf16[512,2048]{1,0:T(8,128)(2,1)} reshape(bf16[128,4,2048]{2,1,0:T(4,128)(2,1)} %all_to_all.10) | data formatting | bytes 4194304 | tf_op jit(solution)/shard_map/reshape | solution.py:190
  326.1 5.3 %fusion.14 = f32[704,512]{1,0:T(8,128)} fusion(bf16[512,2048]{1,0:T(8,128)(2,1)} %reshape.77, bf16[1,704,2048]{2,1,0:T(8,128)(2,1)} %param.18), kind=kOutput, calls=%fused_computation.17 | convolution fusion | flops 1476395008 | bytes 6422528 | tf_op jit(solution)/shard_map/dot_general | solution.py:108
  331.4 0.0 copy-done
  331.4 7.6 %convolution_convert_fusion.1 = bf16[512,2048]{1,0:T(8,128)(2,1)} fusion(bf16[1,704,2048]{2,1,0:T(8,128)(2,1)S(1)} %copy-done, bf16[512,2048]{1,0:T(8,128)(2,1)} %reshape.77, bf16[1,704,2048]{2,1,0:T(8,128)(2,1)} %param.19, f32[704,512]{1,0:T(8,128)} %fusion.14), kind=kOutput, calls=%fused_computation.1 | convolution fusion | flops 2956001280 | bytes 11403264 | tf_op jit(solution)/shard_map/dot_general | solution.py:113
  339.0 4.1 %reshape.78 = bf16[128,4,2048]{2,1,0:T(4,128)(2,1)} reshape(bf16[512,2048]{1,0:T(8,128)(2,1)} %convolution_convert_fusion.1) | data formatting | bytes 4194304 | tf_op jit(solution)/shard_map/reshape | solution.py:192
  343.1 5.7 %all-to-all-start.1 = ((bf16[128,4,2048]{2,1,0:T(4,128)(2,1)}), bf16[128,4,2048]{2,1,0:T(4,128)(2,1)}, u32[]{:S(2)}, u32[]{:S(2)}) async-start(bf16[128,4,2048]{2,1,0:T(4,128)(2,1)} %reshape.78), calls=%async_computation.2 | async-start | bytes 4194304 | tf_op jit(solution)/shard_map/all_to_all | solution.py:191
  348.8 3.0 copy.26
  351.8 2.9 reshape.73
  354.7 24.4 %all-to-all-done.1 = bf16[128,4,2048]{2,1,0:T(4,128)(2,1)} async-done(((bf16[128,4,2048]{2,1,0:T(4,128)(2,1)}), bf16[128,4,2048]{2,1,0:T(4,128)(2,1)}, u32[]{:S(2)}, u32[]{:S(2)}) %all-to-all-start.1) | async-done | bytes 2097184 | tf_op jit(solution)/shard_map/all_to_all | solution.py:191
  379.1 2.2 convert.1
  381.3 1.9 fusion.6
  383.2 2.1 convert_element_type.64
  385.4 1.9 fusion.5
  387.3 1.1 reshape.79
  (8 shorter events, 0.0 us)
Async XLA Ops:
  6.5 324.8 %copy-start = (bf16[1,704,2048]{2,1,0:T(8,128)(2,1)S(1)}, bf16[1,704,2048]{2,1,0:T(8,128)(2,1)}, u32[]{:S(2)}) copy-start(bf16[1,704,2048]{2,1,0:T(8,128)(2,1)} %param.20) | copy-start | bytes 8650756
  6.5 38.5 %all-gather.3.cloned.1.call-start = ((), (), s32[]{:S(2)}) async-start(), calls=%async_computation.3 | async-start | bytes 4718592 | tf_op jit(solution)/shard_map/all_gather | solution.py:137
  7.3 166.4 %all-gather.5.cloned.1.call-start = ((), (), s32[]{:S(2)}) async-start(), calls=%async_computation.4 | async-start | bytes 17825792 | tf_op jit(solution)/shard_map/all_gather | solution.py:151
  60.8 2.3 copy-start.5
  63.0 206.3 %reduce-scatter.2.cloned.1.call-start = ((), (), s32[]{:S(2)}) async-start(), calls=%async_computation.5 | async-start | bytes 4718592 | tf_op jit(solution)/shard_map/reduce_scatter | solution.py:161
  234.1 0.7 copy-start.2
  234.1 0.7 copy-start.3
  234.1 0.7 copy-start.4
  234.1 35.2 %copy-start.1 = (bf16[64,2,2048]{2,1,0:T(2,128)(2,1)S(1)}, bf16[64,2,2048]{2,1,0:T(2,128)(2,1)}, u32[]{:S(2)}) copy-start(bf16[64,2,2048]{2,1,0:T(2,128)(2,1)} %param.12) | copy-start | bytes 1572868
  343.1 36.0 %all-to-all-start.1 = ((bf16[128,4,2048]{2,1,0:T(4,128)(2,1)}), bf16[128,4,2048]{2,1,0:T(4,128)(2,1)}, u32[]{:S(2)}, u32[]{:S(2)}) async-start(bf16[128,4,2048]{2,1,0:T(4,128)(2,1)} %reshape.78), calls=%async_computation.2 | async-start | bytes 4194304 | tf_op jit(solution)/shard_map/all_to_all | solution.py:191
Sparse Core Ops, SparseCore 0:
  9.1 35.9 all-gather.2
  63.1 110.5 all-gather.4
  234.3 34.9 reduce-scatter.1

commit v2 on v1

--- a/solution.py
+++ b/solution.py
@@ -14,10 +14,9 @@
 
 
 def flash_body(scalars, q_ref, k_ref, v_ref, o_ref, m_ref, l_ref, acc_ref, *, scale, key_block):
-    s = pl.program_id(0)
-    j = pl.program_id(2)
-    last = pl.num_programs(2) - 1
-    length = scalars[s]
+    j = pl.program_id(1)
+    last = pl.num_programs(1) - 1
+    length = scalars[0]
     start = j * key_block
 
     @pl.when(j == 0)
@@ -55,50 +54,45 @@
 
     @pl.when(j == last)
     def _():
-        rows = scalars[2] + lax.broadcasted_iota(jnp.int32, acc_ref.shape, 0)
+        rows = scalars[1] + lax.broadcasted_iota(jnp.int32, acc_ref.shape, 0)
         out = acc_ref[...] / l_ref[...]
         o_ref[...] = jnp.where(rows < length, out, 0.0).astype(o_ref.dtype)
 
 
-def flash_attention(scalars, q_all, kv_all, heads, scale):
+def flash_attention(scalars, q_all, kv_all, heads, scale, table):
     rows = q_all.shape[0]
     keys = kv_all.shape[0]
-    tables = scalars.shape[0] - 1
     key_block = KEY_BLOCK
     nk = keys // key_block
 
-    def clamp(j, sc, s):
-        return jnp.minimum(j, (sc[s] - 1) // key_block)
+    def clamp(j, sc):
+        return jnp.minimum(j, (sc[0] - 1) // key_block)
 
     grid_spec = pltpu.PrefetchScalarGridSpec(
         num_scalar_prefetch=1,
-        grid=(tables, heads, nk),
+        grid=(heads, nk),
         in_specs=[
-            pl.BlockSpec((rows, DH), lambda s, h, j, sc: (0, s * heads + h)),
-            pl.BlockSpec((key_block, DH), lambda s, h, j, sc: (clamp(j, sc, s), s * 2 * heads + h)),
-            pl.BlockSpec(
-                (key_block, DH), lambda s, h, j, sc: (clamp(j, sc, s), s * 2 * heads + heads + h)
-            ),
+            pl.BlockSpec((rows, DH), lambda h, j, sc: (0, table * heads + h)),
+            pl.BlockSpec((key_block, DH), lambda h, j, sc: (clamp(j, sc), h)),
+            pl.BlockSpec((key_block, DH), lambda h, j, sc: (clamp(j, sc), heads + h)),
         ],
-        out_specs=pl.BlockSpec((rows, DH), lambda s, h, j, sc: (0, s * heads + h)),
+        out_specs=pl.BlockSpec((rows, DH), lambda h, j, sc: (0, h)),
         scratch_shapes=[
             pltpu.VMEM((rows, DH), jnp.float32),
             pltpu.VMEM((rows, DH), jnp.float32),
             pltpu.VMEM((rows, DH), jnp.float32),
         ],
     )
-    flops = 4 * tables * heads * rows * keys * DH
+    flops = 4 * heads * rows * keys * DH
     return pl.pallas_call(
         functools.partial(flash_body, scale=scale, key_block=key_block),
         grid_spec=grid_spec,
-        out_shape=jax.ShapeDtypeStruct((rows, tables * heads * DH), jnp.bfloat16),
-        compiler_params=pltpu.CompilerParams(
-            dimension_semantics=("arbitrary", "arbitrary", "arbitrary")
-        ),
+        out_shape=jax.ShapeDtypeStruct((rows, heads * DH), jnp.bfloat16),
+        compiler_params=pltpu.CompilerParams(dimension_semantics=("arbitrary", "arbitrary")),
         cost_estimate=pl.CostEstimate(
             flops=flops,
-            transcendentals=tables * heads * rows * keys,
-            bytes_accessed=2 * (q_all.size * 2 + kv_all.size),
+            transcendentals=heads * rows * keys,
+            bytes_accessed=2 * (rows * heads * DH * 2 + kv_all.size),
         ),
     )(scalars, q_all, kv_all, kv_all)
 
@@ -148,22 +142,23 @@
         .astype(jnp.bfloat16)
         .reshape(row_cells, tables * 2 * head_width)
     )
-    kv_all = lax.all_gather(kv_rows, "expert", axis=0, tiled=True)
     offset = lax.axis_index("expert") * row_cells
-    scalars = jnp.concatenate(
-        [lengths.astype(jnp.int32), jnp.reshape(offset, (1,)).astype(jnp.int32)]
-    )
-    attended = flash_attention(scalars, q_all, kv_all, head_count, score_scale)
     count_rows = cell_count * lax.axis_size("head")
-    product = jnp.dot(
-        attended.reshape(count_rows * tables, head_width), w_out, preferred_element_type=jnp.float32
-    )
-    summed = lax.psum_scatter(
-        product.reshape(count_rows, tables, model_width).astype(jnp.bfloat16),
-        "head",
-        scatter_dimension=0,
-        tiled=True,
-    ).astype(jnp.float32)
+    summed_tables = []
+    for table in range(tables):
+        scalars = jnp.stack(
+            [lengths[table].astype(jnp.int32), jnp.asarray(offset, jnp.int32)]
+        )
+        kv_piece = kv_rows[:, table * 2 * head_width : (table + 1) * 2 * head_width]
+        kv_all = lax.all_gather(kv_piece, "expert", axis=0, tiled=True)
+        attended = flash_attention(scalars, q_all, kv_all, head_count, score_scale, table)
+        product = jnp.dot(attended, w_out, preferred_element_type=jnp.float32)
+        summed_tables.append(
+            lax.psum_scatter(
+                product.astype(jnp.bfloat16), "head", scatter_dimension=0, tiled=True
+            ).astype(jnp.float32)
+        )
+    summed = jnp.stack(summed_tables, axis=1)
     residual = table_cells.astype(jnp.float32) + summed
     mean_square = jnp.mean(residual * residual, axis=-1, keepdims=True)
     normed = (residual * lax.rsqrt(mean_square + 1e-06) * norm_gain.astype(jnp.float32)).astype(

time: 396 us -> 403 us (1.018)
  Pallas kernels: 55.8 us -> 61.3 us
  waiting for transfers between devices: 202 us -> 197 us
    pallas_call x1 -> x2, Pallas kernels: 55.8 us -> 61.3 us  [flash_attention(): pl.pallas_call(functools.partial(flash_body, scale=scale, key_block=key_b...]
    reduce_scatter x1 -> x2, waiting for transfers between devices: 34.2 us -> 30.3 us  [shards(): lax.psum_scatter(product.astype(jnp.bfloat16), 'head', scatter_dimension=...]
    all_gather x1 -> x2, waiting for transfers between devices: 105 us -> 103 us  [shards(): kv_all = lax.all_gather(kv_piece, 'expert', axis=0, tiled=True)]
  transfers between devices with their start and end apart: 4 -> 6, of which waited for: 4 -> 5; matrix products, arithmetic and copies ran while one was open for 3% -> 5% of each run, Pallas kernels for 0% -> 15%
where the time goes in v2:
time: 403 us; the launch traced here: 402 us
  waiting for transfers between devices  197 us (49%)
  Pallas kernels  61.3 us (15%)
  blocking collectives  40.6 us (10%)
  local copies, waits for them, and re-layouts  39.3 us (10%)
  matrix products  34 us (8%)
  between operations  13.3 us (3%)
  other arithmetic  10.2 us (3%)
  starting transfers between devices  6.02 us (1%)
    all_gather x2, waiting for transfers between devices, shards(): kv_all = lax.all_gather(kv_piece, 'expert', axis=0, tiled=True)  103 us
    pallas_call x2, Pallas kernels, flash_attention(): pl.pallas_call(functools.partial(flash_body, scale=scale, key_block=key_b...  61.3 us
    all_to_all x1, blocking collectives, shards(): lax.all_to_all(doubled, ('expert', 'head'), split_axis=0, concat_axis=0,...  40.6 us
    all_gather x1, waiting for transfers between devices, shards(): shard_rows = lax.all_gather(table_cells, 'head', axis=0, tiled=True)  37.8 us
    reduce_scatter x2, waiting for transfers between devices, shards(): lax.psum_scatter(product.astype(jnp.bfloat16), 'head', scatter_dimension=...  30.3 us
    all_to_all x1, waiting for transfers between devices, shards(): lax.all_to_all(expert_half(flat_rows, gate_half, up_half, down_half).resh...  24.4 us
  transfers between devices with their start and end apart: 6, of which 5 were waited for; matrix products, arithmetic and copies ran while one was open for 5% of the time, Pallas kernels for 15%

profile of v2, /device:TPU:1, one launch (start us, length us, event | category | flops | bytes accessed | tf_op | source)
XLA Modules:
  0.0 401.5 jit_solution(18199143806560926420)
XLA Ops:
  6.5 0.7 all-gather.4.cloned.1.call-update
  7.3 0.0 all-gather.8.cloned.1.call-start
  7.3 37.8 %all-gather.4.cloned.1.call-done = bf16[512,2,2048]{2,1,0:T(2,128)(2,1)} async-done(((bf16[64,2,2048]{2,1,0:T(2,128)(2,1)}), bf16[512,2,2048]{2,1,0:T(2,128)(2,1)}) %all-gather.4.cloned.1.call-update) | async-done | bytes 4194320 | tf_op jit(solution)/shard_map/all_gather | solution.py:131
  45.1 7.2 %reshape.62 = bf16[1024,2048]{1,0:T(8,128)(2,1)} reshape(bf16[512,2,2048]{2,1,0:T(2,128)(2,1)} %all-gather.4.cloned.1.call-done) | data formatting | bytes 8388608 | tf_op jit(solution)/shard_map/reshape | solution.py:133
  52.3 6.2 %fusion.26 = bf16[1024,512]{0,1:T(8,128)(2,1)} fusion(bf16[1024,2048]{1,0:T(8,128)(2,1)} %reshape.62, bf16[2048,256]{1,0:T(8,128)(2,1)} %param.15, bf16[2048,256]{1,0:T(8,128)(2,1)} %param.14), kind=kOutput, calls=%fused_computation.22 | convolution fusion | flops 2152202240 | bytes 7340032 | tf_op jit(solution)/shard_map/dot_general | solution.py:141
  58.5 2.3 copy.22
  60.8 2.2 reshape.64
  63.0 2.3 fusion.36
  65.3 0.0 all-gather.6.cloned.1.call-start
  65.3 0.7 all-gather.6.cloned.1.call-update
  66.0 0.0 reduce-scatter.5.cloned.1.call-start
  66.1 0.6 fusion.37
  66.7 1.2 pad_add_fusion.1.scalars
  67.9 3.7 convolution_convert_fusion.4
  71.6 1.0 reshape.63.q_ref
  72.6 62.8 %all-gather.8.cloned.1.call-done.k_ref.v_ref = bf16[8192,512]{1,0:T(8,128)(2,1)} async-done(((bf16[512,512]{1,0:T(8,128)(2,1)}), bf16[8192,512]{1,0:T(8,128)(2,1)}) %all-gather.8.cloned.1.call-update) | async-done | bytes 8388624 | tf_op jit(solution)/shard_map/all_gather | solution.py:153
  135.4 27.6 %shard_map.119 = bf16[512,256]{1,0:T(8,128)(2,1)} custom-call(s32[2]{0:T(128)} %pad_add_fusion.1.scalars, bf16[512,512]{1,0:T(8,128)(2,1)} %reshape.63.q_ref, bf16[8192,512]{1,0:T(8,128)(2,1)} %all-gather.8.cloned.1.call-done.k_ref.v_ref, bf16[8192,512]{1,0:T(8,128)(2,1)} %all-gather.8.cloned.1.call-done.k_ref.v_ref), custom_call_target="tpu_custom_call" | custom-call | flops 4294967296 | bytes 8912896 | tf_op jit(solution)/shard_map/pallas_call | solution.py:87
  163.0 3.4 convolution_convert_fusion
  166.4 0.2 reduce-scatter.3.cloned.1.call-start
  166.7 1.2 pad_add_fusion.scalars
  167.9 40.1 %all-gather.6.cloned.1.call-done.k_ref.v_ref = bf16[8192,512]{1,0:T(8,128)(2,1)} async-done(((bf16[512,512]{1,0:T(8,128)(2,1)}), bf16[8192,512]{1,0:T(8,128)(2,1)}) %all-gather.6.cloned.1.call-update) | async-done | bytes 8388624 | tf_op jit(solution)/shard_map/all_gather | solution.py:153
  208.0 33.7 %shard_map.118 = bf16[512,256]{1,0:T(8,128)(2,1)} custom-call(s32[2]{0:T(128)} %pad_add_fusion.scalars, bf16[512,512]{1,0:T(8,128)(2,1)} %reshape.63.q_ref, bf16[8192,512]{1,0:T(8,128)(2,1)} %all-gather.6.cloned.1.call-done.k_ref.v_ref, bf16[8192,512]{1,0:T(8,128)(2,1)} %all-gather.6.cloned.1.call-done.k_ref.v_ref), custom_call_target="tpu_custom_call" | custom-call | flops 4294967296 | bytes 8912896 | tf_op jit(solution)/shard_map/pallas_call | solution.py:87
  241.7 3.4 convolution_convert_fusion.1
  245.2 0.1 copy.24
  245.3 0.1 add.42
  245.5 0.0 reduce-scatter.5.cloned.1.call-done
  245.5 30.3 %reduce-scatter.3.cloned.1.call-done = bf16[64,2048]{1,0:T(8,128)(2,1)} async-done(((bf16[512,2048]{1,0:T(8,128)(2,1)}), bf16[64,2048]{1,0:T(8,128)(2,1)}) %reduce-scatter.3.cloned.1.call-update) | async-done | bytes 262160 | tf_op jit(solution)/shard_map/reduce_scatter | solution.py:157
  275.8 1.3 multiply_reduce_fusion
  277.1 2.3 multiply_convert_fusion
  279.4 0.5 copy.25
  280.0 1.0 reshape.66
  280.9 2.5 convolution_convert_fusion.3
  283.4 2.3 reshape.67
  285.7 2.5 broadcast_in_dim.2
  288.1 40.6 %all_to_all.10 = bf16[128,4,2048]{2,1,0:T(4,128)(2,1)} all-to-all(bf16[128,4,2048]{2,1,0:T(4,128)(2,1)S(1)} %bitcast.48), channel_id=1, replica_groups=mesh['expert'=16,'head'=8] {'expert','head'}, dimensions={0} | all-to-all | bytes 4194304 | tf_op jit(solution)/shard_map/all_to_all | solution.py:182
  328.7 4.0 reshape.69
  332.7 5.3 %fusion.14 = f32[704,512]{1,0:T(8,128)} fusion(bf16[512,2048]{1,0:T(8,128)(2,1)} %reshape.69, bf16[1,704,2048]{2,1,0:T(8,128)(2,1)} %param.18), kind=kOutput, calls=%fused_computation.18 | convolution fusion | flops 1476395008 | bytes 6422528 | tf_op jit(solution)/shard_map/dot_general | solution.py:102
  337.9 7.6 %convolution_convert_fusion.2 = bf16[512,2048]{1,0:T(8,128)(2,1)} fusion(bf16[1,704,2048]{2,1,0:T(8,128)(2,1)S(1)} %copy-done, bf16[512,2048]{1,0:T(8,128)(2,1)} %reshape.69, bf16[1,704,2048]{2,1,0:T(8,128)(2,1)} %param.19, f32[704,512]{1,0:T(8,128)} %fusion.14), kind=kOutput, calls=%fused_computation.2 | convolution fusion | flops 2956001280 | bytes 11403264 | tf_op jit(solution)/shard_map/dot_general | solution.py:107
  345.6 4.1 %reshape.70 = bf16[128,4,2048]{2,1,0:T(4,128)(2,1)} reshape(bf16[512,2048]{1,0:T(8,128)(2,1)} %convolution_convert_fusion.2) | data formatting | bytes 4194304 | tf_op jit(solution)/shard_map/reshape | solution.py:187
  349.7 5.7 %all-to-all-start.1 = ((bf16[128,4,2048]{2,1,0:T(4,128)(2,1)}), bf16[128,4,2048]{2,1,0:T(4,128)(2,1)}, u32[]{:S(2)}, u32[]{:S(2)}) async-start(bf16[128,4,2048]{2,1,0:T(4,128)(2,1)} %reshape.70), calls=%async_computation.3 | async-start | bytes 4194304 | tf_op jit(solution)/shard_map/all_to_all | solution.py:186
  355.4 3.0 copy.23
  358.4 2.9 reshape.65
  361.3 24.4 %all-to-all-done.1 = bf16[128,4,2048]{2,1,0:T(4,128)(2,1)} async-done(((bf16[128,4,2048]{2,1,0:T(4,128)(2,1)}), bf16[128,4,2048]{2,1,0:T(4,128)(2,1)}, u32[]{:S(2)}, u32[]{:S(2)}) %all-to-all-start.1) | async-done | bytes 2097184 | tf_op jit(solution)/shard_map/all_to_all | solution.py:186
  385.7 2.2 convert.4
  387.9 1.9 fusion.6
  389.8 2.1 convert_element_type.66
  391.9 1.9 fusion.5
  393.8 1.1 reshape.71
  (19 shorter events, 0.1 us)
Async XLA Ops:
  6.5 331.4 %copy-start = (bf16[1,704,2048]{2,1,0:T(8,128)(2,1)S(1)}, bf16[1,704,2048]{2,1,0:T(8,128)(2,1)}, u32[]{:S(2)}) copy-start(bf16[1,704,2048]{2,1,0:T(8,128)(2,1)} %param.20) | copy-start | bytes 8650756
  6.5 38.5 %all-gather.4.cloned.1.call-start = ((), (), s32[]{:S(2)}) async-start(), calls=%async_computation.4 | async-start | bytes 4718592 | tf_op jit(solution)/shard_map/all_gather | solution.py:131
  7.3 128.2 %all-gather.8.cloned.1.call-start = ((), (), s32[]{:S(2)}) async-start(), calls=%async_computation.7 | async-start | bytes 8912896 | tf_op jit(solution)/shard_map/all_gather | solution.py:153
  63.0 3.1 copy-start.3
  65.3 142.7 %all-gather.6.cloned.1.call-start = ((), (), s32[]{:S(2)}) async-start(), calls=%async_computation.5 | async-start | bytes 8912896 | tf_op jit(solution)/shard_map/all_gather | solution.py:153
  66.0 179.5 %reduce-scatter.5.cloned.1.call-start = ((), (), s32[]{:S(2)}) async-start(), calls=%async_computation.8 | async-start | bytes 2359296 | tf_op jit(solution)/shard_map/reduce_scatter | solution.py:157
  166.4 109.3 %reduce-scatter.3.cloned.1.call-start = ((), (), s32[]{:S(2)}) async-start(), calls=%async_computation.6 | async-start | bytes 2359296 | tf_op jit(solution)/shard_map/reduce_scatter | solution.py:157
  241.7 3.5 copy-start.2
  241.7 3.5 copy-start.4
  241.7 3.5 copy-start.5
  241.7 34.0 %copy-start.1 = (bf16[64,2,2048]{2,1,0:T(2,128)(2,1)S(1)}, bf16[64,2,2048]{2,1,0:T(2,128)(2,1)}, u32[]{:S(2)}) copy-start(bf16[64,2,2048]{2,1,0:T(2,128)(2,1)} %param.12) | copy-start | bytes 1572868
  349.7 36.0 %all-to-all-start.1 = ((bf16[128,4,2048]{2,1,0:T(4,128)(2,1)}), bf16[128,4,2048]{2,1,0:T(4,128)(2,1)}, u32[]{:S(2)}, u32[]{:S(2)}) async-start(bf16[128,4,2048]{2,1,0:T(4,128)(2,1)} %reshape.70), calls=%async_computation.3 | async-start | bytes 4194304 | tf_op jit(solution)/shard_map/all_to_all | solution.py:186
Sparse Core Ops, SparseCore 0:
  9.1 35.9 all-gather.3
  65.4 69.9 all-gather.7
  137.6 70.3 all-gather.5
  210.3 30.3 reduce-scatter.4
  245.3 30.4 reduce-scatter.2

commit v3 on v1

--- a/solution.py
+++ b/solution.py
@@ -11,13 +11,13 @@
 
 DH = 128
 KEY_BLOCK = 512
+QUERY_BLOCK = 1024
 
 
 def flash_body(scalars, q_ref, k_ref, v_ref, o_ref, m_ref, l_ref, acc_ref, *, scale, key_block):
-    s = pl.program_id(0)
-    j = pl.program_id(2)
-    last = pl.num_programs(2) - 1
-    length = scalars[s]
+    j = pl.program_id(1)
+    last = pl.num_programs(1) - 1
+    length = scalars[0]
     start = j * key_block
 
     @pl.when(j == 0)
@@ -27,10 +27,8 @@
         acc_ref[...] = jnp.zeros(acc_ref.shape, jnp.float32)
 
     def update(masked):
-        q = q_ref[...]
-        k = k_ref[...]
         scores = lax.dot_general(
-            q, k, (((1,), (1,)), ((), ())), preferred_element_type=jnp.float32
+            q_ref[...], k_ref[...], (((1,), (1,)), ((), ())), preferred_element_type=jnp.float32
         ) * scale
         if masked:
             cols = start + lax.broadcasted_iota(jnp.int32, scores.shape, 1)
@@ -55,52 +53,45 @@
 
     @pl.when(j == last)
     def _():
-        rows = scalars[2] + lax.broadcasted_iota(jnp.int32, acc_ref.shape, 0)
-        out = acc_ref[...] / l_ref[...]
-        o_ref[...] = jnp.where(rows < length, out, 0.0).astype(o_ref.dtype)
-
-
-def flash_attention(scalars, q_all, kv_all, heads, scale):
-    rows = q_all.shape[0]
-    keys = kv_all.shape[0]
-    tables = scalars.shape[0] - 1
+        o_ref[...] = (acc_ref[...] / l_ref[...]).astype(o_ref.dtype)
+
+
+def flash_attention(scalars, q_rows, kv_rows, scale):
+    rows = q_rows.shape[0]
+    keys = kv_rows.shape[0]
     key_block = KEY_BLOCK
+    query_block = min(rows, QUERY_BLOCK)
     nk = keys // key_block
 
-    def clamp(j, sc, s):
-        return jnp.minimum(j, (sc[s] - 1) // key_block)
+    def clamp(j, sc):
+        return jnp.minimum(j, (sc[0] - 1) // key_block)
 
     grid_spec = pltpu.PrefetchScalarGridSpec(
         num_scalar_prefetch=1,
-        grid=(tables, heads, nk),
+        grid=(rows // query_block, nk),
         in_specs=[
-            pl.BlockSpec((rows, DH), lambda s, h, j, sc: (0, s * heads + h)),
-            pl.BlockSpec((key_block, DH), lambda s, h, j, sc: (clamp(j, sc, s), s * 2 * heads + h)),
-            pl.BlockSpec(
-                (key_block, DH), lambda s, h, j, sc: (clamp(j, sc, s), s * 2 * heads + heads + h)
-            ),
+            pl.BlockSpec((query_block, DH), lambda i, j, sc: (i, 0)),
+            pl.BlockSpec((key_block, DH), lambda i, j, sc: (clamp(j, sc), 0)),
+            pl.BlockSpec((key_block, DH), lambda i, j, sc: (clamp(j, sc), 1)),
         ],
-        out_specs=pl.BlockSpec((rows, DH), lambda s, h, j, sc: (0, s * heads + h)),
+        out_specs=pl.BlockSpec((query_block, DH), lambda i, j, sc: (i, 0)),
         scratch_shapes=[
-            pltpu.VMEM((rows, DH), jnp.float32),
-            pltpu.VMEM((rows, DH), jnp.float32),
-            pltpu.VMEM((rows, DH), jnp.float32),
+            pltpu.VMEM((query_block, DH), jnp.float32),
+            pltpu.VMEM((query_block, DH), jnp.float32),
+            pltpu.VMEM((query_block, DH), jnp.float32),
         ],
     )
-    flops = 4 * tables * heads * rows * keys * DH
     return pl.pallas_call(
         functools.partial(flash_body, scale=scale, key_block=key_block),
         grid_spec=grid_spec,
-        out_shape=jax.ShapeDtypeStruct((rows, tables * heads * DH), jnp.bfloat16),
-        compiler_params=pltpu.CompilerParams(
-            dimension_semantics=("arbitrary", "arbitrary", "arbitrary")
+        out_shape=jax.ShapeDtypeStruct((rows, DH), jnp.bfloat16),
+        compiler_params=pltpu.CompilerParams(dimension_semantics=("arbitrary", "arbitrary")),
+        cost_estimate=pl.CostEstimate(
+            flops=4 * rows * keys * DH,
+            transcendentals=rows * keys,
+            bytes_accessed=2 * (2 * rows * DH + kv_rows.size * (rows // query_block)),
         ),
-        cost_estimate=pl.CostEstimate(
-            flops=flops,
-            transcendentals=tables * heads * rows * keys,
-            bytes_accessed=2 * (q_all.size * 2 + kv_all.size),
-        ),
-    )(scalars, q_all, kv_all, kv_all)
+    )(scalars, q_rows, kv_rows, kv_rows)
 
 
 def expert_half(slot_rows, gate_half, up_half, down_half):
@@ -137,23 +128,71 @@
     shard_rows = lax.all_gather(table_cells, "head", axis=0, tiled=True)
     row_cells = shard_rows.shape[0]
     flat_rows = shard_rows.reshape(row_cells * tables, model_width)
-    q_all = (
+    pairs = tables * head_count
+    expert_size = lax.axis_size("expert")
+    quarters = expert_size // pairs
+    me = lax.axis_index("expert")
+    q_pairs = (
         jnp.dot(flat_rows, w_query, preferred_element_type=jnp.float32)
         .astype(jnp.bfloat16)
-        .reshape(row_cells, tables * head_width)
-    )
-    kv_weight = jnp.concatenate([w_key, w_value], axis=1)
-    kv_rows = (
+        .reshape(row_cells, pairs, DH)
+    )
+    kv_weight = jnp.concatenate(
+        [w_key.reshape(model_width, head_count, DH), w_value.reshape(model_width, head_count, DH)],
+        axis=2,
+    ).reshape(model_width, 2 * head_width)
+    kv_pairs = (
         jnp.dot(flat_rows, kv_weight, preferred_element_type=jnp.float32)
         .astype(jnp.bfloat16)
-        .reshape(row_cells, tables * 2 * head_width)
-    )
-    kv_all = lax.all_gather(kv_rows, "expert", axis=0, tiled=True)
-    offset = lax.axis_index("expert") * row_cells
-    scalars = jnp.concatenate(
-        [lengths.astype(jnp.int32), jnp.reshape(offset, (1,)).astype(jnp.int32)]
-    )
-    attended = flash_attention(scalars, q_all, kv_all, head_count, score_scale)
+        .reshape(row_cells, pairs, 2 * DH)
+        .transpose(1, 0, 2)
+    )
+    send = jnp.repeat(kv_pairs, quarters, axis=0)
+    kv_here = lax.all_to_all(send, "expert", 0, 0, tiled=True).reshape(
+        expert_size * row_cells, 2 * DH
+    )
+    my_pair = me // quarters
+    my_part = me % quarters
+    q_parts = []
+    for shift in range(quarters):
+        perm = [
+            (src, quarters * ((src % quarters + shift) % quarters) + src // quarters)
+            for src in range(expert_size)
+        ]
+        sent_pair = (my_part + shift) % quarters
+        q_parts.append(
+            lax.ppermute(
+                lax.dynamic_index_in_dim(q_pairs, sent_pair, axis=1, keepdims=False),
+                "expert",
+                perm,
+            )
+        )
+    q_stack = jnp.stack(q_parts)
+    q_rows = jnp.take(q_stack, (my_pair - jnp.arange(quarters)) % quarters, axis=0)
+    scalars = jnp.reshape(lengths[my_pair // head_count], (1,)).astype(jnp.int32)
+    out_rows = flash_attention(
+        scalars, q_rows.reshape(quarters * row_cells, DH), kv_here, score_scale
+    ).reshape(quarters, row_cells, DH)
+    back_parts = []
+    for shift in range(quarters):
+        perm = [
+            (quarters * ((src % quarters + shift) % quarters) + src // quarters, src)
+            for src in range(expert_size)
+        ]
+        source_slot = (my_pair - shift) % quarters
+        back_parts.append(
+            lax.ppermute(
+                lax.dynamic_index_in_dim(out_rows, source_slot, axis=0, keepdims=False),
+                "expert",
+                perm,
+            )
+        )
+    back_stack = jnp.stack(back_parts)
+    attended = jnp.take(back_stack, (jnp.arange(pairs) - my_part) % quarters, axis=0)
+    positions = me * row_cells + jnp.arange(row_cells, dtype=jnp.int32)
+    live = positions[:, None] < lengths[None, :]
+    attended = attended.reshape(tables, head_count, row_cells, DH).transpose(2, 0, 1, 3)
+    attended = jnp.where(live[:, :, None, None], attended, jnp.zeros_like(attended))
     count_rows = cell_count * lax.axis_size("head")
     product = jnp.dot(
         attended.reshape(count_rows * tables, head_width), w_out, preferred_element_type=jnp.float32

time: 396 us -> 413 us (1.043)
  waiting for transfers between devices: 202 us -> 145 us
  starting transfers between devices: 5.75 us -> 48 us
  local copies, waits for them, and re-layouts: 37.1 us -> 54.5 us
  other arithmetic: 8.47 us -> 17.3 us
  Pallas kernels: 55.8 us -> 60.1 us
    all_gather x1 -> x0, waiting for transfers between devices: 105 us -> none  [shards(): kv_all = lax.all_gather(kv_rows, 'expert', axis=0, tiled=True)]
    ppermute x0 -> x8, waiting for transfers between devices: none -> 54.8 us  [the longest x4 40.4 us: shards(): lax.ppermute(lax.dynamic_index_in_dim(q_pairs, sent_pair, axis=1, keepdim...]
    ppermute x0 -> x8, starting transfers between devices: none -> 35.6 us  [the longest x4 24.7 us: shards(): lax.ppermute(lax.dynamic_index_in_dim(out_rows, source_slot, axis=0, keep...]
    all_gather x1, waiting for transfers between devices: 37.8 us -> 27.6 us  [shards(): shard_rows = lax.all_gather(table_cells, 'head', axis=0, tiled=True)]
    all_to_all x0 -> x1, starting transfers between devices: none -> 6.71 us  [shards(): lax.all_to_all(send, 'expert', 0, 0, tiled=True)]
    reshape x2 -> x4, local copies, waits for them, and re-layouts: 3.18 us -> 8.14 us  [the longest x1 2.52 us: shards(): kv_pairs = jnp.dot(flat_rows, kv_weight, preferred_element_type=jnp.float...]
    pallas_call x1, Pallas kernels: 55.8 us -> 60.1 us  [flash_attention(): pl.pallas_call(functools.partial(flash_body, scale=scale, key_block=key_b...]
  transfers between devices with their start and end apart: 4 -> 12, of which waited for: 4 -> 7; matrix products, arithmetic and copies ran while one was open for 3% -> 7% of each run, Pallas kernels for 0% -> 0%
where the time goes in v3:
time: 413 us; the launch traced here: 412 us
  waiting for transfers between devices  145 us (35%)
  Pallas kernels  60.1 us (15%)
  local copies, waits for them, and re-layouts  54.5 us (13%)
  starting transfers between devices  48 us (12%)
  blocking collectives  40.4 us (10%)
  matrix products  32.6 us (8%)
  other arithmetic  17.3 us (4%)
  between operations  13.7 us (3%)
    pallas_call x1, Pallas kernels, flash_attention(): pl.pallas_call(functools.partial(flash_body, scale=scale, key_block=key_b...  60.1 us
    ppermute x4, waiting for transfers between devices, shards(): lax.ppermute(lax.dynamic_index_in_dim(q_pairs, sent_pair, axis=1, keepdim...  40.4 us
    all_to_all x1, blocking collectives, shards(): lax.all_to_all(doubled, ('expert', 'head'), split_axis=0, concat_axis=0,...  40.4 us
    reduce_scatter x1, waiting for transfers between devices, shards(): lax.psum_scatter(product.reshape(count_rows, tables, model_width).astype(...  37.4 us
    all_gather x1, waiting for transfers between devices, shards(): shard_rows = lax.all_gather(table_cells, 'head', axis=0, tiled=True)  27.6 us
    ppermute x4, starting transfers between devices, shards(): lax.ppermute(lax.dynamic_index_in_dim(out_rows, source_slot, axis=0, keep...  24.7 us
    all_to_all x1, waiting for transfers between devices, shards(): lax.all_to_all(expert_half(flat_rows, gate_half, up_half, down_half).resh...  24.4 us
    ppermute x4, waiting for transfers between devices, shards(): lax.ppermute(lax.dynamic_index_in_dim(out_rows, source_slot, axis=0, keep...  14.3 us
  transfers between devices with their start and end apart: 12, of which 7 were waited for; matrix products, arithmetic and copies ran while one was open for 7% of the time, Pallas kernels for 0%

profile of v3, /device:TPU:1, one launch (start us, length us, event | category | flops | bytes accessed | tf_op | source)
XLA Modules:
  0.0 411.6 jit_solution(3959728154253156935)
XLA Ops:
  7.3 2.3 reshape.128
  9.6 2.2 reshape.129
  11.7 3.8 pad_maximum_fusion
  15.5 1.9 copy.54
  17.4 27.6 %all-gather.2.cloned.1.call-done = bf16[512,2,2048]{2,1,0:T(2,128)(2,1)} async-done(((bf16[64,2,2048]{2,1,0:T(2,128)(2,1)}), bf16[512,2,2048]{2,1,0:T(2,128)(2,1)}) %all-gather.2.cloned.1.call-update) | async-done | bytes 4194320 | tf_op jit(solution)/shard_map/all_gather | solution.py:128
  45.1 7.2 %reshape.125 = bf16[1024,2048]{1,0:T(8,128)(2,1)} reshape(bf16[512,2,2048]{2,1,0:T(2,128)(2,1)} %all-gather.2.cloned.1.call-done) | data formatting | bytes 8388608 | tf_op jit(solution)/shard_map/reshape | solution.py:130
  52.3 6.2 %fusion.19 = bf16[1024,512]{0,1:T(8,128)(2,1)} fusion(bf16[2048,512]{1,0:T(8,128)(2,1)} %bitcast.89, bf16[1024,2048]{1,0:T(8,128)(2,1)} %reshape.125), kind=kOutput, calls=%fused_computation.20 | convolution fusion | flops 2148007936 | bytes 7340032 | tf_op jit(solution)/shard_map/dot_general | solution.py:145
  58.5 2.3 copy.42
  60.8 2.5 reshape.131
  63.3 1.4 copy.43
  64.7 2.4 broadcast_in_dim.34
  67.1 6.7 %all-to-all-start = ((bf16[16,512,256]{2,1,0:T(8,128)(2,1)}), bf16[16,512,256]{2,1,0:T(8,128)(2,1)}, u32[]{:S(2)}, u32[]{:S(2)}) async-start(bf16[16,512,256]{2,1,0:T(8,128)(2,1)} %bitcast.85), calls=%async_computation | async-start | bytes 8388608 | tf_op jit(solution)/shard_map/all_to_all | solution.py:151
  74.0 4.5 %convolution_convert_fusion.4 = bf16[1024,256]{1,0:T(8,128)(2,1)} fusion(bf16[1024,2048]{1,0:T(8,128)(2,1)} %reshape.125, bf16[2048,256]{1,0:T(8,128)(2,1)} %param.15), kind=kOutput, calls=%fused_computation.21 | convolution fusion | flops 1074003968 | bytes 5767168 | tf_op jit(solution)/shard_map/dot_general | solution.py:136
  78.6 1.2 reshape.126
  81.6 3.8 collective-permute-start.1
  85.4 4.3 %collective-permute-start.2 = (bf16[512,128]{1,0:T(8,128)(2,1)S(1)}, bf16[512,128]{1,0:T(8,128)(2,1)}, u32[]{:S(2)}, u32[]{:S(2)}) collective-permute-start(bf16[512,128]{1,0:T(8,128)(2,1)S(1)} %bitcast.96), channel_id=1, source_target_pairs={{0,64},{8,96},{16,0},{24,32},{32,72},{40,104},{48,8},{56,40},{64,8... | collective-permute-start | bytes 393224 | tf_op jit(solution)/shard_map/ppermute | solution.py:164
  89.7 2.1 collective-permute-start.3
  93.6 37.6 %collective-permute-done.1 = bf16[512,128]{1,0:T(8,128)(2,1)} collective-permute-done((bf16[512,128]{1,0:T(8,128)(2,1)S(1)}, bf16[512,128]{1,0:T(8,128)(2,1)}, u32[]{:S(2)}, u32[]{:S(2)}) %collective-permute-start.1) | collective-permute-done | bytes 131104 | tf_op jit(solution)/shard_map/ppermute | solution.py:164
  131.2 2.8 collective-permute-done.2
  135.1 1.4 gather_fusion
  136.5 1.9 broadcast_select_fusion.1
  138.5 60.1 %shard_map.118 = bf16[2048,128]{1,0:T(8,128)(2,1)} custom-call(s32[1]{0:T(128)} %dynamic_slice.29.scalars, bf16[2048,128]{1,0:T(8,128)(2,1)} %bitcast.93, bf16[8192,256]{1,0:T(8,128)(2,1)} %bitcast.12.k_ref.v_ref, bf16[8192,256]{1,0:T(8,128)(2,1)} %bitcast.12.k_ref.v_ref), custom_call_target="tpu_custom_call" | custom-call | flops 8589934592 | bytes 9437184 | tf_op jit(solution)/shard_map/pallas_call | solution.py:84
  200.4 17.5 %collective-permute-start.5 = (bf16[512,128]{1,0:T(8,128)(2,1)S(1)}, bf16[512,128]{1,0:T(8,128)(2,1)S(1)}, u32[]{:S(2)}, u32[]{:S(2)}) collective-permute-start(bf16[512,128]{1,0:T(8,128)(2,1)S(1)} %get-tuple-element.11), channel_id=1, source_target_pairs={{32,0},{64,8},{96,16},{0,24},{40,32},{72,40},{104,48},{8,56},{48,6... | collective-permute-start | bytes 393224 | tf_op jit(solution)/shard_map/ppermute | solution.py:184
  217.9 6.5 %collective-permute-start.6 = (bf16[512,128]{1,0:T(8,128)(2,1)S(1)}, bf16[512,128]{1,0:T(8,128)(2,1)S(1)}, u32[]{:S(2)}, u32[]{:S(2)}) collective-permute-start(bf16[512,128]{1,0:T(8,128)(2,1)S(1)} %get-tuple-element.10), channel_id=1, source_target_pairs={{64,0},{96,8},{0,16},{32,24},{72,32},{104,40},{8,48},{40,56},{80,6... | collective-permute-start | bytes 393224 | tf_op jit(solution)/shard_map/ppermute | solution.py:184
  224.5 6.9 %collective-permute-done.6 = bf16[512,128]{1,0:T(8,128)(2,1)S(1)} collective-permute-done((bf16[512,128]{1,0:T(8,128)(2,1)S(1)}, bf16[512,128]{1,0:T(8,128)(2,1)S(1)}, u32[]{:S(2)}, u32[]{:S(2)}) %collective-permute-start.6) | collective-permute-done | bytes 131104 | tf_op jit(solution)/shard_map/ppermute | solution.py:184
  231.4 7.4 %collective-permute-done.7 = bf16[512,128]{1,0:T(8,128)(2,1)S(1)} collective-permute-done((bf16[512,128]{1,0:T(8,128)(2,1)S(1)}, bf16[512,128]{1,0:T(8,128)(2,1)S(1)}, u32[]{:S(2)}, u32[]{:S(2)}) %collective-permute-start.7) | collective-permute-done | bytes 131104 | tf_op jit(solution)/shard_map/ppermute | solution.py:184
  238.9 1.4 gather_fusion.1
  240.3 1.2 broadcast_select_fusion
  242.7 4.6 %convolution_convert_fusion = bf16[512,2,2048]{2,0,1:T(8,128)(2,1)} fusion(bf16[512,2,256]{0,2,1:T(8,128)(2,1)} %bitcast.91, bf16[256,2048]{1,0:T(8,128)(2,1)} %param.18), kind=kOutput, calls=%fused_computation.2 | convolution fusion | flops 1075838976 | bytes 5767168 | tf_op jit(solution)/shard_map/dot_general | solution.py:197
  248.3 37.4 %reduce-scatter.2.cloned.1.call-done = bf16[64,2,2048]{2,0,1:T(8,128)(2,1)} async-done(((bf16[512,2,2048]{2,0,1:T(8,128)(2,1)}), bf16[64,2,2048]{2,0,1:T(8,128)(2,1)}) %reduce-scatter.2.cloned.1.call-update) | async-done | bytes 524304 | tf_op jit(solution)/shard_map/reduce_scatter | solution.py:200
  285.7 1.3 multiply_reduce_fusion
  287.0 2.3 multiply_convert_fusion
  290.9 2.5 convolution_convert_fusion.2
  293.4 2.3 reshape.138
  295.6 2.5 broadcast_in_dim.36
  298.1 40.4 %all_to_all.15 = bf16[128,4,2048]{2,1,0:T(4,128)(2,1)} all-to-all(bf16[128,4,2048]{2,1,0:T(4,128)(2,1)S(1)} %bitcast.87), channel_id=1, replica_groups=mesh['expert'=16,'head'=8] {'expert','head'}, dimensions={0} | all-to-all | bytes 4194304 | tf_op jit(solution)/shard_map/all_to_all | solution.py:226
  338.5 4.0 reshape.140
  342.5 5.3 %fusion.7 = f32[704,512]{1,0:T(8,128)} fusion(bf16[512,2048]{1,0:T(8,128)(2,1)} %reshape.140, bf16[1,704,2048]{2,1,0:T(8,128)(2,1)} %param.20), kind=kOutput, calls=%fused_computation.16 | convolution fusion | flops 1476395008 | bytes 6422528 | tf_op jit(solution)/shard_map/dot_general | solution.py:99
  347.8 7.6 %convolution_convert_fusion.1 = bf16[512,2048]{1,0:T(8,128)(2,1)} fusion(bf16[1,704,2048]{2,1,0:T(8,128)(2,1)S(1)} %copy-done, bf16[512,2048]{1,0:T(8,128)(2,1)} %reshape.140, bf16[1,704,2048]{2,1,0:T(8,128)(2,1)} %param.21, f32[704,512]{1,0:T(8,128)} %fusion.7), kind=kOutput, calls=%fused_computation.3 | convolution fusion | flops 2956001280 | bytes 11403264 | tf_op jit(solution)/shard_map/dot_general | solution.py:104
  355.4 4.1 %reshape.141 = bf16[128,4,2048]{2,1,0:T(4,128)(2,1)} reshape(bf16[512,2048]{1,0:T(8,128)(2,1)} %convolution_convert_fusion.1) | data formatting | bytes 4194304 | tf_op jit(solution)/shard_map/reshape | solution.py:231
  359.5 5.7 %all-to-all-start.2 = ((bf16[128,4,2048]{2,1,0:T(4,128)(2,1)}), bf16[128,4,2048]{2,1,0:T(4,128)(2,1)}, u32[]{:S(2)}, u32[]{:S(2)}) async-start(bf16[128,4,2048]{2,1,0:T(4,128)(2,1)} %reshape.141), calls=%async_computation.3 | async-start | bytes 4194304 | tf_op jit(solution)/shard_map/all_to_all | solution.py:230
  365.2 3.0 copy.46
  368.2 2.9 reshape.136
  371.1 24.4 %all-to-all-done.2 = bf16[128,4,2048]{2,1,0:T(4,128)(2,1)} async-done(((bf16[128,4,2048]{2,1,0:T(4,128)(2,1)}), bf16[128,4,2048]{2,1,0:T(4,128)(2,1)}, u32[]{:S(2)}, u32[]{:S(2)}) %all-to-all-start.2) | async-done | bytes 2097184 | tf_op jit(solution)/shard_map/all_to_all | solution.py:230
  395.5 2.2 convert.1
  397.7 1.8 fusion.6
  399.6 2.2 convert_element_type.64
  401.8 1.9 fusion.5
  (50 shorter events, 12.3 us)
Async XLA Ops:
  6.5 341.2 %copy-start = (bf16[1,704,2048]{2,1,0:T(8,128)(2,1)S(1)}, bf16[1,704,2048]{2,1,0:T(8,128)(2,1)}, u32[]{:S(2)}) copy-start(bf16[1,704,2048]{2,1,0:T(8,128)(2,1)} %param.22) | copy-start | bytes 8650756
  6.5 38.5 %all-gather.2.cloned.1.call-start = ((), (), s32[]{:S(2)}) async-start(), calls=%async_computation.4 | async-start | bytes 4718592 | tf_op jit(solution)/shard_map/all_gather | solution.py:128
  67.1 6.9 %copy-start.5 = (s32[2]{0:T(128)S(1)}, s32[2]{0:T(128)}, u32[]{:S(2)}) copy-start(s32[2]{0:T(128)} %param.23) | copy-start | bytes 28
  67.1 71.4 %all-to-all-start = ((bf16[16,512,256]{2,1,0:T(8,128)(2,1)}), bf16[16,512,256]{2,1,0:T(8,128)(2,1)}, u32[]{:S(2)}, u32[]{:S(2)}) async-start(bf16[16,512,256]{2,1,0:T(8,128)(2,1)} %bitcast.85), calls=%async_computation | async-start | bytes 8388608 | tf_op jit(solution)/shard_map/all_to_all | solution.py:151
  73.8 211.9 %reduce-scatter.2.cloned.1.call-start = ((), (), s32[]{:S(2)}) async-start(), calls=%async_computation.5 | async-start | bytes 4718592 | tf_op jit(solution)/shard_map/reduce_scatter | solution.py:200
  80.9 12.7 %collective-permute-start = (bf16[512,128]{1,0:T(8,128)(2,1)S(1)}, bf16[512,128]{1,0:T(8,128)(2,1)S(1)}, u32[]{:S(2)}, u32[]{:S(2)}) collective-permute-start(bf16[512,128]{1,0:T(8,128)(2,1)S(1)} %bitcast.94), channel_id=1, source_target_pairs={{0,0},{8,32},{16,64},{24,96},{32,8},{40,40},{48,72},{56,104},{64,1... | collective-permute-start | bytes 393224 | tf_op jit(solution)/shard_map/ppermute | solution.py:164
  81.6 49.6 %collective-permute-start.1 = (bf16[512,128]{1,0:T(8,128)(2,1)S(1)}, bf16[512,128]{1,0:T(8,128)(2,1)}, u32[]{:S(2)}, u32[]{:S(2)}) collective-permute-start(bf16[512,128]{1,0:T(8,128)(2,1)S(1)} %bitcast.95), channel_id=1, source_target_pairs={{0,32},{8,64},{16,96},{24,0},{32,40},{40,72},{48,104},{56,8},{64,4... | collective-permute-start | bytes 393224 | tf_op jit(solution)/shard_map/ppermute | solution.py:164
  85.4 48.6 %collective-permute-start.2 = (bf16[512,128]{1,0:T(8,128)(2,1)S(1)}, bf16[512,128]{1,0:T(8,128)(2,1)}, u32[]{:S(2)}, u32[]{:S(2)}) collective-permute-start(bf16[512,128]{1,0:T(8,128)(2,1)S(1)} %bitcast.96), channel_id=1, source_target_pairs={{0,64},{8,96},{16,0},{24,32},{32,72},{40,104},{48,8},{56,40},{64,8... | collective-permute-start | bytes 393224 | tf_op jit(solution)/shard_map/ppermute | solution.py:164
  89.7 44.3 %collective-permute-start.3 = (bf16[512,128]{1,0:T(8,128)(2,1)S(1)}, bf16[512,128]{1,0:T(8,128)(2,1)}, u32[]{:S(2)}, u32[]{:S(2)}) collective-permute-start(bf16[512,128]{1,0:T(8,128)(2,1)S(1)} %bitcast.97), channel_id=1, source_target_pairs={{0,96},{8,0},{16,32},{24,64},{32,104},{40,8},{48,40},{56,72},{64,1... | collective-permute-start | bytes 393224 | tf_op jit(solution)/shard_map/ppermute | solution.py:164
  199.7 24.8 %collective-permute-start.4 = (bf16[512,128]{1,0:T(8,128)(2,1)S(1)}, bf16[512,128]{1,0:T(8,128)(2,1)S(1)}, u32[]{:S(2)}, u32[]{:S(2)}) collective-permute-start(bf16[512,128]{1,0:T(8,128)(2,1)S(1)} %get-tuple-element.8), channel_id=1, source_target_pairs={{0,0},{32,8},{64,16},{96,24},{8,32},{40,40},{72,48},{104,56},{16,6... | collective-permute-start | bytes 393224 | tf_op jit(solution)/shard_map/ppermute | solution.py:184
  200.4 24.1 %collective-permute-start.5 = (bf16[512,128]{1,0:T(8,128)(2,1)S(1)}, bf16[512,128]{1,0:T(8,128)(2,1)S(1)}, u32[]{:S(2)}, u32[]{:S(2)}) collective-permute-start(bf16[512,128]{1,0:T(8,128)(2,1)S(1)} %get-tuple-element.11), channel_id=1, source_target_pairs={{32,0},{64,8},{96,16},{0,24},{40,32},{72,40},{104,48},{8,56},{48,6... | collective-permute-start | bytes 393224 | tf_op jit(solution)/shard_map/ppermute | solution.py:184
  217.9 13.5 %collective-permute-start.6 = (bf16[512,128]{1,0:T(8,128)(2,1)S(1)}, bf16[512,128]{1,0:T(8,128)(2,1)S(1)}, u32[]{:S(2)}, u32[]{:S(2)}) collective-permute-start(bf16[512,128]{1,0:T(8,128)(2,1)S(1)} %get-tuple-element.10), channel_id=1, source_target_pairs={{64,0},{96,8},{0,16},{32,24},{72,32},{104,40},{8,48},{40,56},{80,6... | collective-permute-start | bytes 393224 | tf_op jit(solution)/shard_map/ppermute | solution.py:184
  224.5 14.4 %collective-permute-start.7 = (bf16[512,128]{1,0:T(8,128)(2,1)S(1)}, bf16[512,128]{1,0:T(8,128)(2,1)S(1)}, u32[]{:S(2)}, u32[]{:S(2)}) collective-permute-start(bf16[512,128]{1,0:T(8,128)(2,1)S(1)} %get-tuple-element.9), channel_id=1, source_target_pairs={{96,0},{0,8},{32,16},{64,24},{104,32},{8,40},{40,48},{72,56},{112,... | collective-permute-start | bytes 393224 | tf_op jit(solution)/shard_map/ppermute | solution.py:184
  247.3 0.7 copy-start.2
  247.3 0.7 copy-start.3
  247.3 0.7 copy-start.4
  247.3 38.4 %copy-start.1 = (bf16[64,2,2048]{2,1,0:T(2,128)(2,1)S(1)}, bf16[64,2,2048]{2,1,0:T(2,128)(2,1)}, u32[]{:S(2)}) copy-start(bf16[64,2,2048]{2,1,0:T(2,128)(2,1)} %param.14) | copy-start | bytes 1572868
  359.5 36.0 %all-to-all-start.2 = ((bf16[128,4,2048]{2,1,0:T(4,128)(2,1)}), bf16[128,4,2048]{2,1,0:T(4,128)(2,1)}, u32[]{:S(2)}, u32[]{:S(2)}) async-start(bf16[128,4,2048]{2,1,0:T(4,128)(2,1)} %reshape.141), calls=%async_computation.3 | async-start | bytes 4194304 | tf_op jit(solution)/shard_map/all_to_all | solution.py:230
Sparse Core Ops, SparseCore 0:
  9.1 35.9 all-gather.1
  247.5 38.1 reduce-scatter.1

commit v4 on v1

--- a/solution.py
+++ b/solution.py
@@ -10,7 +10,7 @@
 from jax.sharding import PartitionSpec as P
 
 DH = 128
-KEY_BLOCK = 512
+KEY_BLOCK = 4096
 
 
 def flash_body(scalars, q_ref, k_ref, v_ref, o_ref, m_ref, l_ref, acc_ref, *, scale, key_block):

time: 396 us -> 377 us (0.952)
  Pallas kernels: 55.8 us -> 36.9 us
    pallas_call x1, Pallas kernels: 55.8 us -> 36.9 us  [flash_attention(): pl.pallas_call(functools.partial(flash_body, scale=scale, key_block=key_b...]
where the time goes in v4:
time: 377 us; the launch traced here: 376 us
  waiting for transfers between devices  202 us (54%)
  blocking collectives  40.6 us (11%)
  local copies, waits for them, and re-layouts  37.1 us (10%)
  Pallas kernels  36.9 us (10%)
  matrix products  31.8 us (8%)
  between operations  13.2 us (4%)
  other arithmetic  8.47 us (2%)
  starting transfers between devices  5.75 us (2%)
    all_gather x1, waiting for transfers between devices, shards(): kv_all = lax.all_gather(kv_rows, 'expert', axis=0, tiled=True)  105 us
    all_to_all x1, blocking collectives, shards(): lax.all_to_all(doubled, ('expert', 'head'), split_axis=0, concat_axis=0,...  40.6 us
    all_gather x1, waiting for transfers between devices, shards(): shard_rows = lax.all_gather(table_cells, 'head', axis=0, tiled=True)  37.8 us
    pallas_call x1, Pallas kernels, flash_attention(): pl.pallas_call(functools.partial(flash_body, scale=scale, key_block=key_b...  36.9 us
    reduce_scatter x1, waiting for transfers between devices, shards(): lax.psum_scatter(product.reshape(count_rows, tables, model_width).astype(...  34 us
    all_to_all x1, waiting for transfers between devices, shards(): lax.all_to_all(expert_half(flat_rows, gate_half, up_half, down_half).resh...  24.4 us
    dot_general x1, matrix products, expert_half(): lax.dot_general(hidden, down_half, (((0,), (0,)), ((), ())), preferred_el...  7.63 us
  transfers between devices with their start and end apart: 4, of which 4 were waited for; matrix products, arithmetic and copies ran while one was open for 3% of the time, Pallas kernels for 0%

profile of v4, /device:TPU:1, one launch (start us, length us, event | category | flops | bytes accessed | tf_op | source)
XLA Modules:
  0.0 376.0 jit_solution(6292518577180269398)
XLA Ops:
  6.5 0.0 copy-start
  6.5 0.0 all-gather.3.cloned.1.call-start
  6.5 0.7 all-gather.3.cloned.1.call-update
  7.3 0.0 all-gather.5.cloned.1.call-start
  7.3 37.8 %all-gather.3.cloned.1.call-done = bf16[512,2,2048]{2,1,0:T(2,128)(2,1)} async-done(((bf16[64,2,2048]{2,1,0:T(2,128)(2,1)}), bf16[512,2,2048]{2,1,0:T(2,128)(2,1)}) %all-gather.3.cloned.1.call-update) | async-done | bytes 4194320 | tf_op jit(solution)/shard_map/all_gather | solution.py:137
  45.1 7.2 %reshape.70 = bf16[1024,2048]{1,0:T(8,128)(2,1)} reshape(bf16[512,2,2048]{2,1,0:T(2,128)(2,1)} %all-gather.3.cloned.1.call-done) | data formatting | bytes 8388608 | tf_op jit(solution)/shard_map/reshape | solution.py:139
  52.3 6.2 %fusion.26 = bf16[1024,512]{0,1:T(8,128)(2,1)} fusion(bf16[1024,2048]{1,0:T(8,128)(2,1)} %reshape.70, bf16[2048,256]{1,0:T(8,128)(2,1)} %param.15, bf16[2048,256]{1,0:T(8,128)(2,1)} %param.14), kind=kOutput, calls=%fused_computation.21 | convolution fusion | flops 2152202240 | bytes 7340032 | tf_op jit(solution)/shard_map/dot_general | solution.py:147
  58.5 2.3 copy.24
  60.8 2.2 reshape.72
  63.0 0.0 all-gather.5.cloned.1.call-update
  63.0 0.0 reduce-scatter.2.cloned.1.call-start
  63.1 0.0 copy-done.5
  63.1 0.6 pad_add_fusion.scalars
  63.7 3.7 convolution_convert_fusion.3
  67.4 1.0 reshape.71.q_ref
  68.4 105.3 %all-gather.5.cloned.1.call-done.k_ref.v_ref = bf16[8192,1024]{1,0:T(8,128)(2,1)} async-done(((bf16[512,1024]{1,0:T(8,128)(2,1)}), bf16[8192,1024]{1,0:T(8,128)(2,1)}) %all-gather.5.cloned.1.call-update) | async-done | bytes 16777232 | tf_op jit(solution)/shard_map/all_gather | solution.py:151
  173.7 36.9 %shard_map.118 = bf16[512,512]{1,0:T(8,128)(2,1)} custom-call(s32[3]{0:T(128)} %pad_add_fusion.scalars, bf16[512,512]{1,0:T(8,128)(2,1)} %reshape.71.q_ref, bf16[8192,1024]{1,0:T(8,128)(2,1)} %all-gather.5.cloned.1.call-done.k_ref.v_ref, bf16[8192,1024]{1,0:T(8,128)(2,1)} %all-gather.5.cloned.1.call-done.k_ref.v_ref), custom_call_target="tpu_custom_call" | custom-call | flops 8589934592 | bytes 17825792 | tf_op jit(solution)/shard_map/pallas_call | solution.py:91
  210.6 4.6 %convolution_convert_fusion = bf16[512,2,2048]{2,0,1:T(8,128)(2,1)} fusion(bf16[256,2048]{1,0:T(8,128)(2,1)} %param.16, bf16[64,2,8,256]{3,2,1,0:T(8,128)(2,1)} %bitcast.50), kind=kOutput, calls=%fused_computation | convolution fusion | flops 1075838976 | bytes 5767168 | tf_op jit(solution)/shard_map/dot_general | solution.py:158
  215.2 0.0 reduce-scatter.2.cloned.1.call-update
  215.2 0.6 copy-done.2
  215.8 0.0 copy-done.3
  215.8 0.0 copy-done.4
  215.9 0.1 copy.27
  216.0 0.1 add.40
  216.1 34.0 %reduce-scatter.2.cloned.1.call-done = bf16[64,2,2048]{2,0,1:T(8,128)(2,1)} async-done(((bf16[512,2,2048]{2,0,1:T(8,128)(2,1)}), bf16[64,2,2048]{2,0,1:T(8,128)(2,1)}) %reduce-scatter.2.cloned.1.call-update) | async-done | bytes 524304 | tf_op jit(solution)/shard_map/reduce_scatter | solution.py:161
  250.2 0.0 copy-done.1
  250.2 1.3 multiply_reduce_fusion
  251.5 2.4 multiply_convert_fusion
  253.9 0.5 copy.28
  254.4 1.0 reshape.74
  255.4 2.4 convolution_convert_fusion.2
  257.8 2.3 reshape.75
  260.1 2.5 broadcast_in_dim.2
  262.5 40.6 %all_to_all.10 = bf16[128,4,2048]{2,1,0:T(4,128)(2,1)} all-to-all(bf16[128,4,2048]{2,1,0:T(4,128)(2,1)S(1)} %bitcast.49), channel_id=1, replica_groups=mesh['expert'=16,'head'=8] {'expert','head'}, dimensions={0} | all-to-all | bytes 4194304 | tf_op jit(solution)/shard_map/all_to_all | solution.py:187
  303.2 4.0 %reshape.77 = bf16[512,2048]{1,0:T(8,128)(2,1)} reshape(bf16[128,4,2048]{2,1,0:T(4,128)(2,1)} %all_to_all.10) | data formatting | bytes 4194304 | tf_op jit(solution)/shard_map/reshape | solution.py:190
  307.1 5.3 %fusion.14 = f32[704,512]{1,0:T(8,128)} fusion(bf16[512,2048]{1,0:T(8,128)(2,1)} %reshape.77, bf16[1,704,2048]{2,1,0:T(8,128)(2,1)} %param.18), kind=kOutput, calls=%fused_computation.17 | convolution fusion | flops 1476395008 | bytes 6422528 | tf_op jit(solution)/shard_map/dot_general | solution.py:108
  312.4 0.0 copy-done
  312.4 7.6 %convolution_convert_fusion.1 = bf16[512,2048]{1,0:T(8,128)(2,1)} fusion(bf16[1,704,2048]{2,1,0:T(8,128)(2,1)S(1)} %copy-done, bf16[512,2048]{1,0:T(8,128)(2,1)} %reshape.77, bf16[1,704,2048]{2,1,0:T(8,128)(2,1)} %param.19, f32[704,512]{1,0:T(8,128)} %fusion.14), kind=kOutput, calls=%fused_computation.1 | convolution fusion | flops 2956001280 | bytes 11403264 | tf_op jit(solution)/shard_map/dot_general | solution.py:113
  320.0 4.1 %reshape.78 = bf16[128,4,2048]{2,1,0:T(4,128)(2,1)} reshape(bf16[512,2048]{1,0:T(8,128)(2,1)} %convolution_convert_fusion.1) | data formatting | bytes 4194304 | tf_op jit(solution)/shard_map/reshape | solution.py:192
  324.2 5.7 %all-to-all-start.1 = ((bf16[128,4,2048]{2,1,0:T(4,128)(2,1)}), bf16[128,4,2048]{2,1,0:T(4,128)(2,1)}, u32[]{:S(2)}, u32[]{:S(2)}) async-start(bf16[128,4,2048]{2,1,0:T(4,128)(2,1)} %reshape.78), calls=%async_computation.2 | async-start | bytes 4194304 | tf_op jit(solution)/shard_map/all_to_all | solution.py:191
  329.8 3.0 copy.26
  332.8 2.9 reshape.73
  335.7 24.4 %all-to-all-done.1 = bf16[128,4,2048]{2,1,0:T(4,128)(2,1)} async-done(((bf16[128,4,2048]{2,1,0:T(4,128)(2,1)}), bf16[128,4,2048]{2,1,0:T(4,128)(2,1)}, u32[]{:S(2)}, u32[]{:S(2)}) %all-to-all-start.1) | async-done | bytes 2097184 | tf_op jit(solution)/shard_map/all_to_all | solution.py:191
  360.1 2.2 convert.1
  362.4 1.9 fusion.6
  364.3 2.1 convert_element_type.64
  366.4 1.9 fusion.5
  368.3 1.1 reshape.79
  (8 shorter events, 0.0 us)
Async XLA Ops:
  6.5 305.9 %copy-start = (bf16[1,704,2048]{2,1,0:T(8,128)(2,1)S(1)}, bf16[1,704,2048]{2,1,0:T(8,128)(2,1)}, u32[]{:S(2)}) copy-start(bf16[1,704,2048]{2,1,0:T(8,128)(2,1)} %param.20) | copy-start | bytes 8650756
  6.5 38.5 %all-gather.3.cloned.1.call-start = ((), (), s32[]{:S(2)}) async-start(), calls=%async_computation.3 | async-start | bytes 4718592 | tf_op jit(solution)/shard_map/all_gather | solution.py:137
  7.3 166.4 %all-gather.5.cloned.1.call-start = ((), (), s32[]{:S(2)}) async-start(), calls=%async_computation.4 | async-start | bytes 17825792 | tf_op jit(solution)/shard_map/all_gather | solution.py:151
  60.8 2.3 copy-start.5
  63.0 187.2 %reduce-scatter.2.cloned.1.call-start = ((), (), s32[]{:S(2)}) async-start(), calls=%async_computation.5 | async-start | bytes 4718592 | tf_op jit(solution)/shard_map/reduce_scatter | solution.py:161
  215.2 0.7 copy-start.2
  215.2 0.7 copy-start.3
  215.2 0.7 copy-start.4
  215.2 35.0 %copy-start.1 = (bf16[64,2,2048]{2,1,0:T(2,128)(2,1)S(1)}, bf16[64,2,2048]{2,1,0:T(2,128)(2,1)}, u32[]{:S(2)}) copy-start(bf16[64,2,2048]{2,1,0:T(2,128)(2,1)} %param.12) | copy-start | bytes 1572868
  324.2 36.0 %all-to-all-start.1 = ((bf16[128,4,2048]{2,1,0:T(4,128)(2,1)}), bf16[128,4,2048]{2,1,0:T(4,128)(2,1)}, u32[]{:S(2)}, u32[]{:S(2)}) async-start(bf16[128,4,2048]{2,1,0:T(4,128)(2,1)} %reshape.78), calls=%async_computation.2 | async-start | bytes 4194304 | tf_op jit(solution)/shard_map/all_to_all | solution.py:191
Sparse Core Ops, SparseCore 0:
  9.1 35.9 all-gather.2
  63.1 110.5 all-gather.4
  215.3 34.7 reduce-scatter.1

commit v5 on v4

--- a/solution.py
+++ b/solution.py
@@ -183,25 +183,22 @@
     gate_half = w_gate[0]
     up_half = w_up[0]
     down_half = w_down[0]
-    doubled = jnp.repeat(send_rows.reshape(expert_count, slot_cap, model_width), 2, axis=0)
-    received = lax.all_to_all(doubled, ("expert", "head"), split_axis=0, concat_axis=0, tiled=True)
-    sources = received.shape[0]
-    item_count = received.shape[1]
-    flat_rows = received.reshape(sources * item_count, model_width)
-    gathered = lax.all_to_all(
-        expert_half(flat_rows, gate_half, up_half, down_half).reshape(
-            sources, item_count, model_width
-        ),
-        ("expert", "head"),
-        split_axis=0,
-        concat_axis=0,
-        tiled=True,
-    )
-    halves = gathered.reshape(expert_count, 2, slot_cap, model_width).astype(jnp.float32)
-    combined = (
-        (halves[:, 0] + halves[:, 1])
-        .astype(jnp.bfloat16)
-        .reshape(expert_count * slot_cap, model_width)
+    pieces = 2
+    spread = send_rows.reshape(expert_count * pieces, slot_cap // pieces, model_width)
+    received = lax.all_to_all(spread, ("expert", "head"), 0, 0, tiled=True)
+    swap = [(index, index ^ 1) for index in range(lax.axis_size("head"))]
+    from_partner = lax.ppermute(received, "head", swap)
+    both = jnp.concatenate([received, from_partner], axis=1)
+    sources = both.shape[0]
+    item_count = both.shape[1]
+    half_out = expert_half(
+        both.reshape(sources * item_count, model_width), gate_half, up_half, down_half
+    ).reshape(sources, item_count, model_width)
+    mine = half_out[:, : slot_cap // pieces]
+    theirs = lax.ppermute(half_out[:, slot_cap // pieces :], "head", swap)
+    summed_halves = (mine.astype(jnp.float32) + theirs.astype(jnp.float32)).astype(jnp.bfloat16)
+    combined = lax.all_to_all(summed_halves, ("expert", "head"), 0, 0, tiled=True).reshape(
+        expert_count * slot_cap, model_width
     )
     expert_out = lax.dot_general(
         slot_table, combined, (((0,), (0,)), ((), ())), preferred_element_type=jnp.float32

time: 377 us -> 357 us (0.947)
  blocking collectives: 40.6 us -> 29.5 us
  waiting for transfers between devices: 202 us -> 195 us
  Pallas kernels: 36.9 us -> 31.6 us
    all_to_all x1, waiting for transfers between devices: 24.4 us -> 13 us  [shards(): lax.all_to_all(summed_halves, ('expert', 'head'), 0, 0, tiled=True)]
    all_to_all x1, blocking collectives: 40.6 us -> 29.5 us  [shards(): received = lax.all_to_all(spread, ('expert', 'head'), 0, 0, tiled=True)]
    pallas_call x1, Pallas kernels: 36.9 us -> 31.6 us  [flash_attention(): pl.pallas_call(functools.partial(flash_body, scale=scale, key_block=key_b...]
    ppermute x0 -> x2, waiting for transfers between devices: none -> 4.58 us  [the longest x1 2.29 us: shards(): theirs = lax.ppermute(half_out[:, slot_cap // pieces:], 'head', swap)]
    reshape x3 -> x4, local copies, waits for them, and re-layouts: 10.3 us -> 12.9 us  [the longest x1 4.11 us: shards(): half_out = expert_half(both.reshape(sources * item_count, model_width), g...]
  transfers between devices with their start and end apart: 4 -> 6, of which waited for: 4 -> 6; matrix products, arithmetic and copies ran while one was open for 3% -> 3% of each run, Pallas kernels for 0% -> 0%
where the time goes in v5:
time: 357 us; the launch traced here: 356 us
  waiting for transfers between devices  195 us (55%)
  local copies, waits for them, and re-layouts  38 us (11%)
  matrix products  31.8 us (9%)
  Pallas kernels  31.6 us (9%)
  blocking collectives  29.5 us (8%)
  between operations  13.2 us (4%)
  other arithmetic  9.67 us (3%)
  starting transfers between devices  6.64 us (2%)
    all_gather x1, waiting for transfers between devices, shards(): kv_all = lax.all_gather(kv_rows, 'expert', axis=0, tiled=True)  105 us
    all_gather x1, waiting for transfers between devices, shards(): shard_rows = lax.all_gather(table_cells, 'head', axis=0, tiled=True)  37.8 us
    reduce_scatter x1, waiting for transfers between devices, shards(): lax.psum_scatter(product.reshape(count_rows, tables, model_width).astype(...  34 us
    pallas_call x1, Pallas kernels, flash_attention(): pl.pallas_call(functools.partial(flash_body, scale=scale, key_block=key_b...  31.6 us
    all_to_all x1, blocking collectives, shards(): received = lax.all_to_all(spread, ('expert', 'head'), 0, 0, tiled=True)  29.5 us
    all_to_all x1, waiting for transfers between devices, shards(): lax.all_to_all(summed_halves, ('expert', 'head'), 0, 0, tiled=True)  13 us
    dot_general x1, matrix products, expert_half(): lax.dot_general(hidden, down_half, (((0,), (0,)), ((), ())), preferred_el...  7.63 us
    reshape x1, local copies, waits for them, and re-layouts, shards(): flat_rows = shard_rows.reshape(row_cells * tables, model_width)  7.21 us
  transfers between devices with their start and end apart: 6, of which 6 were waited for; matrix products, arithmetic and copies ran while one was open for 3% of the time, Pallas kernels for 0%

profile of v5, /device:TPU:1, one launch (start us, length us, event | category | flops | bytes accessed | tf_op | source)
XLA Modules:
  0.0 355.7 jit_solution(4272653186460884977)
XLA Ops:
  6.5 0.0 copy-start
  6.5 0.7 all-gather.3.cloned.1.call-update
  7.3 0.0 all-gather.5.cloned.1.call-start
  7.3 37.8 %all-gather.3.cloned.1.call-done = bf16[512,2,2048]{2,1,0:T(2,128)(2,1)} async-done(((bf16[64,2,2048]{2,1,0:T(2,128)(2,1)}), bf16[512,2,2048]{2,1,0:T(2,128)(2,1)}) %all-gather.3.cloned.1.call-update) | async-done | bytes 4194320 | tf_op jit(solution)/shard_map/all_gather | solution.py:137
  45.1 7.2 %reshape.62 = bf16[1024,2048]{1,0:T(8,128)(2,1)} reshape(bf16[512,2,2048]{2,1,0:T(2,128)(2,1)} %all-gather.3.cloned.1.call-done) | data formatting | bytes 8388608 | tf_op jit(solution)/shard_map/reshape | solution.py:139
  52.3 6.2 %fusion.19 = bf16[1024,512]{0,1:T(8,128)(2,1)} fusion(bf16[1024,2048]{1,0:T(8,128)(2,1)} %reshape.62, bf16[2048,256]{1,0:T(8,128)(2,1)} %param.15, bf16[2048,256]{1,0:T(8,128)(2,1)} %param.14), kind=kOutput, calls=%fused_computation.20 | convolution fusion | flops 2152202240 | bytes 7340032 | tf_op jit(solution)/shard_map/dot_general | solution.py:147
  58.5 2.3 copy.24
  60.8 2.2 reshape.64
  63.0 0.0 all-gather.5.cloned.1.call-update
  63.0 0.0 reduce-scatter.2.cloned.1.call-start
  63.1 0.7 pad_add_fusion.scalars
  63.7 3.7 %convolution_convert_fusion.3 = bf16[1024,256]{1,0:T(8,128)(2,1)S(1)} fusion(bf16[1024,2048]{1,0:T(8,128)(2,1)} %reshape.62, bf16[2048,256]{1,0:T(8,128)(2,1)} %param.13), kind=kOutput, calls=%fused_computation.21 | convolution fusion | flops 1074003968 | bytes 5767168 | tf_op jit(solution)/shard_map/dot_general | solution.py:141
  67.5 1.0 reshape.63.q_ref
  68.4 105.3 %all-gather.5.cloned.1.call-done.k_ref.v_ref = bf16[8192,1024]{1,0:T(8,128)(2,1)} async-done(((bf16[512,1024]{1,0:T(8,128)(2,1)}), bf16[8192,1024]{1,0:T(8,128)(2,1)}) %all-gather.5.cloned.1.call-update) | async-done | bytes 16777232 | tf_op jit(solution)/shard_map/all_gather | solution.py:151
  173.7 31.6 %shard_map.118 = bf16[512,512]{1,0:T(8,128)(2,1)} custom-call(s32[3]{0:T(128)} %pad_add_fusion.scalars, bf16[512,512]{1,0:T(8,128)(2,1)} %reshape.63.q_ref, bf16[8192,1024]{1,0:T(8,128)(2,1)} %all-gather.5.cloned.1.call-done.k_ref.v_ref, bf16[8192,1024]{1,0:T(8,128)(2,1)} %all-gather.5.cloned.1.call-done.k_ref.v_ref), custom_call_target="tpu_custom_call" | custom-call | flops 8589934592 | bytes 17825792 | tf_op jit(solution)/shard_map/pallas_call | solution.py:91
  205.3 4.6 %convolution_convert_fusion = bf16[512,2,2048]{2,0,1:T(8,128)(2,1)} fusion(bf16[256,2048]{1,0:T(8,128)(2,1)} %param.16, bf16[64,2,8,256]{3,2,1,0:T(8,128)(2,1)} %bitcast.42), kind=kOutput, calls=%fused_computation | convolution fusion | flops 1075838976 | bytes 5767168 | tf_op jit(solution)/shard_map/dot_general | solution.py:158
  209.9 0.0 reduce-scatter.2.cloned.1.call-update
  209.9 0.6 copy-done.3
  210.6 0.0 copy-done.4
  210.6 0.0 copy-done.5
  210.6 0.1 copy.27
  210.7 0.1 add.38
  210.8 34.0 %reduce-scatter.2.cloned.1.call-done = bf16[64,2,2048]{2,0,1:T(8,128)(2,1)} async-done(((bf16[512,2,2048]{2,0,1:T(8,128)(2,1)}), bf16[64,2,2048]{2,0,1:T(8,128)(2,1)}) %reduce-scatter.2.cloned.1.call-update) | async-done | bytes 524304 | tf_op jit(solution)/shard_map/reduce_scatter | solution.py:161
  244.9 1.3 multiply_reduce_fusion
  246.2 2.4 multiply_convert_fusion.1
  248.6 0.5 copy.28
  249.1 1.0 reshape.66
  250.1 2.4 convolution_convert_fusion.2
  252.6 2.5 reshape.67
  255.1 29.5 %all_to_all.10 = bf16[128,2,2048]{2,1,0:T(2,128)(2,1)S(1)} all-to-all(bf16[128,2,2048]{2,1,0:T(2,128)(2,1)} %reshape.67), channel_id=1, replica_groups=mesh['expert'=16,'head'=8] {'expert','head'}, dimensions={0} | all-to-all | bytes 2097152 | tf_op jit(solution)/shard_map/all_to_all | solution.py:188
  284.6 1.2 collective-permute-start
  285.7 2.3 collective-permute-done
  288.0 3.2 pad_maximum_fusion
  291.2 4.0 %reshape.68 = bf16[512,2048]{1,0:T(8,128)(2,1)} reshape(bf16[128,4,2048]{2,1,0:T(4,128)(2,1)} %pad_maximum_fusion) | data formatting | bytes 4194304 | tf_op jit(solution)/shard_map/reshape | solution.py:195
  295.2 5.3 %fusion.13 = f32[704,512]{1,0:T(8,128)} fusion(bf16[512,2048]{1,0:T(8,128)(2,1)} %reshape.68, bf16[1,704,2048]{2,1,0:T(8,128)(2,1)} %param.18), kind=kOutput, calls=%fused_computation.17 | convolution fusion | flops 1476395008 | bytes 6422528 | tf_op jit(solution)/shard_map/dot_general | solution.py:108
  300.4 7.6 %convolution_convert_fusion.1 = bf16[512,2048]{1,0:T(8,128)(2,1)} fusion(bf16[1,704,2048]{2,1,0:T(8,128)(2,1)S(1)} %copy-done, f32[704,512]{1,0:T(8,128)} %fusion.13, bf16[512,2048]{1,0:T(8,128)(2,1)} %reshape.68, bf16[1,704,2048]{2,1,0:T(8,128)(2,1)} %param.19), kind=kOutput, calls=%fused_computation.1 | convolution fusion | flops 2956001280 | bytes 11403264 | tf_op jit(solution)/shard_map/dot_general | solution.py:113
  308.1 4.1 %reshape.69 = bf16[128,4,2048]{2,1,0:T(4,128)(2,1)} reshape(bf16[512,2048]{1,0:T(8,128)(2,1)} %convolution_convert_fusion.1) | data formatting | bytes 4194304 | tf_op jit(solution)/shard_map/reshape | solution.py:196
  312.2 2.9 slice.9
  315.1 0.4 collective-permute-start.1
  315.5 2.3 collective-permute-done.1
  317.8 2.1 add_convert_fusion
  320.0 4.9 %all-to-all-start.1 = ((bf16[128,2,2048]{2,1,0:T(2,128)(2,1)}), bf16[128,2,2048]{2,1,0:T(2,128)(2,1)}, u32[]{:S(2)}, u32[]{:S(2)}) async-start(bf16[128,2,2048]{2,1,0:T(2,128)(2,1)} %add_convert_fusion), calls=%async_computation.2 | async-start | bytes 2097152 | tf_op jit(solution)/shard_map/all_to_all | solution.py:200
  324.9 3.0 copy.26
  328.0 2.9 reshape.65
  330.9 13.0 %all-to-all-done.1 = bf16[128,2,2048]{2,1,0:T(2,128)(2,1)} async-done(((bf16[128,2,2048]{2,1,0:T(2,128)(2,1)}), bf16[128,2,2048]{2,1,0:T(2,128)(2,1)}, u32[]{:S(2)}, u32[]{:S(2)}) %all-to-all-start.1) | async-done | bytes 1048608 | tf_op jit(solution)/shard_map/all_to_all | solution.py:200
  343.9 2.3 reshape.70
  346.1 1.9 fusion.5
  348.0 1.1 reshape.71
  (14 shorter events, 0.0 us)
Async XLA Ops:
  6.5 293.9 %copy-start = (bf16[1,704,2048]{2,1,0:T(8,128)(2,1)S(1)}, bf16[1,704,2048]{2,1,0:T(8,128)(2,1)}, u32[]{:S(2)}) copy-start(bf16[1,704,2048]{2,1,0:T(8,128)(2,1)} %param.20) | copy-start | bytes 8650756
  6.5 38.5 %all-gather.3.cloned.1.call-start = ((), (), s32[]{:S(2)}) async-start(), calls=%async_computation.3 | async-start | bytes 4718592 | tf_op jit(solution)/shard_map/all_gather | solution.py:137
  7.3 166.5 %all-gather.5.cloned.1.call-start = ((), (), s32[]{:S(2)}) async-start(), calls=%async_computation.4 | async-start | bytes 17825792 | tf_op jit(solution)/shard_map/all_gather | solution.py:151
  60.8 2.3 copy-start.6
  63.0 181.9 %reduce-scatter.2.cloned.1.call-start = ((), (), s32[]{:S(2)}) async-start(), calls=%async_computation.5 | async-start | bytes 4718592 | tf_op jit(solution)/shard_map/reduce_scatter | solution.py:161
  209.9 0.7 copy-start.3
  209.9 0.7 copy-start.4
  209.9 0.7 copy-start.5
  209.9 35.0 %copy-start.2 = (bf16[64,2,2048]{2,1,0:T(2,128)(2,1)S(1)}, bf16[64,2,2048]{2,1,0:T(2,128)(2,1)}, u32[]{:S(2)}) copy-start(bf16[64,2,2048]{2,1,0:T(2,128)(2,1)} %param.12) | copy-start | bytes 1572868
  284.6 3.5 collective-permute-start
  312.2 5.7 %copy-start.1 = (bf16[128,4,2048]{2,1,0:T(4,128)(2,1)S(1)}, bf16[128,4,2048]{2,1,0:T(4,128)(2,1)}, u32[]{:S(2)}) copy-start(bf16[128,4,2048]{2,1,0:T(4,128)(2,1)} %reshape.69) | copy-start | bytes 6291460
  315.1 2.7 collective-permute-start.1
  320.0 23.9 %all-to-all-start.1 = ((bf16[128,2,2048]{2,1,0:T(2,128)(2,1)}), bf16[128,2,2048]{2,1,0:T(2,128)(2,1)}, u32[]{:S(2)}, u32[]{:S(2)}) async-start(bf16[128,2,2048]{2,1,0:T(2,128)(2,1)} %add_convert_fusion), calls=%async_computation.2 | async-start | bytes 2097152 | tf_op jit(solution)/shard_map/all_to_all | solution.py:200
Sparse Core Ops, SparseCore 0:
  9.1 35.9 all-gather.2
  63.1 110.5 all-gather.4
  210.1 34.7 reduce-scatter.1

commit v6 on v5

--- a/solution.py
+++ b/solution.py
@@ -55,15 +55,13 @@
 
     @pl.when(j == last)
     def _():
-        rows = scalars[2] + lax.broadcasted_iota(jnp.int32, acc_ref.shape, 0)
-        out = acc_ref[...] / l_ref[...]
-        o_ref[...] = jnp.where(rows < length, out, 0.0).astype(o_ref.dtype)
+        o_ref[...] = (acc_ref[...] / l_ref[...]).astype(o_ref.dtype)
 
 
 def flash_attention(scalars, q_all, kv_all, heads, scale):
     rows = q_all.shape[0]
     keys = kv_all.shape[0]
-    tables = scalars.shape[0] - 1
+    tables = scalars.shape[0]
     key_block = KEY_BLOCK
     nk = keys // key_block
 
@@ -149,21 +147,40 @@
         .reshape(row_cells, tables * 2 * head_width)
     )
     kv_all = lax.all_gather(kv_rows, "expert", axis=0, tiled=True)
-    offset = lax.axis_index("expert") * row_cells
-    scalars = jnp.concatenate(
-        [lengths.astype(jnp.int32), jnp.reshape(offset, (1,)).astype(jnp.int32)]
-    )
-    attended = flash_attention(scalars, q_all, kv_all, head_count, score_scale)
-    count_rows = cell_count * lax.axis_size("head")
-    product = jnp.dot(
-        attended.reshape(count_rows * tables, head_width), w_out, preferred_element_type=jnp.float32
-    )
-    summed = lax.psum_scatter(
-        product.reshape(count_rows, tables, model_width).astype(jnp.bfloat16),
-        "head",
-        scatter_dimension=0,
-        tiled=True,
-    ).astype(jnp.float32)
+    head_size = lax.axis_size("head")
+    chunks = 2
+    q_chunks = q_all.reshape(head_size, chunks, cell_count // chunks, tables * head_width)
+    parts = []
+    for chunk in range(chunks):
+        attended = flash_attention(
+            lengths.astype(jnp.int32),
+            q_chunks[:, chunk].reshape(row_cells // chunks, tables * head_width),
+            kv_all,
+            head_count,
+            score_scale,
+        )
+        product = jnp.dot(
+            attended.reshape(row_cells // chunks * tables, head_width),
+            w_out,
+            preferred_element_type=jnp.float32,
+        )
+        parts.append(
+            lax.psum_scatter(
+                product.reshape(row_cells // chunks, tables, model_width).astype(jnp.bfloat16),
+                "head",
+                scatter_dimension=0,
+                tiled=True,
+            )
+        )
+    own_cells = (
+        lax.axis_index("expert") * row_cells
+        + lax.axis_index("head") * cell_count
+        + jnp.arange(cell_count, dtype=jnp.int32)
+    )
+    live = own_cells[:, None] < lengths[None, :]
+    summed = jnp.where(
+        live[:, :, None], jnp.concatenate(parts, axis=0).astype(jnp.float32), 0.0
+    )
     residual = table_cells.astype(jnp.float32) + summed
     mean_square = jnp.mean(residual * residual, axis=-1, keepdims=True)
     normed = (residual * lax.rsqrt(mean_square + 1e-06) * norm_gain.astype(jnp.float32)).astype(

time: 357 us -> 375 us (1.050)
  Pallas kernels: 31.6 us -> 42.8 us
  waiting for transfers between devices: 195 us -> 200 us
    pallas_call x1 -> x2, Pallas kernels: 31.6 us -> 42.8 us  [flash_attention(): pl.pallas_call(functools.partial(flash_body, scale=scale, key_block=key_b...]
    reduce_scatter x1 -> x2, waiting for transfers between devices: 34 us -> 39.9 us  [shards(): lax.psum_scatter(product.reshape(row_cells // chunks, tables, model_width...]
  transfers between devices with their start and end apart: 6 -> 7, of which waited for: 6 -> 7; matrix products, arithmetic and copies ran while one was open for 3% -> 4% of each run, Pallas kernels for 0% -> 6%
where the time goes in v6:
time: 375 us; the launch traced here: 374 us
  waiting for transfers between devices  200 us (53%)
  Pallas kernels  42.8 us (11%)
  local copies, waits for them, and re-layouts  39.4 us (11%)
  matrix products  34.8 us (9%)
  blocking collectives  29.3 us (8%)
  between operations  13.3 us (4%)
  other arithmetic  7.1 us (2%)
  starting transfers between devices  6.79 us (2%)
    all_gather x1, waiting for transfers between devices, shards(): kv_all = lax.all_gather(kv_rows, 'expert', axis=0, tiled=True)  104 us
    pallas_call x2, Pallas kernels, flash_attention(): pl.pallas_call(functools.partial(flash_body, scale=scale, key_block=key_b...  42.8 us
    reduce_scatter x2, waiting for transfers between devices, shards(): lax.psum_scatter(product.reshape(row_cells // chunks, tables, model_width...  39.9 us
    all_gather x1, waiting for transfers between devices, shards(): shard_rows = lax.all_gather(table_cells, 'head', axis=0, tiled=True)  37.8 us
    all_to_all x1, blocking collectives, shards(): received = lax.all_to_all(spread, ('expert', 'head'), 0, 0, tiled=True)  29.3 us
    all_to_all x1, waiting for transfers between devices, shards(): lax.all_to_all(summed_halves, ('expert', 'head'), 0, 0, tiled=True)  13.1 us
    dot_general x1, matrix products, expert_half(): lax.dot_general(hidden, down_half, (((0,), (0,)), ((), ())), preferred_el...  7.64 us
  transfers between devices with their start and end apart: 7, of which 7 were waited for; matrix products, arithmetic and copies ran while one was open for 4% of the time, Pallas kernels for 6%

profile of v6, /device:TPU:1, one launch (start us, length us, event | category | flops | bytes accessed | tf_op | source)
XLA Modules:
  0.0 373.7 jit_solution(16691841620845932680)
XLA Ops:
  6.5 0.7 all-gather.3.cloned.1.call-update
  7.3 0.0 all-gather.5.cloned.1.call-start
  7.3 37.8 %all-gather.3.cloned.1.call-done = bf16[512,2,2048]{2,1,0:T(2,128)(2,1)} async-done(((bf16[64,2,2048]{2,1,0:T(2,128)(2,1)}), bf16[512,2,2048]{2,1,0:T(2,128)(2,1)}) %all-gather.3.cloned.1.call-update) | async-done | bytes 4194320 | tf_op jit(solution)/shard_map/all_gather | solution.py:135
  45.1 7.2 %reshape.89 = bf16[1024,2048]{1,0:T(8,128)(2,1)} reshape(bf16[512,2,2048]{2,1,0:T(2,128)(2,1)} %all-gather.3.cloned.1.call-done) | data formatting | bytes 8388608 | tf_op jit(solution)/shard_map/reshape | solution.py:137
  52.3 6.2 %fusion.19 = bf16[1024,512]{0,1:T(8,128)(2,1)} fusion(bf16[1024,2048]{1,0:T(8,128)(2,1)} %reshape.89, bf16[2048,256]{1,0:T(8,128)(2,1)} %param.15, bf16[2048,256]{1,0:T(8,128)(2,1)} %param.14), kind=kOutput, calls=%fused_computation.21 | convolution fusion | flops 2152202240 | bytes 7340032 | tf_op jit(solution)/shard_map/dot_general | solution.py:145
  58.5 2.3 copy.31
  60.8 2.2 reshape.90
  63.0 0.0 reduce-scatter.5.cloned.1.call-start
  63.1 4.5 %convolution_convert_fusion.4 = bf16[1024,256]{1,0:T(8,128)(2,1)} fusion(bf16[1024,2048]{1,0:T(8,128)(2,1)} %reshape.89, bf16[2048,256]{1,0:T(8,128)(2,1)} %param.13), kind=kOutput, calls=%fused_computation.22 | convolution fusion | flops 1074003968 | bytes 5767168 | tf_op jit(solution)/shard_map/dot_general | solution.py:139
  67.6 1.2 reshape_reshape.3
  68.8 0.8 fusion.37
  69.6 104.1 %all-gather.5.cloned.1.call-done.k_ref.v_ref = bf16[8192,1024]{1,0:T(8,128)(2,1)} async-done(((bf16[512,1024]{1,0:T(8,128)(2,1)}), bf16[8192,1024]{1,0:T(8,128)(2,1)}) %all-gather.5.cloned.1.call-update) | async-done | bytes 16777232 | tf_op jit(solution)/shard_map/all_gather | solution.py:149
  173.7 21.4 %shard_map.119 = bf16[256,512]{1,0:T(8,128)(2,1)} custom-call(s32[2]{0:T(128)} %scalars.3, bf16[256,512]{1,0:T(8,128)(2,1)} %bitcast.54, bf16[8192,1024]{1,0:T(8,128)(2,1)} %all-gather.5.cloned.1.call-done.k_ref.v_ref, bf16[8192,1024]{1,0:T(8,128)(2,1)} %all-gather.5.cloned.1.call-done.k_ref.v_ref), custom_call_target="tpu_custom_call" | custom-call | flops 4294967296 | bytes 17301504 | tf_op jit(solution)/shard_map/pallas_call | solution.py:89
  195.1 3.4 convolution_convert_fusion
  198.5 0.2 reduce-scatter.3.cloned.1.call-start
  198.7 21.4 %shard_map.118 = bf16[256,512]{1,0:T(8,128)(2,1)} custom-call(s32[2]{0:T(128)} %scalars.3, bf16[256,512]{1,0:T(8,128)(2,1)} %bitcast.53, bf16[8192,1024]{1,0:T(8,128)(2,1)} %all-gather.5.cloned.1.call-done.k_ref.v_ref, bf16[8192,1024]{1,0:T(8,128)(2,1)} %all-gather.5.cloned.1.call-done.k_ref.v_ref), custom_call_target="tpu_custom_call" | custom-call | flops 4294967296 | bytes 17301504 | tf_op jit(solution)/shard_map/pallas_call | solution.py:89
  220.2 3.4 convolution_convert_fusion.1
  223.7 0.1 copy.36
  223.8 0.1 add.56
  224.0 0.1 broadcast_compare_fusion
  224.1 5.1 %reduce-scatter.5.cloned.1.call-done = bf16[32,2,2048]{2,0,1:T(8,128)(2,1)} async-done(((bf16[256,2,2048]{2,0,1:T(8,128)(2,1)}), bf16[32,2,2048]{2,0,1:T(8,128)(2,1)}) %reduce-scatter.5.cloned.1.call-update) | async-done | bytes 262160 | tf_op jit(solution)/shard_map/reduce_scatter | solution.py:168
  229.2 34.8 %reduce-scatter.3.cloned.1.call-done = bf16[32,2,2048]{2,0,1:T(8,128)(2,1)} async-done(((bf16[256,2,2048]{2,0,1:T(8,128)(2,1)}), bf16[32,2,2048]{2,0,1:T(8,128)(2,1)}) %reduce-scatter.3.cloned.1.call-update) | async-done | bytes 262160 | tf_op jit(solution)/shard_map/reduce_scatter | solution.py:168
  264.0 1.5 multiply_reduce_fusion
  265.5 1.0 copy-done.1
  266.5 0.2 multiply_convert_fusion.1
  266.6 0.5 copy.37
  267.2 1.0 reshape.92
  268.2 2.5 convolution_convert_fusion.3
  270.6 2.6 reshape.93
  273.2 29.3 %all_to_all.10 = bf16[128,2,2048]{2,1,0:T(2,128)(2,1)S(1)} all-to-all(bf16[128,2,2048]{2,1,0:T(2,128)(2,1)} %reshape.93), channel_id=1, replica_groups=mesh['expert'=16,'head'=8] {'expert','head'}, dimensions={0} | all-to-all | bytes 2097152 | tf_op jit(solution)/shard_map/all_to_all | solution.py:205
  302.5 1.2 collective-permute-start
  303.7 2.3 collective-permute-done
  306.0 3.2 pad_maximum_fusion
  309.2 4.0 %reshape.94 = bf16[512,2048]{1,0:T(8,128)(2,1)} reshape(bf16[128,4,2048]{2,1,0:T(4,128)(2,1)} %pad_maximum_fusion) | data formatting | bytes 4194304 | tf_op jit(solution)/shard_map/reshape | solution.py:212
  313.1 5.3 %fusion.13 = f32[704,512]{1,0:T(8,128)} fusion(bf16[512,2048]{1,0:T(8,128)(2,1)} %reshape.94, bf16[1,704,2048]{2,1,0:T(8,128)(2,1)} %param.18), kind=kOutput, calls=%fused_computation.18 | convolution fusion | flops 1476395008 | bytes 6422528 | tf_op jit(solution)/shard_map/dot_general | solution.py:106
  318.4 7.6 %convolution_convert_fusion.2 = bf16[512,2048]{1,0:T(8,128)(2,1)} fusion(bf16[1,704,2048]{2,1,0:T(8,128)(2,1)S(1)} %copy-done, f32[704,512]{1,0:T(8,128)} %fusion.13, bf16[512,2048]{1,0:T(8,128)(2,1)} %reshape.94, bf16[1,704,2048]{2,1,0:T(8,128)(2,1)} %param.19), kind=kOutput, calls=%fused_computation.2 | convolution fusion | flops 2956001280 | bytes 11403264 | tf_op jit(solution)/shard_map/dot_general | solution.py:111
  326.0 4.1 %reshape.95 = bf16[128,4,2048]{2,1,0:T(4,128)(2,1)} reshape(bf16[512,2048]{1,0:T(8,128)(2,1)} %convolution_convert_fusion.2) | data formatting | bytes 4194304 | tf_op jit(solution)/shard_map/reshape | solution.py:213
  330.2 2.9 slice.19
  333.1 0.5 collective-permute-start.1
  333.5 2.3 collective-permute-done.1
  335.8 2.1 add_convert_fusion
  338.0 4.9 %all-to-all-start.1 = ((bf16[128,2,2048]{2,1,0:T(2,128)(2,1)}), bf16[128,2,2048]{2,1,0:T(2,128)(2,1)}, u32[]{:S(2)}, u32[]{:S(2)}) async-start(bf16[128,2,2048]{2,1,0:T(2,128)(2,1)} %add_convert_fusion), calls=%async_computation.3 | async-start | bytes 2097152 | tf_op jit(solution)/shard_map/all_to_all | solution.py:217
  342.8 3.0 copy.35
  345.9 2.9 reshape.91
  348.8 13.1 %all-to-all-done.1 = bf16[128,2,2048]{2,1,0:T(2,128)(2,1)} async-done(((bf16[128,2,2048]{2,1,0:T(2,128)(2,1)}), bf16[128,2,2048]{2,1,0:T(2,128)(2,1)}, u32[]{:S(2)}, u32[]{:S(2)}) %all-to-all-start.1) | async-done | bytes 1048608 | tf_op jit(solution)/shard_map/all_to_all | solution.py:217
  361.9 2.3 reshape.96
  364.2 1.9 fusion.5
  366.1 1.1 reshape.97
  (23 shorter events, 0.1 us)
Async XLA Ops:
  6.5 311.9 %copy-start = (bf16[1,704,2048]{2,1,0:T(8,128)(2,1)S(1)}, bf16[1,704,2048]{2,1,0:T(8,128)(2,1)}, u32[]{:S(2)}) copy-start(bf16[1,704,2048]{2,1,0:T(8,128)(2,1)} %param.20) | copy-start | bytes 8650756
  6.5 38.5 %all-gather.3.cloned.1.call-start = ((), (), s32[]{:S(2)}) async-start(), calls=%async_computation.4 | async-start | bytes 4718592 | tf_op jit(solution)/shard_map/all_gather | solution.py:135
  7.3 166.5 %all-gather.5.cloned.1.call-start = ((), (), s32[]{:S(2)}) async-start(), calls=%async_computation.5 | async-start | bytes 17825792 | tf_op jit(solution)/shard_map/all_gather | solution.py:149
  63.0 166.2 %reduce-scatter.5.cloned.1.call-start = ((), (), s32[]{:S(2)}) async-start(), calls=%async_computation.7 | async-start | bytes 2359296 | tf_op jit(solution)/shard_map/reduce_scatter | solution.py:168
  198.5 65.5 %reduce-scatter.3.cloned.1.call-start = ((), (), s32[]{:S(2)}) async-start(), calls=%async_computation.6 | async-start | bytes 2359296 | tf_op jit(solution)/shard_map/reduce_scatter | solution.py:168
  220.2 3.5 copy-start.4
  220.2 3.5 copy-start.6
  220.2 3.5 copy-start.7
  220.2 3.8 %copy-start.5 = (s32[2]{0:T(128)S(1)}, s32[2]{0:T(128)}, u32[]{:S(2)}) copy-start(s32[2]{0:T(128)} %scalars.3) | copy-start | bytes 28
  220.2 43.8 %copy-start.3 = (bf16[64,2,2048]{2,1,0:T(2,128)(2,1)S(1)}, bf16[64,2,2048]{2,1,0:T(2,128)(2,1)}, u32[]{:S(2)}) copy-start(bf16[64,2,2048]{2,1,0:T(2,128)(2,1)} %param.12) | copy-start | bytes 1572868
  265.5 1.0 copy-start.1
  302.5 3.5 collective-permute-start
  330.2 5.7 %copy-start.2 = (bf16[128,4,2048]{2,1,0:T(4,128)(2,1)S(1)}, bf16[128,4,2048]{2,1,0:T(4,128)(2,1)}, u32[]{:S(2)}) copy-start(bf16[128,4,2048]{2,1,0:T(4,128)(2,1)} %reshape.95) | copy-start | bytes 6291460
  333.1 2.8 collective-permute-start.1
  338.0 23.9 %all-to-all-start.1 = ((bf16[128,2,2048]{2,1,0:T(2,128)(2,1)}), bf16[128,2,2048]{2,1,0:T(2,128)(2,1)}, u32[]{:S(2)}, u32[]{:S(2)}) async-start(bf16[128,2,2048]{2,1,0:T(2,128)(2,1)} %add_convert_fusion), calls=%async_computation.3 | async-start | bytes 2097152 | tf_op jit(solution)/shard_map/all_to_all | solution.py:217
Sparse Core Ops, SparseCore 0:
  9.1 35.9 all-gather.2
  63.1 110.5 all-gather.4
  198.6 30.4 reduce-scatter.4
  231.4 32.4 reduce-scatter.2

commit v7 on v5

--- a/solution.py
+++ b/solution.py
@@ -154,16 +154,26 @@
         [lengths.astype(jnp.int32), jnp.reshape(offset, (1,)).astype(jnp.int32)]
     )
     attended = flash_attention(scalars, q_all, kv_all, head_count, score_scale)
-    count_rows = cell_count * lax.axis_size("head")
-    product = jnp.dot(
-        attended.reshape(count_rows * tables, head_width), w_out, preferred_element_type=jnp.float32
-    )
-    summed = lax.psum_scatter(
-        product.reshape(count_rows, tables, model_width).astype(jnp.bfloat16),
-        "head",
-        scatter_dimension=0,
-        tiled=True,
-    ).astype(jnp.float32)
+    head_size = lax.axis_size("head")
+    me_head = lax.axis_index("head")
+    w_parts = [w_out]
+    for shift in range(1, head_size):
+        w_parts.append(
+            lax.ppermute(
+                w_out, "head", [(index, (index + shift) % head_size) for index in range(head_size)]
+            )
+        )
+    w_rel = jnp.concatenate(w_parts, axis=0)
+    by_owner = lax.all_to_all(
+        attended.reshape(head_size, cell_count, tables, head_width), "head", 0, 0, tiled=True
+    )
+    groups_rel = (me_head - jnp.arange(head_size)) % head_size
+    rel = jnp.take(by_owner, groups_rel, axis=0).transpose(1, 2, 0, 3)
+    summed = jnp.dot(
+        rel.reshape(cell_count * tables, head_size * head_width),
+        w_rel,
+        preferred_element_type=jnp.float32,
+    ).reshape(cell_count, tables, model_width)
     residual = table_cells.astype(jnp.float32) + summed
     mean_square = jnp.mean(residual * residual, axis=-1, keepdims=True)
     normed = (residual * lax.rsqrt(mean_square + 1e-06) * norm_gain.astype(jnp.float32)).astype(

time: 357 us -> 347 us (0.972)
  waiting for transfers between devices: 195 us -> 145 us
  local copies, waits for them, and re-layouts: 38 us -> 63.6 us
  starting transfers between devices: 6.64 us -> 21 us
  Pallas kernels: 31.6 us -> 36.7 us
  blocking collectives: 29.5 us -> 25.5 us
    all_gather x1, waiting for transfers between devices: 105 us -> 5.55 us  [shards(): kv_all = lax.all_gather(kv_rows, 'expert', axis=0, tiled=True)]
    ppermute x0 -> x7, waiting for transfers between devices: none -> 78.7 us  [shards(): lax.ppermute(w_out, 'head', [(index, (index + shift) % head_size) for ind...]
    reduce_scatter x1 -> x0, waiting for transfers between devices: 34 us -> none  [shards(): lax.psum_scatter(product.reshape(count_rows, tables, model_width).astype(...]
    unnamed x14 -> x23, local copies, waits for them, and re-layouts: 0.69 us -> 17.4 us
    ppermute x0 -> x7, starting transfers between devices: none -> 9.22 us  [shards(): lax.ppermute(w_out, 'head', [(index, (index + shift) % head_size) for ind...]
    all_to_all x0 -> x1, starting transfers between devices: none -> 5.13 us  [shards(): lax.all_to_all(attended.reshape(head_size, cell_count, tables, head_width...]
    pallas_call x1, Pallas kernels: 31.6 us -> 36.7 us  [flash_attention(): pl.pallas_call(functools.partial(flash_body, scale=scale, key_block=key_b...]
    all_to_all x0 -> x1, waiting for transfers between devices: none -> 4.77 us  [shards(): lax.all_to_all(attended.reshape(head_size, cell_count, tables, head_width...]
  transfers between devices with their start and end apart: 6 -> 13, of which waited for: 6 -> 8; matrix products, arithmetic and copies ran while one was open for 3% -> 9% of each run, Pallas kernels for 0% -> 11%
where the time goes in v7:
time: 347 us; the launch traced here: 346 us
  waiting for transfers between devices  145 us (42%)
  local copies, waits for them, and re-layouts  63.6 us (18%)
  Pallas kernels  36.7 us (11%)
  matrix products  29.5 us (9%)
  blocking collectives  25.5 us (7%)
  starting transfers between devices  21 us (6%)
  between operations  13.5 us (4%)
  other arithmetic  10.6 us (3%)
    ppermute x7, waiting for transfers between devices, shards(): lax.ppermute(w_out, 'head', [(index, (index + shift) % head_size) for ind...  78.7 us
    all_gather x1, waiting for transfers between devices, shards(): shard_rows = lax.all_gather(table_cells, 'head', axis=0, tiled=True)  37.8 us
    pallas_call x1, Pallas kernels, flash_attention(): pl.pallas_call(functools.partial(flash_body, scale=scale, key_block=key_b...  36.7 us
    all_to_all x1, blocking collectives, shards(): received = lax.all_to_all(spread, ('expert', 'head'), 0, 0, tiled=True)  25.5 us
    unnamed x23, local copies, waits for them, and re-layouts  17.4 us
    all_to_all x1, waiting for transfers between devices, shards(): lax.all_to_all(summed_halves, ('expert', 'head'), 0, 0, tiled=True)  13 us
    ppermute x7, starting transfers between devices, shards(): lax.ppermute(w_out, 'head', [(index, (index + shift) % head_size) for ind...  9.22 us
    dot_general x1, matrix products, expert_half(): lax.dot_general(hidden, down_half, (((0,), (0,)), ((), ())), preferred_el...  7.62 us
  transfers between devices with their start and end apart: 13, of which 8 were waited for; matrix products, arithmetic and copies ran while one was open for 9% of the time, Pallas kernels for 11%

profile of v7, /device:TPU:1, one launch (start us, length us, event | category | flops | bytes accessed | tf_op | source)
XLA Modules:
  0.0 345.5 jit_solution(14677243490622225607)
XLA Ops:
  7.3 37.8 %all-gather.3.cloned.1.call-done = bf16[512,2,2048]{2,1,0:T(2,128)(2,1)} async-done(((bf16[64,2,2048]{2,1,0:T(2,128)(2,1)}), bf16[512,2,2048]{2,1,0:T(2,128)(2,1)}) %all-gather.3.cloned.1.call-update) | async-done | bytes 4194320 | tf_op jit(solution)/shard_map/all_gather | solution.py:137
  45.1 7.2 %reshape.119 = bf16[1024,2048]{1,0:T(8,128)(2,1)} reshape(bf16[512,2,2048]{2,1,0:T(2,128)(2,1)} %all-gather.3.cloned.1.call-done) | data formatting | bytes 8388608 | tf_op jit(solution)/shard_map/reshape | solution.py:139
  52.3 6.2 %fusion.23 = bf16[1024,512]{0,1:T(8,128)(2,1)} fusion(bf16[1024,2048]{1,0:T(8,128)(2,1)} %reshape.119, bf16[2048,256]{1,0:T(8,128)(2,1)} %param.15, bf16[2048,256]{1,0:T(8,128)(2,1)} %param.14), kind=kOutput, calls=%fused_computation.21 | convolution fusion | flops 2152202240 | bytes 7340032 | tf_op jit(solution)/shard_map/dot_general | solution.py:147
  58.5 2.3 copy.24
  60.7 2.3 reshape.121
  65.4 1.7 collective-permute-start.3
  67.1 2.6 collective-permute-start.4
  69.8 2.4 constant_dynamic-update-slice_fusion.7
  73.0 12.8 %collective-permute-done = bf16[256,2048]{1,0:T(8,128)(2,1)} collective-permute-done((bf16[256,2048]{1,0:T(8,128)(2,1)}, bf16[256,2048]{1,0:T(8,128)(2,1)}, u32[]{:S(2)}, u32[]{:S(2)}) %collective-permute-start) | collective-permute-done | bytes 1048608 | tf_op jit(solution)/shard_map/ppermute | solution.py:162
  85.8 2.6 collective-permute-start.5
  88.4 2.3 constant_dynamic-update-slice_fusion.6
  90.7 65.8 %collective-permute-done.1 = bf16[256,2048]{1,0:T(8,128)(2,1)} collective-permute-done((bf16[256,2048]{1,0:T(8,128)(2,1)}, bf16[256,2048]{1,0:T(8,128)(2,1)}, u32[]{:S(2)}, u32[]{:S(2)}) %collective-permute-start.1) | collective-permute-done | bytes 1048608 | tf_op jit(solution)/shard_map/ppermute | solution.py:162
  156.5 2.3 constant_dynamic-update-slice_fusion.5
  158.9 2.5 constant_dynamic-update-slice_fusion.4
  161.3 2.3 constant_dynamic-update-slice_fusion.3
  163.7 2.3 constant_dynamic-update-slice_fusion.2
  166.0 1.2 convolution_convert_fusion.2
  168.2 5.5 %all-gather.5.cloned.1.call-done.k_ref.v_ref = bf16[8192,1024]{1,0:T(8,128)(2,1)} async-done(((bf16[512,1024]{1,0:T(8,128)(2,1)}), bf16[8192,1024]{1,0:T(8,128)(2,1)}) %all-gather.5.cloned.1.call-update) | async-done | bytes 16777232 | tf_op jit(solution)/shard_map/all_gather | solution.py:151
  173.8 36.7 %shard_map.118 = bf16[512,512]{1,0:T(8,128)(2,1)} custom-call(s32[3]{0:T(128)} %pad_add_fusion.scalars, bf16[512,512]{1,0:T(8,128)(2,1)} %reshape.120.q_ref, bf16[8192,1024]{1,0:T(8,128)(2,1)} %all-gather.5.cloned.1.call-done.k_ref.v_ref, bf16[8192,1024]{1,0:T(8,128)(2,1)} %all-gather.5.cloned.1.call-done.k_ref.v_ref), custom_call_target="tpu_custom_call" | custom-call | flops 8589934592 | bytes 17825792 | tf_op jit(solution)/shard_map/pallas_call | solution.py:91
  210.5 2.0 reshape.122
  212.4 5.1 %all-to-all-start = ((bf16[8,64,2,256]{3,2,1,0:T(2,128)(2,1)}), bf16[8,64,2,256]{3,2,1,0:T(2,128)(2,1)S(1)}, u32[]{:S(2)}, u32[]{:S(2)}) async-start(bf16[8,64,2,256]{3,2,1,0:T(2,128)(2,1)} %reshape.122), calls=%async_computation | async-start | bytes 1048576 | tf_op jit(solution)/shard_map/all_to_all | solution.py:167
  217.6 2.3 constant_dynamic-update-slice_fusion.1
  219.9 2.4 constant_dynamic-update-slice_fusion
  222.3 4.8 %all-to-all-done = bf16[8,64,2,256]{3,2,1,0:T(2,128)(2,1)S(1)} async-done(((bf16[8,64,2,256]{3,2,1,0:T(2,128)(2,1)}), bf16[8,64,2,256]{3,2,1,0:T(2,128)(2,1)S(1)}, u32[]{:S(2)}, u32[]{:S(2)}) %all-to-all-start) | async-done | bytes 524320 | tf_op jit(solution)/shard_map/all_to_all | solution.py:167
  227.0 2.4 gather_fusion
  229.4 1.6 fusion.31
  232.0 1.3 dot_general.32
  233.3 5.1 %multiply_reduce_fusion = (f32[64,2]{0,1:T(2,128)S(1)}, f32[64,2,2048]{2,0,1:T(8,128)S(1)}) fusion(bf16[64,2,2048]{2,0,1:T(8,128)(2,1)S(1)} %dot_general.32, bf16[2048,2048]{1,0:T(8,128)(2,1)} %constant_dynamic-update-slice_fusion, bf16[64,2,2048]{2,1,0:T(2,128)(2,1)} %param.12), kind=kOutput, calls=%fused_computation.25 | convolution fusion | flops 1074790272 | bytes 10486272 | tf_op jit(solution)/shard_map/dot_general | solution.py:172
  241.1 2.5 convolution_convert_fusion.1
  243.6 2.5 reshape.125
  246.1 25.5 %all_to_all.15 = bf16[128,2,2048]{2,1,0:T(2,128)(2,1)S(1)} all-to-all(bf16[128,2,2048]{2,1,0:T(2,128)(2,1)} %reshape.125), channel_id=1, replica_groups=mesh['expert'=16,'head'=8] {'expert','head'}, dimensions={0} | all-to-all | bytes 2097152 | tf_op jit(solution)/shard_map/all_to_all | solution.py:198
  271.7 1.2 collective-permute-start.7
  272.8 2.3 collective-permute-done.7
  275.1 3.1 pad_maximum_fusion
  278.3 4.0 %reshape.126 = bf16[512,2048]{1,0:T(8,128)(2,1)} reshape(bf16[128,4,2048]{2,1,0:T(4,128)(2,1)} %pad_maximum_fusion) | data formatting | bytes 4194304 | tf_op jit(solution)/shard_map/reshape | solution.py:205
  282.2 5.3 %fusion.17 = f32[704,512]{1,0:T(8,128)} fusion(bf16[512,2048]{1,0:T(8,128)(2,1)} %reshape.126, bf16[1,704,2048]{2,1,0:T(8,128)(2,1)} %param.18), kind=kOutput, calls=%fused_computation.18 | convolution fusion | flops 1476395008 | bytes 6422528 | tf_op jit(solution)/shard_map/dot_general | solution.py:108
  287.5 7.6 %convolution_convert_fusion = bf16[512,2048]{1,0:T(8,128)(2,1)} fusion(bf16[1,704,2048]{2,1,0:T(8,128)(2,1)S(1)} %copy-done, f32[704,512]{1,0:T(8,128)} %fusion.17, bf16[512,2048]{1,0:T(8,128)(2,1)} %reshape.126, bf16[1,704,2048]{2,1,0:T(8,128)(2,1)} %param.19), kind=kOutput, calls=%fused_computation.3 | convolution fusion | flops 2956001280 | bytes 11403264 | tf_op jit(solution)/shard_map/dot_general | solution.py:113
  295.1 4.1 %reshape.127 = bf16[128,4,2048]{2,1,0:T(4,128)(2,1)} reshape(bf16[512,2048]{1,0:T(8,128)(2,1)} %convolution_convert_fusion) | data formatting | bytes 4194304 | tf_op jit(solution)/shard_map/reshape | solution.py:206
  299.2 2.8 slice.11
  302.5 2.3 collective-permute-done.8
  304.7 3.7 %add_convert_fusion = bf16[128,2,2048]{2,1,0:T(2,128)(2,1)} fusion(bf16[128,2,2048]{2,1,0:T(2,128)(2,1)S(1)} %collective-permute-done.8, bf16[128,4,2048]{2,1,0:T(4,128)(2,1)} %reshape.127), kind=kLoop, calls=%fused_computation.16 | loop fusion | flops 2097152 | bytes 3145728 | tf_op jit(solution)/shard_map/convert_element_type | solution.py:209
  308.5 5.0 %all-to-all-start.2 = ((bf16[128,2,2048]{2,1,0:T(2,128)(2,1)}), bf16[128,2,2048]{2,1,0:T(2,128)(2,1)}, u32[]{:S(2)}, u32[]{:S(2)}) async-start(bf16[128,2,2048]{2,1,0:T(2,128)(2,1)} %add_convert_fusion), calls=%async_computation.2 | async-start | bytes 2097152 | tf_op jit(solution)/shard_map/all_to_all | solution.py:210
  313.5 3.0 copy.26
  316.5 2.9 reshape.123
  319.4 13.0 %all-to-all-done.2 = bf16[128,2,2048]{2,1,0:T(2,128)(2,1)} async-done(((bf16[128,2,2048]{2,1,0:T(2,128)(2,1)}), bf16[128,2,2048]{2,1,0:T(2,128)(2,1)}, u32[]{:S(2)}, u32[]{:S(2)}) %all-to-all-start.2) | async-done | bytes 1048608 | tf_op jit(solution)/shard_map/all_to_all | solution.py:210
  332.4 2.2 reshape.128
  334.6 1.6 fusion.32
  336.2 1.3 add_convert_fusion.1
  (45 shorter events, 10.3 us)
Async XLA Ops:
  6.5 281.0 %copy-start = (bf16[1,704,2048]{2,1,0:T(8,128)(2,1)S(1)}, bf16[1,704,2048]{2,1,0:T(8,128)(2,1)}, u32[]{:S(2)}) copy-start(bf16[1,704,2048]{2,1,0:T(8,128)(2,1)} %param.20) | copy-start | bytes 8650756
  6.5 38.5 %all-gather.3.cloned.1.call-start = ((), (), s32[]{:S(2)}) async-start(), calls=%async_computation.3 | async-start | bytes 4718592 | tf_op jit(solution)/shard_map/all_gather | solution.py:137
  7.3 166.5 %all-gather.5.cloned.1.call-start = ((), (), s32[]{:S(2)}) async-start(), calls=%async_computation.4 | async-start | bytes 17825792 | tf_op jit(solution)/shard_map/all_gather | solution.py:151
  60.7 11.4 %copy-start.4 = (s32[64,2]{0,1:T(2,128)S(1)}, s32[64,2]{0,1:T(2,128)}, u32[]{:S(2)}) copy-start(s32[64,2]{0,1:T(2,128)} %param.23) | copy-start | bytes 1540
  60.7 11.4 %copy-start.5 = (s32[64,2]{0,1:T(2,128)S(1)}, s32[64,2]{0,1:T(2,128)}, u32[]{:S(2)}) copy-start(s32[64,2]{0,1:T(2,128)} %param.22) | copy-start | bytes 1540
  60.7 11.4 %copy-start.7 = (s32[2]{0:T(128)S(1)}, s32[2]{0:T(128)}, u32[]{:S(2)}) copy-start(s32[2]{0:T(128)} %param.21) | copy-start | bytes 28
  60.7 12.0 %copy-start.3 = (bf16[2048]{0:T(1024)(128)(2,1)S(1)}, bf16[2048]{0:T(1024)(128)(2,1)}, u32[]{:S(2)}) copy-start(bf16[2048]{0:T(1024)(128)(2,1)} %param.17) | copy-start | bytes 12292
  63.1 22.8 %collective-permute-start = (bf16[256,2048]{1,0:T(8,128)(2,1)}, bf16[256,2048]{1,0:T(8,128)(2,1)}, u32[]{:S(2)}, u32[]{:S(2)}) collective-permute-start(bf16[256,2048]{1,0:T(8,128)(2,1)} %param.16), channel_id=1, source_target_pairs={{0,1},{1,2},{2,3},{3,4},{4,5},{5,6},{6,7},{7,0},{8,9},{9,10},{10,1... | collective-permute-start | bytes 3145736 | tf_op jit(solution)/shard_map/ppermute | solution.py:162
  63.3 93.2 %collective-permute-start.1 = (bf16[256,2048]{1,0:T(8,128)(2,1)}, bf16[256,2048]{1,0:T(8,128)(2,1)}, u32[]{:S(2)}, u32[]{:S(2)}) collective-permute-start(bf16[256,2048]{1,0:T(8,128)(2,1)} %param.16), channel_id=1, source_target_pairs={{0,2},{1,3},{2,4},{3,5},{4,6},{5,7},{6,0},{7,1},{8,10},{9,11},{10,... | collective-permute-start | bytes 3145736 | tf_op jit(solution)/shard_map/ppermute | solution.py:162
  64.3 94.6 %collective-permute-start.2 = (bf16[256,2048]{1,0:T(8,128)(2,1)}, bf16[256,2048]{1,0:T(8,128)(2,1)}, u32[]{:S(2)}, u32[]{:S(2)}) collective-permute-start(bf16[256,2048]{1,0:T(8,128)(2,1)} %param.16), channel_id=1, source_target_pairs={{0,3},{1,4},{2,5},{3,6},{4,7},{5,0},{6,1},{7,2},{8,11},{9,12},{10,... | collective-permute-start | bytes 3145736 | tf_op jit(solution)/shard_map/ppermute | solution.py:162
  65.4 95.9 %collective-permute-start.3 = (bf16[256,2048]{1,0:T(8,128)(2,1)}, bf16[256,2048]{1,0:T(8,128)(2,1)}, u32[]{:S(2)}, u32[]{:S(2)}) collective-permute-start(bf16[256,2048]{1,0:T(8,128)(2,1)} %param.16), channel_id=1, source_target_pairs={{0,4},{1,5},{2,6},{3,7},{4,0},{5,1},{6,2},{7,3},{8,12},{9,13},{10,... | collective-permute-start | bytes 3145736 | tf_op jit(solution)/shard_map/ppermute | solution.py:162
  67.1 96.6 %collective-permute-start.4 = (bf16[256,2048]{1,0:T(8,128)(2,1)}, bf16[256,2048]{1,0:T(8,128)(2,1)}, u32[]{:S(2)}, u32[]{:S(2)}) collective-permute-start(bf16[256,2048]{1,0:T(8,128)(2,1)} %param.16), channel_id=1, source_target_pairs={{0,5},{1,6},{2,7},{3,0},{4,1},{5,2},{6,3},{7,4},{8,13},{9,14},{10,... | collective-permute-start | bytes 3145736 | tf_op jit(solution)/shard_map/ppermute | solution.py:162
  85.8 131.7 %collective-permute-start.5 = (bf16[256,2048]{1,0:T(8,128)(2,1)}, bf16[256,2048]{1,0:T(8,128)(2,1)}, u32[]{:S(2)}, u32[]{:S(2)}) collective-permute-start(bf16[256,2048]{1,0:T(8,128)(2,1)} %param.16), channel_id=1, source_target_pairs={{0,6},{1,7},{2,0},{3,1},{4,2},{5,3},{6,4},{7,5},{8,14},{9,15},{10,... | collective-permute-start | bytes 3145736 | tf_op jit(solution)/shard_map/ppermute | solution.py:162
  156.5 63.3 %collective-permute-start.6 = (bf16[256,2048]{1,0:T(8,128)(2,1)}, bf16[256,2048]{1,0:T(8,128)(2,1)}, u32[]{:S(2)}, u32[]{:S(2)}) collective-permute-start(bf16[256,2048]{1,0:T(8,128)(2,1)} %param.16), channel_id=1, source_target_pairs={{0,7},{1,0},{2,1},{3,2},{4,3},{5,4},{6,5},{7,6},{8,15},{9,8},{10,9... | collective-permute-start | bytes 3145736 | tf_op jit(solution)/shard_map/ppermute | solution.py:162
  158.9 7.1 %copy-start.2 = (bf16[1024,2048]{1,0:T(8,128)(2,1)S(1)}, bf16[1024,2048]{1,0:T(8,128)(2,1)}, u32[]{:S(2)}) copy-start(bf16[1024,2048]{1,0:T(8,128)(2,1)} %reshape.119) | copy-start | bytes 12582916
  158.9 7.1 %copy-start.6 = (bf16[2048,256]{1,0:T(8,128)(2,1)S(1)}, bf16[2048,256]{1,0:T(8,128)(2,1)}, u32[]{:S(2)}) copy-start(bf16[2048,256]{1,0:T(8,128)(2,1)} %param.13) | copy-start | bytes 3145732
  212.4 14.6 %all-to-all-start = ((bf16[8,64,2,256]{3,2,1,0:T(2,128)(2,1)}), bf16[8,64,2,256]{3,2,1,0:T(2,128)(2,1)S(1)}, u32[]{:S(2)}, u32[]{:S(2)}) async-start(bf16[8,64,2,256]{3,2,1,0:T(2,128)(2,1)} %reshape.122), calls=%async_computation | async-start | bytes 1048576 | tf_op jit(solution)/shard_map/all_to_all | solution.py:167
  238.5 1.0 copy-start.1
  271.7 3.5 collective-permute-start.7
  302.0 2.7 collective-permute-start.8
  308.5 23.9 %all-to-all-start.2 = ((bf16[128,2,2048]{2,1,0:T(2,128)(2,1)}), bf16[128,2,2048]{2,1,0:T(2,128)(2,1)}, u32[]{:S(2)}, u32[]{:S(2)}) async-start(bf16[128,2,2048]{2,1,0:T(2,128)(2,1)} %add_convert_fusion), calls=%async_computation.2 | async-start | bytes 2097152 | tf_op jit(solution)/shard_map/all_to_all | solution.py:210
Sparse Core Ops, SparseCore 0:
  9.1 35.9 all-gather.2
  63.2 110.5 all-gather.4

commit v8 on v7

--- a/solution.py
+++ b/solution.py
@@ -134,9 +134,9 @@
     head_width = w_query.shape[1]
     head_count = head_width // DH
     score_scale = 1.0 / math.sqrt(DH)
-    shard_rows = lax.all_gather(table_cells, "head", axis=0, tiled=True)
-    row_cells = shard_rows.shape[0]
-    flat_rows = shard_rows.reshape(row_cells * tables, model_width)
+    cells_flat = table_cells.reshape(cell_count * tables, model_width)
+    flat_rows = lax.all_gather(cells_flat, "head", axis=0, tiled=True)
+    row_cells = flat_rows.shape[0] // tables
     q_all = (
         jnp.dot(flat_rows, w_query, preferred_element_type=jnp.float32)
         .astype(jnp.bfloat16)
@@ -173,8 +173,8 @@
         rel.reshape(cell_count * tables, head_size * head_width),
         w_rel,
         preferred_element_type=jnp.float32,
-    ).reshape(cell_count, tables, model_width)
-    residual = table_cells.astype(jnp.float32) + summed
+    )
+    residual = cells_flat.astype(jnp.float32) + summed
     mean_square = jnp.mean(residual * residual, axis=-1, keepdims=True)
     normed = (residual * lax.rsqrt(mean_square + 1e-06) * norm_gain.astype(jnp.float32)).astype(
         jnp.bfloat16

time: 347 us -> 327 us (0.942)
  blocking collectives: 25.5 us -> 48.7 us
  waiting for transfers between devices: 145 us -> 130 us
  local copies, waits for them, and re-layouts: 63.6 us -> 49.6 us
  Pallas kernels: 36.7 us -> 31.4 us
  starting transfers between devices: 21 us -> 16.3 us
    all_to_all x0 -> x1, blocking collectives: none -> 23.2 us  [shards(): lax.all_to_all(summed_halves, ('expert', 'head'), 0, 0, tiled=True)]
    all_to_all x1 -> x0, waiting for transfers between devices: 13 us -> none  [shards(): lax.all_to_all(summed_halves, ('expert', 'head'), 0, 0, tiled=True)]
    reshape x3 -> x1, local copies, waits for them, and re-layouts: 11.1 us -> 2.18 us  [shards(): cells_flat = table_cells.reshape(cell_count * tables, model_width)]
    pallas_call x1, Pallas kernels: 36.7 us -> 31.4 us  [flash_attention(): pl.pallas_call(functools.partial(flash_body, scale=scale, key_block=key_b...]
    all_to_all x1 -> x0, starting transfers between devices: 4.99 us -> none  [shards(): lax.all_to_all(summed_halves, ('expert', 'head'), 0, 0, tiled=True)]
    unnamed x23 -> x26, local copies, waits for them, and re-layouts: 17.4 us -> 17.5 us
  transfers between devices with their start and end apart: 13 -> 12, of which waited for: 8 -> 7; matrix products, arithmetic and copies ran while one was open for 9% -> 7% of each run, Pallas kernels for 11% -> 10%
where the time goes in v8:
time: 327 us; the launch traced here: 326 us
  waiting for transfers between devices  130 us (40%)
  local copies, waits for them, and re-layouts  49.6 us (15%)
  blocking collectives  48.7 us (15%)
  Pallas kernels  31.4 us (10%)
  matrix products  28.5 us (9%)
  starting transfers between devices  16.3 us (5%)
  between operations  13.5 us (4%)
  other arithmetic  7.73 us (2%)
    ppermute x7, waiting for transfers between devices, shards(): lax.ppermute(w_out, 'head', [(index, (index + shift) % head_size) for ind...  78.6 us
    all_gather x1, waiting for transfers between devices, shards(): flat_rows = lax.all_gather(cells_flat, 'head', axis=0, tiled=True)  36.3 us
    pallas_call x1, Pallas kernels, flash_attention(): pl.pallas_call(functools.partial(flash_body, scale=scale, key_block=key_b...  31.4 us
    all_to_all x1, blocking collectives, shards(): received = lax.all_to_all(spread, ('expert', 'head'), 0, 0, tiled=True)  25.5 us
    all_to_all x1, blocking collectives, shards(): lax.all_to_all(summed_halves, ('expert', 'head'), 0, 0, tiled=True)  23.2 us
    unnamed x26, local copies, waits for them, and re-layouts  17.5 us
    ppermute x7, starting transfers between devices, shards(): lax.ppermute(w_out, 'head', [(index, (index + shift) % head_size) for ind...  9.23 us
    dot_general x1, matrix products, expert_half(): lax.dot_general(hidden, down_half, (((0,), (0,)), ((), ())), preferred_el...  7.62 us
  transfers between devices with their start and end apart: 12, of which 7 were waited for; matrix products, arithmetic and copies ran while one was open for 7% of the time, Pallas kernels for 10%

profile of v8, /device:TPU:1, one launch (start us, length us, event | category | flops | bytes accessed | tf_op | source)
XLA Modules:
  0.0 325.6 jit_solution(138718642958623907)
XLA Ops:
  6.5 2.2 reshape.111
  8.8 36.3 %all-gather.3.cloned.1.call-done = bf16[1024,2048]{1,0:T(8,128)(2,1)} async-done(((bf16[128,2048]{1,0:T(8,128)(2,1)}), bf16[1024,2048]{1,0:T(8,128)(2,1)}) %all-gather.3.cloned.1.call-update) | async-done | bytes 4194320 | tf_op jit(solution)/shard_map/all_gather | solution.py:138
  45.1 6.2 %fusion.19 = bf16[1024,512]{0,1:T(8,128)(2,1)} fusion(bf16[1024,2048]{1,0:T(8,128)(2,1)} %all-gather.3.cloned.1.call-done, bf16[2048,256]{1,0:T(8,128)(2,1)} %param.15, bf16[2048,256]{1,0:T(8,128)(2,1)} %param.14), kind=kOutput, calls=%fused_computation.21 | convolution fusion | flops 2152202240 | bytes 7340032 | tf_op jit(solution)/shard_map/dot_general | solution.py:147
  51.3 2.3 copy.17
  53.6 2.3 reshape.114
  56.2 1.0 collective-permute-start.1
  57.1 1.1 collective-permute-start.2
  58.3 1.7 collective-permute-start.3
  59.9 2.6 collective-permute-start.4
  62.6 2.4 constant_dynamic-update-slice_fusion.7
  65.9 12.8 %collective-permute-done = bf16[256,2048]{1,0:T(8,128)(2,1)} collective-permute-done((bf16[256,2048]{1,0:T(8,128)(2,1)}, bf16[256,2048]{1,0:T(8,128)(2,1)}, u32[]{:S(2)}, u32[]{:S(2)}) %collective-permute-start) | collective-permute-done | bytes 1048608 | tf_op jit(solution)/shard_map/ppermute | solution.py:162
  78.7 2.6 collective-permute-start.5
  81.2 2.3 constant_dynamic-update-slice_fusion.6
  83.6 65.8 %collective-permute-done.1 = bf16[256,2048]{1,0:T(8,128)(2,1)} collective-permute-done((bf16[256,2048]{1,0:T(8,128)(2,1)}, bf16[256,2048]{1,0:T(8,128)(2,1)}, u32[]{:S(2)}, u32[]{:S(2)}) %collective-permute-start.1) | collective-permute-done | bytes 1048608 | tf_op jit(solution)/shard_map/ppermute | solution.py:162
  149.4 2.3 constant_dynamic-update-slice_fusion.5
  151.7 2.5 constant_dynamic-update-slice_fusion.4
  154.2 2.3 constant_dynamic-update-slice_fusion.3
  156.5 2.3 constant_dynamic-update-slice_fusion.2
  158.9 1.2 convolution_convert_fusion.2
  160.1 1.0 reshape.113.q_ref
  161.2 5.4 %all-gather.5.cloned.1.call-done.k_ref.v_ref = bf16[8192,1024]{1,0:T(8,128)(2,1)} async-done(((bf16[512,1024]{1,0:T(8,128)(2,1)}), bf16[8192,1024]{1,0:T(8,128)(2,1)}) %all-gather.5.cloned.1.call-update) | async-done | bytes 16777232 | tf_op jit(solution)/shard_map/all_gather | solution.py:151
  166.6 31.4 %shard_map.118 = bf16[512,512]{1,0:T(8,128)(2,1)} custom-call(s32[3]{0:T(128)} %pad_add_fusion.scalars, bf16[512,512]{1,0:T(8,128)(2,1)} %reshape.113.q_ref, bf16[8192,1024]{1,0:T(8,128)(2,1)} %all-gather.5.cloned.1.call-done.k_ref.v_ref, bf16[8192,1024]{1,0:T(8,128)(2,1)} %all-gather.5.cloned.1.call-done.k_ref.v_ref), custom_call_target="tpu_custom_call" | custom-call | flops 8589934592 | bytes 17825792 | tf_op jit(solution)/shard_map/pallas_call | solution.py:91
  198.0 1.2 reshape.115
  200.1 5.1 %all-to-all-start = ((bf16[8,64,2,256]{3,1,2,0:T(8,128)(2,1)}), bf16[8,64,2,256]{3,1,2,0:T(8,128)(2,1)}, u32[]{:S(2)}, u32[]{:S(2)}) async-start(bf16[8,64,2,256]{3,1,2,0:T(8,128)(2,1)} %copy.18), calls=%async_computation | async-start | bytes 1048576 | tf_op jit(solution)/shard_map/all_to_all | solution.py:167
  205.2 2.3 constant_dynamic-update-slice_fusion.1
  207.5 2.4 constant_dynamic-update-slice_fusion
  210.0 4.8 %all-to-all-done = bf16[8,64,2,256]{3,1,2,0:T(8,128)(2,1)} async-done(((bf16[8,64,2,256]{3,1,2,0:T(8,128)(2,1)}), bf16[8,64,2,256]{3,1,2,0:T(8,128)(2,1)}, u32[]{:S(2)}, u32[]{:S(2)}) %all-to-all-start) | async-done | bytes 524320 | tf_op jit(solution)/shard_map/all_to_all | solution.py:167
  214.8 2.4 gather_fusion
  217.2 1.2 select_bitcast_fusion
  218.8 4.8 %multiply_reduce_fusion = (f32[128]{0:T(128)S(1)}, f32[128,2048]{1,0:T(8,128)S(1)}) fusion(bf16[128,2048]{1,0:T(8,128)(2,1)S(1)} %bitcast.43, bf16[2048,2048]{1,0:T(8,128)(2,1)} %constant_dynamic-update-slice_fusion, bf16[128,2048]{1,0:T(8,128)(2,1)S(1)} %copy-done.2), kind=kOutput, calls=%fused_computation.24 | convolution fusion | flops 1074790272 | bytes 10486272 | tf_op jit(solution)/shard_map/dot_general | solution.py:172
  223.6 1.0 copy-done.1
  224.6 1.5 convolution_convert_fusion.1
  226.1 2.5 reshape.117
  228.6 25.5 %all_to_all.15 = bf16[128,2,2048]{2,1,0:T(2,128)(2,1)S(1)} all-to-all(bf16[128,2,2048]{2,1,0:T(2,128)(2,1)} %reshape.117), channel_id=1, replica_groups=mesh['expert'=16,'head'=8] {'expert','head'}, dimensions={0} | all-to-all | bytes 2097152 | tf_op jit(solution)/shard_map/all_to_all | solution.py:198
  254.1 1.2 collective-permute-start.7
  255.3 2.3 collective-permute-done.7
  257.6 3.2 pad_maximum_fusion
  260.7 4.0 %reshape.118 = bf16[512,2048]{1,0:T(8,128)(2,1)} reshape(bf16[128,4,2048]{2,1,0:T(4,128)(2,1)} %pad_maximum_fusion) | data formatting | bytes 4194304 | tf_op jit(solution)/shard_map/reshape | solution.py:205
  264.7 5.3 %fusion.13 = f32[704,512]{1,0:T(8,128)} fusion(bf16[512,2048]{1,0:T(8,128)(2,1)} %reshape.118, bf16[1,704,2048]{2,1,0:T(8,128)(2,1)} %param.18), kind=kOutput, calls=%fused_computation.18 | convolution fusion | flops 1476395008 | bytes 6422528 | tf_op jit(solution)/shard_map/dot_general | solution.py:108
  270.0 7.6 %convolution_convert_fusion = bf16[512,2048]{1,0:T(8,128)(2,1)} fusion(bf16[1,704,2048]{2,1,0:T(8,128)(2,1)S(1)} %copy-done, f32[704,512]{1,0:T(8,128)} %fusion.13, bf16[512,2048]{1,0:T(8,128)(2,1)} %reshape.118, bf16[1,704,2048]{2,1,0:T(8,128)(2,1)} %param.19), kind=kOutput, calls=%fused_computation.1 | convolution fusion | flops 2956001280 | bytes 11403264 | tf_op jit(solution)/shard_map/dot_general | solution.py:113
  277.6 4.1 %reshape.119 = bf16[128,4,2048]{2,1,0:T(4,128)(2,1)} reshape(bf16[512,2048]{1,0:T(8,128)(2,1)} %convolution_convert_fusion) | data formatting | bytes 4194304 | tf_op jit(solution)/shard_map/reshape | solution.py:206
  281.7 2.8 slice.11
  285.2 2.3 collective-permute-done.8
  287.5 2.7 add_convert_fusion
  290.2 23.2 %all_to_all.16 = bf16[128,2,2048]{2,1,0:T(2,128)(2,1)} all-to-all(bf16[128,2,2048]{2,1,0:T(2,128)(2,1)S(1)} %add_convert_fusion), channel_id=1, replica_groups=mesh['expert'=16,'head'=8] {'expert','head'}, dimensions={0} | all-to-all | bytes 2097152 | tf_op jit(solution)/shard_map/all_to_all | solution.py:210
  313.5 2.3 reshape.120
  315.7 1.9 fusion.5
  317.6 1.1 reshape.121
  (41 shorter events, 3.3 us)
Async XLA Ops:
  6.5 263.4 %copy-start = (bf16[1,704,2048]{2,1,0:T(8,128)(2,1)S(1)}, bf16[1,704,2048]{2,1,0:T(8,128)(2,1)}, u32[]{:S(2)}) copy-start(bf16[1,704,2048]{2,1,0:T(8,128)(2,1)} %param.20) | copy-start | bytes 8650756
  6.5 38.5 %all-gather.3.cloned.1.call-start = ((), (), s32[]{:S(2)}) async-start(), calls=%async_computation.3 | async-start | bytes 4718592 | tf_op jit(solution)/shard_map/all_gather | solution.py:138
  8.7 157.9 %all-gather.5.cloned.1.call-start = ((), (), s32[]{:S(2)}) async-start(), calls=%async_computation.4 | async-start | bytes 17825792 | tf_op jit(solution)/shard_map/all_gather | solution.py:151
  53.6 11.4 %copy-start.4 = (s32[64,2]{0,1:T(2,128)S(1)}, s32[64,2]{0,1:T(2,128)}, u32[]{:S(2)}) copy-start(s32[64,2]{0,1:T(2,128)} %param.23) | copy-start | bytes 1540
  53.6 11.4 %copy-start.5 = (s32[64,2]{0,1:T(2,128)S(1)}, s32[64,2]{0,1:T(2,128)}, u32[]{:S(2)}) copy-start(s32[64,2]{0,1:T(2,128)} %param.22) | copy-start | bytes 1540
  53.6 11.4 %copy-start.8 = (s32[2]{0:T(128)S(1)}, s32[2]{0:T(128)}, u32[]{:S(2)}) copy-start(s32[2]{0:T(128)} %param.21) | copy-start | bytes 28
  53.6 12.1 %copy-start.3 = (bf16[2048]{0:T(1024)(128)(2,1)S(1)}, bf16[2048]{0:T(1024)(128)(2,1)}, u32[]{:S(2)}) copy-start(bf16[2048]{0:T(1024)(128)(2,1)} %param.17) | copy-start | bytes 12292
  55.9 22.8 %collective-permute-start = (bf16[256,2048]{1,0:T(8,128)(2,1)}, bf16[256,2048]{1,0:T(8,128)(2,1)}, u32[]{:S(2)}, u32[]{:S(2)}) collective-permute-start(bf16[256,2048]{1,0:T(8,128)(2,1)} %param.16), channel_id=1, source_target_pairs={{0,1},{1,2},{2,3},{3,4},{4,5},{5,6},{6,7},{7,0},{8,9},{9,10},{10,1... | collective-permute-start | bytes 3145736 | tf_op jit(solution)/shard_map/ppermute | solution.py:162
  56.2 93.2 %collective-permute-start.1 = (bf16[256,2048]{1,0:T(8,128)(2,1)}, bf16[256,2048]{1,0:T(8,128)(2,1)}, u32[]{:S(2)}, u32[]{:S(2)}) collective-permute-start(bf16[256,2048]{1,0:T(8,128)(2,1)} %param.16), channel_id=1, source_target_pairs={{0,2},{1,3},{2,4},{3,5},{4,6},{5,7},{6,0},{7,1},{8,10},{9,11},{10,... | collective-permute-start | bytes 3145736 | tf_op jit(solution)/shard_map/ppermute | solution.py:162
  57.1 94.6 %collective-permute-start.2 = (bf16[256,2048]{1,0:T(8,128)(2,1)}, bf16[256,2048]{1,0:T(8,128)(2,1)}, u32[]{:S(2)}, u32[]{:S(2)}) collective-permute-start(bf16[256,2048]{1,0:T(8,128)(2,1)} %param.16), channel_id=1, source_target_pairs={{0,3},{1,4},{2,5},{3,6},{4,7},{5,0},{6,1},{7,2},{8,11},{9,12},{10,... | collective-permute-start | bytes 3145736 | tf_op jit(solution)/shard_map/ppermute | solution.py:162
  58.3 95.9 %collective-permute-start.3 = (bf16[256,2048]{1,0:T(8,128)(2,1)}, bf16[256,2048]{1,0:T(8,128)(2,1)}, u32[]{:S(2)}, u32[]{:S(2)}) collective-permute-start(bf16[256,2048]{1,0:T(8,128)(2,1)} %param.16), channel_id=1, source_target_pairs={{0,4},{1,5},{2,6},{3,7},{4,0},{5,1},{6,2},{7,3},{8,12},{9,13},{10,... | collective-permute-start | bytes 3145736 | tf_op jit(solution)/shard_map/ppermute | solution.py:162
  59.9 96.6 %collective-permute-start.4 = (bf16[256,2048]{1,0:T(8,128)(2,1)}, bf16[256,2048]{1,0:T(8,128)(2,1)}, u32[]{:S(2)}, u32[]{:S(2)}) collective-permute-start(bf16[256,2048]{1,0:T(8,128)(2,1)} %param.16), channel_id=1, source_target_pairs={{0,5},{1,6},{2,7},{3,0},{4,1},{5,2},{6,3},{7,4},{8,13},{9,14},{10,... | collective-permute-start | bytes 3145736 | tf_op jit(solution)/shard_map/ppermute | solution.py:162
  78.7 126.5 %collective-permute-start.5 = (bf16[256,2048]{1,0:T(8,128)(2,1)}, bf16[256,2048]{1,0:T(8,128)(2,1)}, u32[]{:S(2)}, u32[]{:S(2)}) collective-permute-start(bf16[256,2048]{1,0:T(8,128)(2,1)} %param.16), channel_id=1, source_target_pairs={{0,6},{1,7},{2,0},{3,1},{4,2},{5,3},{6,4},{7,5},{8,14},{9,15},{10,... | collective-permute-start | bytes 3145736 | tf_op jit(solution)/shard_map/ppermute | solution.py:162
  149.4 58.1 %collective-permute-start.6 = (bf16[256,2048]{1,0:T(8,128)(2,1)}, bf16[256,2048]{1,0:T(8,128)(2,1)}, u32[]{:S(2)}, u32[]{:S(2)}) collective-permute-start(bf16[256,2048]{1,0:T(8,128)(2,1)} %param.16), channel_id=1, source_target_pairs={{0,7},{1,0},{2,1},{3,2},{4,3},{5,4},{6,5},{7,6},{8,15},{9,8},{10,9... | collective-permute-start | bytes 3145736 | tf_op jit(solution)/shard_map/ppermute | solution.py:162
  151.7 7.1 %copy-start.6 = (bf16[1024,2048]{1,0:T(8,128)(2,1)S(1)}, bf16[1024,2048]{1,0:T(8,128)(2,1)}, u32[]{:S(2)}) copy-start(bf16[1024,2048]{1,0:T(8,128)(2,1)} %all-gather.3.cloned.1.call-done) | copy-start | bytes 12582916
  151.7 7.1 %copy-start.7 = (bf16[2048,256]{1,0:T(8,128)(2,1)S(1)}, bf16[2048,256]{1,0:T(8,128)(2,1)}, u32[]{:S(2)}) copy-start(bf16[2048,256]{1,0:T(8,128)(2,1)} %param.13) | copy-start | bytes 3145732
  200.1 14.7 %all-to-all-start = ((bf16[8,64,2,256]{3,1,2,0:T(8,128)(2,1)}), bf16[8,64,2,256]{3,1,2,0:T(8,128)(2,1)}, u32[]{:S(2)}, u32[]{:S(2)}) async-start(bf16[8,64,2,256]{3,1,2,0:T(8,128)(2,1)} %copy.18), calls=%async_computation | async-start | bytes 1048576 | tf_op jit(solution)/shard_map/all_to_all | solution.py:167
  207.5 11.3 %copy-start.2 = (bf16[128,2048]{1,0:T(8,128)(2,1)S(1)}, bf16[128,2048]{1,0:T(8,128)(2,1)}, u32[]{:S(2)}) copy-start(bf16[128,2048]{1,0:T(8,128)(2,1)} %reshape.111) | copy-start | bytes 1572868
  223.6 1.0 copy-start.1
  254.1 3.5 %collective-permute-start.7 = (bf16[128,2,2048]{2,1,0:T(2,128)(2,1)S(1)}, bf16[128,2,2048]{2,1,0:T(2,128)(2,1)S(1)}, u32[]{:S(2)}, u32[]{:S(2)}) collective-permute-start(bf16[128,2,2048]{2,1,0:T(2,128)(2,1)S(1)} %all_to_all.15), channel_id=1, source_target_pairs={{0,1},{1,0},{2,3},{3,2},{4,5},{5,4},{6,7},{7,6},{8,9},{9,8},{10,11... | collective-permute-start | bytes 3145736 | tf_op jit(solution)/shard_map/ppermute | solution.py:200
  284.5 3.0 collective-permute-start.8
Sparse Core Ops, SparseCore 0:
  9.1 35.9 all-gather.2
  56.0 110.5 all-gather.4

commit v9 on v8

--- a/solution.py
+++ b/solution.py
@@ -194,22 +194,15 @@
     up_half = w_up[0]
     down_half = w_down[0]
     pieces = 2
-    spread = send_rows.reshape(expert_count * pieces, slot_cap // pieces, model_width)
-    received = lax.all_to_all(spread, ("expert", "head"), 0, 0, tiled=True)
+    received = lax.all_to_all(send_rows, ("expert", "head"), 0, 0, tiled=True)
     swap = [(index, index ^ 1) for index in range(lax.axis_size("head"))]
     from_partner = lax.ppermute(received, "head", swap)
-    both = jnp.concatenate([received, from_partner], axis=1)
-    sources = both.shape[0]
-    item_count = both.shape[1]
-    half_out = expert_half(
-        both.reshape(sources * item_count, model_width), gate_half, up_half, down_half
-    ).reshape(sources, item_count, model_width)
-    mine = half_out[:, : slot_cap // pieces]
-    theirs = lax.ppermute(half_out[:, slot_cap // pieces :], "head", swap)
+    both = jnp.concatenate([received, from_partner], axis=0)
+    half_out = expert_half(both, gate_half, up_half, down_half)
+    mine = half_out[: received.shape[0]]
+    theirs = lax.ppermute(half_out[received.shape[0] :], "head", swap)
     summed_halves = (mine.astype(jnp.float32) + theirs.astype(jnp.float32)).astype(jnp.bfloat16)
-    combined = lax.all_to_all(summed_halves, ("expert", "head"), 0, 0, tiled=True).reshape(
-        expert_count * slot_cap, model_width
-    )
+    combined = lax.all_to_all(summed_halves, ("expert", "head"), 0, 0, tiled=True)
     expert_out = lax.dot_general(
         slot_table, combined, (((0,), (0,)), ((), ())), preferred_element_type=jnp.float32
     )

time: 327 us -> 324 us (level)
  Pallas kernels: 31.4 us -> 36.7 us
  other arithmetic: 7.73 us -> 4.39 us
    reshape x4 -> x0, local copies, waits for them, and re-layouts: 12.9 us -> none  [the longest x1 4.12 us: shards(): half_out = expert_half(both.reshape(sources * item_count, model_width), g...]
    all_to_all x0 -> x4, local copies, waits for them, and re-layouts: none -> 9.59 us  [the longest x2 4.79 us: shards(): received = lax.all_to_all(send_rows, ('expert', 'head'), 0, 0, tiled=True)]
    pallas_call x1, Pallas kernels: 31.4 us -> 36.7 us  [flash_attention(): pl.pallas_call(functools.partial(flash_body, scale=scale, key_block=key_b...]
    unnamed x26 -> x31, local copies, waits for them, and re-layouts: 17.5 us -> 20.1 us
  transfers between devices with their start and end apart: 12 -> 12, of which waited for: 7 -> 7; matrix products, arithmetic and copies ran while one was open for 7% -> 8% of each run, Pallas kernels for 10% -> 11%
where the time goes in v9:
time: 324 us; the launch traced here: 323 us
  waiting for transfers between devices  129 us (40%)
  blocking collectives  49.7 us (15%)
  local copies, waits for them, and re-layouts  47.5 us (15%)
  Pallas kernels  36.7 us (11%)
  matrix products  26.1 us (8%)
  starting transfers between devices  16 us (5%)
  between operations  13.5 us (4%)
  other arithmetic  4.39 us (1%)
    ppermute x7, waiting for transfers between devices, shards(): lax.ppermute(w_out, 'head', [(index, (index + shift) % head_size) for ind...  78.7 us
    pallas_call x1, Pallas kernels, flash_attention(): pl.pallas_call(functools.partial(flash_body, scale=scale, key_block=key_b...  36.7 us
    all_gather x1, waiting for transfers between devices, shards(): flat_rows = lax.all_gather(cells_flat, 'head', axis=0, tiled=True)  36.3 us
    all_to_all x1, blocking collectives, shards(): received = lax.all_to_all(send_rows, ('expert', 'head'), 0, 0, tiled=True)  25.6 us
    all_to_all x1, blocking collectives, shards(): lax.all_to_all(summed_halves, ('expert', 'head'), 0, 0, tiled=True)  24.1 us
    unnamed x31, local copies, waits for them, and re-layouts  20.1 us
    ppermute x7, starting transfers between devices, shards(): lax.ppermute(w_out, 'head', [(index, (index + shift) % head_size) for ind...  9.23 us
    dot_general x1, matrix products, expert_half(): lax.dot_general(hidden, down_half, (((0,), (0,)), ((), ())), preferred_el...  7.64 us
  transfers between devices with their start and end apart: 12, of which 7 were waited for; matrix products, arithmetic and copies ran while one was open for 8% of the time, Pallas kernels for 11%

profile of v9, /device:TPU:1, one launch (start us, length us, event | category | flops | bytes accessed | tf_op | source)
XLA Modules:
  0.0 322.7 jit_solution(15074331449459479522)
XLA Ops:
  6.5 2.2 reshape.103
  8.8 36.3 %all-gather.3.cloned.1.call-done = bf16[1024,2048]{1,0:T(8,128)(2,1)} async-done(((bf16[128,2048]{1,0:T(8,128)(2,1)}), bf16[1024,2048]{1,0:T(8,128)(2,1)}) %all-gather.3.cloned.1.call-update) | async-done | bytes 4194320 | tf_op jit(solution)/shard_map/all_gather | solution.py:138
  45.1 6.2 %fusion.19 = bf16[1024,512]{0,1:T(8,128)(2,1)} fusion(bf16[1024,2048]{1,0:T(8,128)(2,1)} %all-gather.3.cloned.1.call-done, bf16[2048,256]{1,0:T(8,128)(2,1)} %param.15, bf16[2048,256]{1,0:T(8,128)(2,1)} %param.14), kind=kOutput, calls=%fused_computation.20 | convolution fusion | flops 2152202240 | bytes 7340032 | tf_op jit(solution)/shard_map/dot_general | solution.py:147
  51.3 2.3 copy.17
  53.6 2.3 reshape.106
  56.1 1.0 collective-permute-start.1
  57.1 1.1 collective-permute-start.2
  58.2 1.7 collective-permute-start.3
  59.9 2.6 collective-permute-start.4
  62.6 2.4 constant_dynamic-update-slice_fusion.7
  65.8 12.8 %collective-permute-done = bf16[256,2048]{1,0:T(8,128)(2,1)} collective-permute-done((bf16[256,2048]{1,0:T(8,128)(2,1)}, bf16[256,2048]{1,0:T(8,128)(2,1)}, u32[]{:S(2)}, u32[]{:S(2)}) %collective-permute-start) | collective-permute-done | bytes 1048608 | tf_op jit(solution)/shard_map/ppermute | solution.py:162
  78.6 2.6 collective-permute-start.5
  81.2 2.3 constant_dynamic-update-slice_fusion.6
  83.5 65.8 %collective-permute-done.1 = bf16[256,2048]{1,0:T(8,128)(2,1)} collective-permute-done((bf16[256,2048]{1,0:T(8,128)(2,1)}, bf16[256,2048]{1,0:T(8,128)(2,1)}, u32[]{:S(2)}, u32[]{:S(2)}) %collective-permute-start.1) | collective-permute-done | bytes 1048608 | tf_op jit(solution)/shard_map/ppermute | solution.py:162
  149.4 2.3 constant_dynamic-update-slice_fusion.5
  151.7 2.5 constant_dynamic-update-slice_fusion.4
  154.1 2.3 constant_dynamic-update-slice_fusion.3
  156.5 2.3 constant_dynamic-update-slice_fusion.2
  158.8 1.3 convolution_convert_fusion.2
  160.1 1.0 reshape.105.q_ref
  161.1 5.5 %all-gather.5.cloned.1.call-done.k_ref.v_ref = bf16[8192,1024]{1,0:T(8,128)(2,1)} async-done(((bf16[512,1024]{1,0:T(8,128)(2,1)}), bf16[8192,1024]{1,0:T(8,128)(2,1)}) %all-gather.5.cloned.1.call-update) | async-done | bytes 16777232 | tf_op jit(solution)/shard_map/all_gather | solution.py:151
  166.6 36.7 %shard_map.118 = bf16[512,512]{1,0:T(8,128)(2,1)} custom-call(s32[3]{0:T(128)} %pad_add_fusion.scalars, bf16[512,512]{1,0:T(8,128)(2,1)} %reshape.105.q_ref, bf16[8192,1024]{1,0:T(8,128)(2,1)} %all-gather.5.cloned.1.call-done.k_ref.v_ref, bf16[8192,1024]{1,0:T(8,128)(2,1)} %all-gather.5.cloned.1.call-done.k_ref.v_ref), custom_call_target="tpu_custom_call" | custom-call | flops 8589934592 | bytes 17825792 | tf_op jit(solution)/shard_map/pallas_call | solution.py:91
  203.3 1.2 reshape.107
  205.3 5.1 %all-to-all-start = ((bf16[8,64,2,256]{3,1,2,0:T(8,128)(2,1)}), bf16[8,64,2,256]{3,1,2,0:T(8,128)(2,1)}, u32[]{:S(2)}, u32[]{:S(2)}) async-start(bf16[8,64,2,256]{3,1,2,0:T(8,128)(2,1)} %copy.18), calls=%async_computation | async-start | bytes 1048576 | tf_op jit(solution)/shard_map/all_to_all | solution.py:167
  210.4 2.3 constant_dynamic-update-slice_fusion.1
  212.7 2.5 constant_dynamic-update-slice_fusion
  215.2 4.8 %all-to-all-done = bf16[8,64,2,256]{3,1,2,0:T(8,128)(2,1)} async-done(((bf16[8,64,2,256]{3,1,2,0:T(8,128)(2,1)}), bf16[8,64,2,256]{3,1,2,0:T(8,128)(2,1)}, u32[]{:S(2)}, u32[]{:S(2)}) %all-to-all-start) | async-done | bytes 524320 | tf_op jit(solution)/shard_map/all_to_all | solution.py:167
  220.0 2.4 gather_fusion
  222.4 1.2 select_bitcast_fusion
  224.0 4.8 %multiply_reduce_fusion = (f32[128]{0:T(128)S(1)}, f32[128,2048]{1,0:T(8,128)S(1)}) fusion(bf16[128,2048]{1,0:T(8,128)(2,1)S(1)} %bitcast.43, bf16[2048,2048]{1,0:T(8,128)(2,1)} %constant_dynamic-update-slice_fusion, bf16[128,2048]{1,0:T(8,128)(2,1)S(1)} %copy-done.2), kind=kOutput, calls=%fused_computation.23 | convolution fusion | flops 1074790272 | bytes 10486272 | tf_op jit(solution)/shard_map/dot_general | solution.py:172
  229.8 1.5 convolution_convert_fusion.1
  231.3 2.5 all_to_all.20
  233.9 25.6 %all_to_all.29 = bf16[128,2,2048]{2,1,0:T(2,128)(2,1)} all-to-all(bf16[128,2,2048]{2,1,0:T(2,128)(2,1)} %all_to_all.20), channel_id=1, replica_groups=mesh['expert'=16,'head'=8] {'expert','head'}, dimensions={0} | all-to-all | bytes 2097152 | tf_op jit(solution)/shard_map/all_to_all | solution.py:197
  259.5 2.3 all_to_all.22
  261.7 1.2 collective-permute-start.7
  262.9 1.3 constant_dynamic-update-slice_fusion.9
  264.2 1.2 collective-permute-done.7
  265.5 1.3 copy-done.3
  266.8 2.8 fusion.13
  269.6 7.6 %convolution_convert_fusion = bf16[512,2048]{1,0:T(8,128)(2,1)} fusion(bf16[1,704,2048]{2,1,0:T(8,128)(2,1)S(1)} %copy-done, f32[704,512]{1,0:T(8,128)} %fusion.13, bf16[512,2048]{1,0:T(8,128)(2,1)} %copy-done.3, bf16[1,704,2048]{2,1,0:T(8,128)(2,1)} %param.19), kind=kOutput, calls=%fused_computation.1 | convolution fusion | flops 2956001280 | bytes 11403264 | tf_op jit(solution)/shard_map/dot_general | solution.py:113
  277.3 1.3 slice.11
  279.0 2.3 collective-permute-done.8
  281.3 2.6 add_convert_fusion
  283.9 2.5 all_to_all.23
  286.5 24.1 %all_to_all.30 = bf16[128,2,2048]{2,1,0:T(2,128)(2,1)} all-to-all(bf16[128,2,2048]{2,1,0:T(2,128)(2,1)} %all_to_all.23), channel_id=1, replica_groups=mesh['expert'=16,'head'=8] {'expert','head'}, dimensions={0} | all-to-all | bytes 2097152 | tf_op jit(solution)/shard_map/all_to_all | solution.py:205
  310.6 2.3 all_to_all.25
  312.9 1.9 fusion.5
  314.8 1.1 reshape.109
  (46 shorter events, 4.1 us)
Async XLA Ops:
  6.5 263.1 %copy-start = (bf16[1,704,2048]{2,1,0:T(8,128)(2,1)S(1)}, bf16[1,704,2048]{2,1,0:T(8,128)(2,1)}, u32[]{:S(2)}) copy-start(bf16[1,704,2048]{2,1,0:T(8,128)(2,1)} %param.20) | copy-start | bytes 8650756
  6.5 38.5 %all-gather.3.cloned.1.call-start = ((), (), s32[]{:S(2)}) async-start(), calls=%async_computation.3 | async-start | bytes 4718592 | tf_op jit(solution)/shard_map/all_gather | solution.py:138
  8.7 157.8 %all-gather.5.cloned.1.call-start = ((), (), s32[]{:S(2)}) async-start(), calls=%async_computation.4 | async-start | bytes 17825792 | tf_op jit(solution)/shard_map/all_gather | solution.py:151
  53.5 11.4 %copy-start.5 = (s32[64,2]{0,1:T(2,128)S(1)}, s32[64,2]{0,1:T(2,128)}, u32[]{:S(2)}) copy-start(s32[64,2]{0,1:T(2,128)} %param.23) | copy-start | bytes 1540
  53.5 11.4 %copy-start.6 = (s32[64,2]{0,1:T(2,128)S(1)}, s32[64,2]{0,1:T(2,128)}, u32[]{:S(2)}) copy-start(s32[64,2]{0,1:T(2,128)} %param.22) | copy-start | bytes 1540
  53.5 11.4 %copy-start.10 = (s32[2]{0:T(128)S(1)}, s32[2]{0:T(128)}, u32[]{:S(2)}) copy-start(s32[2]{0:T(128)} %param.21) | copy-start | bytes 28
  53.5 12.0 %copy-start.4 = (bf16[2048]{0:T(1024)(128)(2,1)S(1)}, bf16[2048]{0:T(1024)(128)(2,1)}, u32[]{:S(2)}) copy-start(bf16[2048]{0:T(1024)(128)(2,1)} %param.17) | copy-start | bytes 12292
  55.9 22.8 %collective-permute-start = (bf16[256,2048]{1,0:T(8,128)(2,1)}, bf16[256,2048]{1,0:T(8,128)(2,1)}, u32[]{:S(2)}, u32[]{:S(2)}) collective-permute-start(bf16[256,2048]{1,0:T(8,128)(2,1)} %param.16), channel_id=1, source_target_pairs={{0,1},{1,2},{2,3},{3,4},{4,5},{5,6},{6,7},{7,0},{8,9},{9,10},{10,1... | collective-permute-start | bytes 3145736 | tf_op jit(solution)/shard_map/ppermute | solution.py:162
  56.1 93.2 %collective-permute-start.1 = (bf16[256,2048]{1,0:T(8,128)(2,1)}, bf16[256,2048]{1,0:T(8,128)(2,1)}, u32[]{:S(2)}, u32[]{:S(2)}) collective-permute-start(bf16[256,2048]{1,0:T(8,128)(2,1)} %param.16), channel_id=1, source_target_pairs={{0,2},{1,3},{2,4},{3,5},{4,6},{5,7},{6,0},{7,1},{8,10},{9,11},{10,... | collective-permute-start | bytes 3145736 | tf_op jit(solution)/shard_map/ppermute | solution.py:162
  57.1 94.6 %collective-permute-start.2 = (bf16[256,2048]{1,0:T(8,128)(2,1)}, bf16[256,2048]{1,0:T(8,128)(2,1)}, u32[]{:S(2)}, u32[]{:S(2)}) collective-permute-start(bf16[256,2048]{1,0:T(8,128)(2,1)} %param.16), channel_id=1, source_target_pairs={{0,3},{1,4},{2,5},{3,6},{4,7},{5,0},{6,1},{7,2},{8,11},{9,12},{10,... | collective-permute-start | bytes 3145736 | tf_op jit(solution)/shard_map/ppermute | solution.py:162
  58.2 95.9 %collective-permute-start.3 = (bf16[256,2048]{1,0:T(8,128)(2,1)}, bf16[256,2048]{1,0:T(8,128)(2,1)}, u32[]{:S(2)}, u32[]{:S(2)}) collective-permute-start(bf16[256,2048]{1,0:T(8,128)(2,1)} %param.16), channel_id=1, source_target_pairs={{0,4},{1,5},{2,6},{3,7},{4,0},{5,1},{6,2},{7,3},{8,12},{9,13},{10,... | collective-permute-start | bytes 3145736 | tf_op jit(solution)/shard_map/ppermute | solution.py:162
  59.9 96.6 %collective-permute-start.4 = (bf16[256,2048]{1,0:T(8,128)(2,1)}, bf16[256,2048]{1,0:T(8,128)(2,1)}, u32[]{:S(2)}, u32[]{:S(2)}) collective-permute-start(bf16[256,2048]{1,0:T(8,128)(2,1)} %param.16), channel_id=1, source_target_pairs={{0,5},{1,6},{2,7},{3,0},{4,1},{5,2},{6,3},{7,4},{8,13},{9,14},{10,... | collective-permute-start | bytes 3145736 | tf_op jit(solution)/shard_map/ppermute | solution.py:162
  78.6 131.8 %collective-permute-start.5 = (bf16[256,2048]{1,0:T(8,128)(2,1)}, bf16[256,2048]{1,0:T(8,128)(2,1)}, u32[]{:S(2)}, u32[]{:S(2)}) collective-permute-start(bf16[256,2048]{1,0:T(8,128)(2,1)} %param.16), channel_id=1, source_target_pairs={{0,6},{1,7},{2,0},{3,1},{4,2},{5,3},{6,4},{7,5},{8,14},{9,15},{10,... | collective-permute-start | bytes 3145736 | tf_op jit(solution)/shard_map/ppermute | solution.py:162
  149.4 63.4 %collective-permute-start.6 = (bf16[256,2048]{1,0:T(8,128)(2,1)}, bf16[256,2048]{1,0:T(8,128)(2,1)}, u32[]{:S(2)}, u32[]{:S(2)}) collective-permute-start(bf16[256,2048]{1,0:T(8,128)(2,1)} %param.16), channel_id=1, source_target_pairs={{0,7},{1,0},{2,1},{3,2},{4,3},{5,4},{6,5},{7,6},{8,15},{9,8},{10,9... | collective-permute-start | bytes 3145736 | tf_op jit(solution)/shard_map/ppermute | solution.py:162
  151.7 7.1 %copy-start.7 = (bf16[1024,2048]{1,0:T(8,128)(2,1)S(1)}, bf16[1024,2048]{1,0:T(8,128)(2,1)}, u32[]{:S(2)}) copy-start(bf16[1024,2048]{1,0:T(8,128)(2,1)} %all-gather.3.cloned.1.call-done) | copy-start | bytes 12582916
  151.7 7.1 %copy-start.9 = (bf16[2048,256]{1,0:T(8,128)(2,1)S(1)}, bf16[2048,256]{1,0:T(8,128)(2,1)}, u32[]{:S(2)}) copy-start(bf16[2048,256]{1,0:T(8,128)(2,1)} %param.13) | copy-start | bytes 3145732
  205.3 14.7 %all-to-all-start = ((bf16[8,64,2,256]{3,1,2,0:T(8,128)(2,1)}), bf16[8,64,2,256]{3,1,2,0:T(8,128)(2,1)}, u32[]{:S(2)}, u32[]{:S(2)}) async-start(bf16[8,64,2,256]{3,1,2,0:T(8,128)(2,1)} %copy.18), calls=%async_computation | async-start | bytes 1048576 | tf_op jit(solution)/shard_map/all_to_all | solution.py:167
  212.7 11.3 %copy-start.2 = (bf16[128,2048]{1,0:T(8,128)(2,1)S(1)}, bf16[128,2048]{1,0:T(8,128)(2,1)}, u32[]{:S(2)}) copy-start(bf16[128,2048]{1,0:T(8,128)(2,1)} %reshape.103) | copy-start | bytes 1572868
  228.9 1.0 copy-start.1
  261.7 5.1 %copy-start.8 = (bf16[1,704,2048]{2,1,0:T(8,128)(2,1)S(1)}, bf16[1,704,2048]{2,1,0:T(8,128)(2,1)}, u32[]{:S(2)}) copy-start(bf16[1,704,2048]{2,1,0:T(8,128)(2,1)} %param.18) | copy-start | bytes 8650756
  261.7 3.7 %collective-permute-start.7 = (bf16[256,2048]{1,0:T(8,128)(2,1)}, bf16[256,2048]{1,0:T(8,128)(2,1)S(1)}, u32[]{:S(2)}, u32[]{:S(2)}) collective-permute-start(bf16[256,2048]{1,0:T(8,128)(2,1)} %all_to_all.22), channel_id=1, source_target_pairs={{0,1},{1,0},{2,3},{3,2},{4,5},{5,4},{6,7},{7,6},{8,9},{9,8},{10,11... | collective-permute-start | bytes 3145736 | tf_op jit(solution)/shard_map/ppermute | solution.py:199
  265.5 1.3 copy-start.3
  278.6 2.7 collective-permute-start.8
Sparse Core Ops, SparseCore 0:
  9.1 35.9 all-gather.2
  56.0 110.5 all-gather.4

commit v10 on v9

--- a/solution.py
+++ b/solution.py
@@ -101,6 +101,84 @@
             bytes_accessed=2 * (q_all.size * 2 + kv_all.size),
         ),
     )(scalars, q_all, kv_all, kv_all)
+
+
+MESH_ID = pl.DeviceIdType.MESH
+
+
+def head_gather_body(x_ref, out_ref, send_sem, recv_sem, local_sem, *, size):
+    chips = size // 2
+    me = lax.axis_index("head")
+    core = me % 2
+    z = me // 2
+    partner = me + 1 - 2 * core
+
+    def peer_of(k):
+        return ((z + k) % chips) * 2 + core
+
+    def source_of(k):
+        return ((z + chips - k) % chips) * 2 + core
+
+    barrier = pltpu.get_barrier_semaphore()
+    for k in range(1, chips):
+        pl.semaphore_signal(barrier, 1, device_id={"head": peer_of(k)}, device_id_type=MESH_ID)
+    pl.semaphore_signal(barrier, 1, device_id={"head": partner}, device_id_type=MESH_ID)
+    pl.semaphore_wait(barrier, chips)
+
+    local = pltpu.make_async_copy(x_ref, out_ref.at[me], local_sem)
+    local.start()
+    sent = []
+    for k in range(1, chips):
+        copy = pltpu.make_async_remote_copy(
+            x_ref, out_ref.at[me], send_sem.at[k - 1], recv_sem.at[me],
+            device_id={"head": peer_of(k)}, device_id_type=MESH_ID,
+        )
+        copy.start()
+        sent.append(copy)
+    own = pltpu.make_async_remote_copy(
+        x_ref, out_ref.at[me], send_sem.at[chips - 1], recv_sem.at[me],
+        device_id={"head": partner}, device_id_type=MESH_ID,
+    )
+    own.start()
+    sent.append(own)
+    for k in range(1, chips):
+        source = source_of(k)
+        arriving = pltpu.make_async_remote_copy(
+            x_ref, out_ref.at[source], send_sem.at[k - 1], recv_sem.at[source],
+            device_id={"head": source}, device_id_type=MESH_ID,
+        )
+        arriving.wait_recv()
+        forward = pltpu.make_async_remote_copy(
+            out_ref.at[source], out_ref.at[source], send_sem.at[chips - 1 + k],
+            recv_sem.at[source], device_id={"head": partner}, device_id_type=MESH_ID,
+        )
+        forward.start()
+        sent.append(forward)
+    for j in range(chips):
+        slot = j * 2 + 1 - core
+        arriving = pltpu.make_async_remote_copy(
+            x_ref, out_ref.at[slot], send_sem.at[0], recv_sem.at[slot],
+            device_id={"head": partner}, device_id_type=MESH_ID,
+        )
+        arriving.wait_recv()
+    local.wait()
+    for copy in sent:
+        copy.wait_send()
+
+
+def head_gather(x, size):
+    return pl.pallas_call(
+        functools.partial(head_gather_body, size=size),
+        out_shape=jax.ShapeDtypeStruct((size,) + x.shape, x.dtype),
+        in_specs=[pl.BlockSpec(memory_space=pltpu.VMEM)],
+        out_specs=pl.BlockSpec(memory_space=pl.ANY),
+        scratch_shapes=[
+            pltpu.SemaphoreType.DMA((size - 1,)),
+            pltpu.SemaphoreType.DMA((size,)),
+            pltpu.SemaphoreType.DMA,
+        ],
+        compiler_params=pltpu.CompilerParams(collective_id=0, has_side_effects=True),
+    )(x)
 
 
 def expert_half(slot_rows, gate_half, up_half, down_half):
@@ -135,7 +213,10 @@
     head_count = head_width // DH
     score_scale = 1.0 / math.sqrt(DH)
     cells_flat = table_cells.reshape(cell_count * tables, model_width)
-    flat_rows = lax.all_gather(cells_flat, "head", axis=0, tiled=True)
+    head_size = lax.axis_size("head")
+    flat_rows = head_gather(cells_flat, head_size).reshape(
+        head_size * cells_flat.shape[0], model_width
+    )
     row_cells = flat_rows.shape[0] // tables
     q_all = (
         jnp.dot(flat_rows, w_query, preferred_element_type=jnp.float32)

time: 324 us -> 315 us (0.972)
  waiting for transfers between devices: 129 us -> 90.9 us
  Pallas kernels: 36.7 us -> 63.7 us
    all_gather x1 -> x0, waiting for transfers between devices: 36.3 us -> none  [shards(): flat_rows = lax.all_gather(cells_flat, 'head', axis=0, tiled=True)]
    pallas_call x0 -> x1, Pallas kernels: none -> 33.7 us  [head_gather(): pl.pallas_call(functools.partial(head_gather_body, size=size), out_shape=...]
    pallas_call x1, Pallas kernels: 36.7 us -> 30 us  [flash_attention(): pl.pallas_call(functools.partial(flash_body, scale=scale, key_block=key_b...]
    ppermute x7, waiting for transfers between devices: 78.7 us -> 72.5 us  [shards(): lax.ppermute(w_out, 'head', [(index, (index + shift) % head_size) for ind...]
    all_gather x1, waiting for transfers between devices: 5.49 us -> 10.1 us  [shards(): kv_all = lax.all_gather(kv_rows, 'expert', axis=0, tiled=True)]
    unnamed x31 -> x27, local copies, waits for them, and re-layouts: 20.1 us -> 20.1 us
  transfers between devices with their start and end apart: 12 -> 11, of which waited for: 7 -> 7; matrix products, arithmetic and copies ran while one was open for 8% -> 9% of each run, Pallas kernels for 11% -> 10%
where the time goes in v10:
time: 315 us; the launch traced here: 314 us
  waiting for transfers between devices  90.9 us (29%)
  Pallas kernels  63.7 us (20%)
  blocking collectives  49.7 us (16%)
  local copies, waits for them, and re-layouts  47.3 us (15%)
  matrix products  28.6 us (9%)
  starting transfers between devices  15.6 us (5%)
  between operations  13.6 us (4%)
  other arithmetic  4.41 us (1%)
    ppermute x7, waiting for transfers between devices, shards(): lax.ppermute(w_out, 'head', [(index, (index + shift) % head_size) for ind...  72.5 us
    pallas_call x1, Pallas kernels, head_gather(): pl.pallas_call(functools.partial(head_gather_body, size=size), out_shape=...  33.7 us
    pallas_call x1, Pallas kernels, flash_attention(): pl.pallas_call(functools.partial(flash_body, scale=scale, key_block=key_b...  30 us
    all_to_all x1, blocking collectives, shards(): received = lax.all_to_all(send_rows, ('expert', 'head'), 0, 0, tiled=True)  25.6 us
    all_to_all x1, blocking collectives, shards(): lax.all_to_all(summed_halves, ('expert', 'head'), 0, 0, tiled=True)  24.1 us
    unnamed x27, local copies, waits for them, and re-layouts  20.1 us
    all_gather x1, waiting for transfers between devices, shards(): kv_all = lax.all_gather(kv_rows, 'expert', axis=0, tiled=True)  10.1 us
    ppermute x7, starting transfers between devices, shards(): lax.ppermute(w_out, 'head', [(index, (index + shift) % head_size) for ind...  8.85 us
  transfers between devices with their start and end apart: 11, of which 7 were waited for; matrix products, arithmetic and copies ran while one was open for 9% of the time, Pallas kernels for 10%

profile of v10, /device:TPU:1, one launch (start us, length us, event | category | flops | bytes accessed | tf_op | source)
XLA Modules:
  0.0 313.8 jit_solution(4100006843170707425)
XLA Ops:
  6.5 2.2 reshape.106.x_ref
  8.7 33.7 %shard_map.118 = bf16[8,128,2048]{2,1,0:T(8,128)(2,1)} custom-call(bf16[128,2048]{1,0:T(8,128)(2,1)} %reshape.106.x_ref), custom_call_target="tpu_custom_call" | custom-call | tf_op jit(solution)/shard_map/pallas_call | solution.py:170
  42.4 6.2 %fusion.19 = bf16[1024,512]{0,1:T(8,128)(2,1)} fusion(bf16[1024,2048]{1,0:T(8,128)(2,1)} %bitcast.44, bf16[2048,256]{1,0:T(8,128)(2,1)} %param.15, bf16[2048,256]{1,0:T(8,128)(2,1)} %param.14), kind=kOutput, calls=%fused_computation.20 | convolution fusion | flops 2152202240 | bytes 7340032 | tf_op jit(solution)/shard_map/dot_general | solution.py:228
  48.6 2.3 copy.17
  50.9 2.3 reshape.110
  53.2 1.5 collective-permute-start.1
  54.7 1.1 collective-permute-start.2
  55.8 1.3 collective-permute-start.3
  57.1 2.6 collective-permute-start.4
  59.7 3.7 %convolution_convert_fusion.2 = bf16[1024,256]{1,0:T(8,128)(2,1)S(1)} fusion(bf16[1024,2048]{1,0:T(8,128)(2,1)} %bitcast.45, bf16[2048,256]{1,0:T(8,128)(2,1)} %param.13), kind=kOutput, calls=%fused_computation.21 | convolution fusion | flops 1074003968 | bytes 5767168 | tf_op jit(solution)/shard_map/dot_general | solution.py:222
  63.5 2.4 constant_dynamic-update-slice_fusion.7
  67.8 8.1 %collective-permute-done = bf16[256,2048]{1,0:T(8,128)(2,1)} collective-permute-done((bf16[256,2048]{1,0:T(8,128)(2,1)}, bf16[256,2048]{1,0:T(8,128)(2,1)}, u32[]{:S(2)}, u32[]{:S(2)}) %collective-permute-start) | collective-permute-done | bytes 1048608 | tf_op jit(solution)/shard_map/ppermute | solution.py:243
  75.9 2.3 collective-permute-start.5
  78.2 2.3 constant_dynamic-update-slice_fusion.6
  80.6 21.6 %collective-permute-done.1 = bf16[256,2048]{1,0:T(8,128)(2,1)} collective-permute-done((bf16[256,2048]{1,0:T(8,128)(2,1)}, bf16[256,2048]{1,0:T(8,128)(2,1)}, u32[]{:S(2)}, u32[]{:S(2)}) %collective-permute-start.1) | collective-permute-done | bytes 1048608 | tf_op jit(solution)/shard_map/ppermute | solution.py:243
  102.2 2.3 constant_dynamic-update-slice_fusion.5
  104.5 42.9 %collective-permute-done.2 = bf16[256,2048]{1,0:T(8,128)(2,1)} collective-permute-done((bf16[256,2048]{1,0:T(8,128)(2,1)}, bf16[256,2048]{1,0:T(8,128)(2,1)}, u32[]{:S(2)}, u32[]{:S(2)}) %collective-permute-start.2) | collective-permute-done | bytes 1048608 | tf_op jit(solution)/shard_map/ppermute | solution.py:243
  147.3 2.3 constant_dynamic-update-slice_fusion.4
  149.7 2.3 constant_dynamic-update-slice_fusion.3
  152.0 2.3 constant_dynamic-update-slice_fusion.2
  154.3 10.1 %all-gather.2.cloned.1.call-done.k_ref.v_ref = bf16[8192,1024]{1,0:T(8,128)(2,1)} async-done(((bf16[512,1024]{1,0:T(8,128)(2,1)}), bf16[8192,1024]{1,0:T(8,128)(2,1)}) %all-gather.2.cloned.1.call-update) | async-done | bytes 16777232 | tf_op jit(solution)/shard_map/all_gather | solution.py:232
  164.4 30.0 %shard_map.119 = bf16[512,512]{1,0:T(8,128)(2,1)} custom-call(s32[3]{0:T(128)} %pad_add_fusion.scalars, bf16[512,512]{1,0:T(8,128)(2,1)} %reshape.109.q_ref, bf16[8192,1024]{1,0:T(8,128)(2,1)} %all-gather.2.cloned.1.call-done.k_ref.v_ref, bf16[8192,1024]{1,0:T(8,128)(2,1)} %all-gather.2.cloned.1.call-done.k_ref.v_ref), custom_call_target="tpu_custom_call" | custom-call | flops 8589934592 | bytes 17825792 | tf_op jit(solution)/shard_map/pallas_call | solution.py:91
  194.4 1.2 reshape.111
  196.5 5.1 %all-to-all-start = ((bf16[8,64,2,256]{3,1,2,0:T(8,128)(2,1)}), bf16[8,64,2,256]{3,1,2,0:T(8,128)(2,1)}, u32[]{:S(2)}, u32[]{:S(2)}) async-start(bf16[8,64,2,256]{3,1,2,0:T(8,128)(2,1)} %copy.18), calls=%async_computation | async-start | bytes 1048576 | tf_op jit(solution)/shard_map/all_to_all | solution.py:248
  201.6 2.3 constant_dynamic-update-slice_fusion.1
  203.9 2.4 constant_dynamic-update-slice_fusion
  206.4 4.8 %all-to-all-done = bf16[8,64,2,256]{3,1,2,0:T(8,128)(2,1)} async-done(((bf16[8,64,2,256]{3,1,2,0:T(8,128)(2,1)}), bf16[8,64,2,256]{3,1,2,0:T(8,128)(2,1)}, u32[]{:S(2)}, u32[]{:S(2)}) %all-to-all-start) | async-done | bytes 524320 | tf_op jit(solution)/shard_map/all_to_all | solution.py:248
  211.2 2.4 gather_fusion
  213.6 1.2 select_bitcast_fusion
  215.2 4.8 %multiply_reduce_fusion = (f32[128]{0:T(128)S(1)}, f32[128,2048]{1,0:T(8,128)S(1)}) fusion(bf16[128,2048]{1,0:T(8,128)(2,1)S(1)} %bitcast.46, bf16[2048,2048]{1,0:T(8,128)(2,1)} %constant_dynamic-update-slice_fusion, bf16[128,2048]{1,0:T(8,128)(2,1)S(1)} %copy-done.2), kind=kOutput, calls=%fused_computation.23 | convolution fusion | flops 1074790272 | bytes 10486272 | tf_op jit(solution)/shard_map/dot_general | solution.py:253
  221.0 1.5 convolution_convert_fusion.1
  222.5 2.5 all_to_all.20
  225.0 25.6 %all_to_all.29 = bf16[128,2,2048]{2,1,0:T(2,128)(2,1)} all-to-all(bf16[128,2,2048]{2,1,0:T(2,128)(2,1)} %all_to_all.20), channel_id=1, replica_groups=mesh['expert'=16,'head'=8] {'expert','head'}, dimensions={0} | all-to-all | bytes 2097152 | tf_op jit(solution)/shard_map/all_to_all | solution.py:278
  250.6 2.2 all_to_all.22
  252.8 1.2 collective-permute-start.7
  254.0 1.3 constant_dynamic-update-slice_fusion.9
  255.3 1.2 collective-permute-done.7
  256.6 1.3 copy-done.3
  257.9 2.8 fusion.13
  260.8 7.6 %convolution_convert_fusion = bf16[512,2048]{1,0:T(8,128)(2,1)} fusion(bf16[1,704,2048]{2,1,0:T(8,128)(2,1)S(1)} %copy-done, f32[704,512]{1,0:T(8,128)} %fusion.13, bf16[512,2048]{1,0:T(8,128)(2,1)} %copy-done.3, bf16[1,704,2048]{2,1,0:T(8,128)(2,1)} %param.19), kind=kOutput, calls=%fused_computation.1 | convolution fusion | flops 2956001280 | bytes 11403264 | tf_op jit(solution)/shard_map/dot_general | solution.py:191
  268.4 1.3 slice.11
  270.2 2.3 collective-permute-done.8
  272.4 2.6 add_convert_fusion
  275.0 2.5 all_to_all.23
  277.6 24.1 %all_to_all.30 = bf16[128,2,2048]{2,1,0:T(2,128)(2,1)} all-to-all(bf16[128,2,2048]{2,1,0:T(2,128)(2,1)} %all_to_all.23), channel_id=1, replica_groups=mesh['expert'=16,'head'=8] {'expert','head'}, dimensions={0} | all-to-all | bytes 2097152 | tf_op jit(solution)/shard_map/all_to_all | solution.py:286
  301.7 2.2 all_to_all.25
  303.9 1.9 fusion.5
  305.8 1.1 reshape.113
  (40 shorter events, 4.8 us)
Async XLA Ops:
  6.5 254.2 %copy-start = (bf16[1,704,2048]{2,1,0:T(8,128)(2,1)S(1)}, bf16[1,704,2048]{2,1,0:T(8,128)(2,1)}, u32[]{:S(2)}) copy-start(bf16[1,704,2048]{2,1,0:T(8,128)(2,1)} %param.20) | copy-start | bytes 8650756
  6.5 157.9 %all-gather.2.cloned.1.call-start = ((), (), s32[]{:S(2)}) async-start(), calls=%async_computation.3 | async-start | bytes 17825792 | tf_op jit(solution)/shard_map/all_gather | solution.py:232
  53.2 12.8 %copy-start.5 = (s32[64,2]{0,1:T(2,128)S(1)}, s32[64,2]{0,1:T(2,128)}, u32[]{:S(2)}) copy-start(s32[64,2]{0,1:T(2,128)} %param.23) | copy-start | bytes 1540
  53.2 12.8 %copy-start.6 = (s32[64,2]{0,1:T(2,128)S(1)}, s32[64,2]{0,1:T(2,128)}, u32[]{:S(2)}) copy-start(s32[64,2]{0,1:T(2,128)} %param.22) | copy-start | bytes 1540
  53.2 12.8 %copy-start.8 = (s32[2]{0:T(128)S(1)}, s32[2]{0:T(128)}, u32[]{:S(2)}) copy-start(s32[2]{0:T(128)} %param.21) | copy-start | bytes 28
  53.2 22.7 %collective-permute-start = (bf16[256,2048]{1,0:T(8,128)(2,1)}, bf16[256,2048]{1,0:T(8,128)(2,1)}, u32[]{:S(2)}, u32[]{:S(2)}) collective-permute-start(bf16[256,2048]{1,0:T(8,128)(2,1)} %param.16), channel_id=1, source_target_pairs={{0,1},{1,2},{2,3},{3,4},{4,5},{5,6},{6,7},{7,0},{8,9},{9,10},{10,1... | collective-permute-start | bytes 3145736 | tf_op jit(solution)/shard_map/ppermute | solution.py:243
  53.2 48.9 %collective-permute-start.1 = (bf16[256,2048]{1,0:T(8,128)(2,1)}, bf16[256,2048]{1,0:T(8,128)(2,1)}, u32[]{:S(2)}, u32[]{:S(2)}) collective-permute-start(bf16[256,2048]{1,0:T(8,128)(2,1)} %param.16), channel_id=1, source_target_pairs={{0,2},{1,3},{2,4},{3,5},{4,6},{5,7},{6,0},{7,1},{8,10},{9,11},{10,... | collective-permute-start | bytes 3145736 | tf_op jit(solution)/shard_map/ppermute | solution.py:243
  54.7 92.7 %collective-permute-start.2 = (bf16[256,2048]{1,0:T(8,128)(2,1)}, bf16[256,2048]{1,0:T(8,128)(2,1)}, u32[]{:S(2)}, u32[]{:S(2)}) collective-permute-start(bf16[256,2048]{1,0:T(8,128)(2,1)} %param.16), channel_id=1, source_target_pairs={{0,3},{1,4},{2,5},{3,6},{4,7},{5,0},{6,1},{7,2},{8,11},{9,12},{10,... | collective-permute-start | bytes 3145736 | tf_op jit(solution)/shard_map/ppermute | solution.py:243
  55.8 93.8 %collective-permute-start.3 = (bf16[256,2048]{1,0:T(8,128)(2,1)}, bf16[256,2048]{1,0:T(8,128)(2,1)}, u32[]{:S(2)}, u32[]{:S(2)}) collective-permute-start(bf16[256,2048]{1,0:T(8,128)(2,1)} %param.16), channel_id=1, source_target_pairs={{0,4},{1,5},{2,6},{3,7},{4,0},{5,1},{6,2},{7,3},{8,12},{9,13},{10,... | collective-permute-start | bytes 3145736 | tf_op jit(solution)/shard_map/ppermute | solution.py:243
  57.1 94.9 %collective-permute-start.4 = (bf16[256,2048]{1,0:T(8,128)(2,1)}, bf16[256,2048]{1,0:T(8,128)(2,1)}, u32[]{:S(2)}, u32[]{:S(2)}) collective-permute-start(bf16[256,2048]{1,0:T(8,128)(2,1)} %param.16), channel_id=1, source_target_pairs={{0,5},{1,6},{2,7},{3,0},{4,1},{5,2},{6,3},{7,4},{8,13},{9,14},{10,... | collective-permute-start | bytes 3145736 | tf_op jit(solution)/shard_map/ppermute | solution.py:243
  63.5 4.1 %copy-start.4 = (bf16[2048]{0:T(1024)(128)(2,1)S(1)}, bf16[2048]{0:T(1024)(128)(2,1)}, u32[]{:S(2)}) copy-start(bf16[2048]{0:T(1024)(128)(2,1)} %param.17) | copy-start | bytes 12292
  75.9 125.7 %collective-permute-start.5 = (bf16[256,2048]{1,0:T(8,128)(2,1)}, bf16[256,2048]{1,0:T(8,128)(2,1)}, u32[]{:S(2)}, u32[]{:S(2)}) collective-permute-start(bf16[256,2048]{1,0:T(8,128)(2,1)} %param.16), channel_id=1, source_target_pairs={{0,6},{1,7},{2,0},{3,1},{4,2},{5,3},{6,4},{7,5},{8,14},{9,15},{10,... | collective-permute-start | bytes 3145736 | tf_op jit(solution)/shard_map/ppermute | solution.py:243
  102.2 101.7 %collective-permute-start.6 = (bf16[256,2048]{1,0:T(8,128)(2,1)}, bf16[256,2048]{1,0:T(8,128)(2,1)}, u32[]{:S(2)}, u32[]{:S(2)}) collective-permute-start(bf16[256,2048]{1,0:T(8,128)(2,1)} %param.16), channel_id=1, source_target_pairs={{0,7},{1,0},{2,1},{3,2},{4,3},{5,4},{6,5},{7,6},{8,15},{9,8},{10,9... | collective-permute-start | bytes 3145736 | tf_op jit(solution)/shard_map/ppermute | solution.py:243
  196.5 14.7 %all-to-all-start = ((bf16[8,64,2,256]{3,1,2,0:T(8,128)(2,1)}), bf16[8,64,2,256]{3,1,2,0:T(8,128)(2,1)}, u32[]{:S(2)}, u32[]{:S(2)}) async-start(bf16[8,64,2,256]{3,1,2,0:T(8,128)(2,1)} %copy.18), calls=%async_computation | async-start | bytes 1048576 | tf_op jit(solution)/shard_map/all_to_all | solution.py:248
  203.9 11.3 %copy-start.2 = (bf16[128,2048]{1,0:T(8,128)(2,1)S(1)}, bf16[128,2048]{1,0:T(8,128)(2,1)}, u32[]{:S(2)}) copy-start(bf16[128,2048]{1,0:T(8,128)(2,1)} %reshape.106.x_ref) | copy-start | bytes 1572868
  220.0 1.0 copy-start.1
  252.8 5.1 %copy-start.7 = (bf16[1,704,2048]{2,1,0:T(8,128)(2,1)S(1)}, bf16[1,704,2048]{2,1,0:T(8,128)(2,1)}, u32[]{:S(2)}) copy-start(bf16[1,704,2048]{2,1,0:T(8,128)(2,1)} %param.18) | copy-start | bytes 8650756
  252.8 3.7 %collective-permute-start.7 = (bf16[256,2048]{1,0:T(8,128)(2,1)}, bf16[256,2048]{1,0:T(8,128)(2,1)S(1)}, u32[]{:S(2)}, u32[]{:S(2)}) collective-permute-start(bf16[256,2048]{1,0:T(8,128)(2,1)} %all_to_all.22), channel_id=1, source_target_pairs={{0,1},{1,0},{2,3},{3,2},{4,5},{5,4},{6,7},{7,6},{8,9},{9,8},{10,11... | collective-permute-start | bytes 3145736 | tf_op jit(solution)/shard_map/ppermute | solution.py:280
  256.6 1.3 copy-start.3
  269.7 2.7 collective-permute-start.8
Sparse Core Ops, SparseCore 0:
  53.3 111.0 all-gather.1

commit v11 on v9

--- a/solution.py
+++ b/solution.py
@@ -101,6 +101,72 @@
             bytes_accessed=2 * (q_all.size * 2 + kv_all.size),
         ),
     )(scalars, q_all, kv_all, kv_all)
+
+
+MESH_ID = pl.DeviceIdType.MESH
+
+
+def head_gather_body(x_ref, out_ref, send_sem, recv_sem, local_sem, *, size):
+    chips = size // 2
+    me = lax.axis_index("head")
+    core = me % 2
+    z = me // 2
+    partner = me + 1 - 2 * core
+    step = 1 - 2 * core
+    ahead = ((z + chips + step) % chips) * 2 + core
+    behind = ((z + chips - step) % chips) * 2 + core
+    far = ((z + 2) % chips) * 2 + core
+
+    def remote(src, slot, sem, device):
+        return pltpu.make_async_remote_copy(
+            src, out_ref.at[slot], send_sem.at[sem], recv_sem.at[slot],
+            device_id={"head": device}, device_id_type=MESH_ID,
+        )
+
+    barrier = pltpu.get_barrier_semaphore()
+    for device in (ahead, behind, partner):
+        pl.semaphore_signal(barrier, 1, device_id={"head": device}, device_id_type=MESH_ID)
+    pl.semaphore_wait(barrier, 3)
+
+    local = pltpu.make_async_copy(x_ref, out_ref.at[me], local_sem)
+    local.start()
+    sent = [remote(x_ref, me, 0, ahead), remote(x_ref, me, 1, behind), remote(x_ref, me, 2, partner)]
+    for copy in sent:
+        copy.start()
+    remote(x_ref, behind, 0, behind).wait_recv()
+    relay = remote(out_ref.at[behind], behind, 3, ahead)
+    relay.start()
+    to_partner = remote(out_ref.at[behind], behind, 4, partner)
+    to_partner.start()
+    sent += [relay, to_partner]
+    remote(x_ref, ahead, 0, ahead).wait_recv()
+    to_partner = remote(out_ref.at[ahead], ahead, 5, partner)
+    to_partner.start()
+    sent.append(to_partner)
+    remote(x_ref, far, 0, behind).wait_recv()
+    to_partner = remote(out_ref.at[far], far, 6, partner)
+    to_partner.start()
+    sent.append(to_partner)
+    for j in range(chips):
+        remote(x_ref, j * 2 + 1 - core, 0, partner).wait_recv()
+    local.wait()
+    for copy in sent:
+        copy.wait_send()
+
+
+def head_gather(x, size):
+    return pl.pallas_call(
+        functools.partial(head_gather_body, size=size),
+        out_shape=jax.ShapeDtypeStruct((size,) + x.shape, x.dtype),
+        in_specs=[pl.BlockSpec(memory_space=pltpu.VMEM)],
+        out_specs=pl.BlockSpec(memory_space=pl.ANY),
+        scratch_shapes=[
+            pltpu.SemaphoreType.DMA((size - 1,)),
+            pltpu.SemaphoreType.DMA((size,)),
+            pltpu.SemaphoreType.DMA,
+        ],
+        compiler_params=pltpu.CompilerParams(collective_id=0, has_side_effects=True),
+    )(x)
 
 
 def expert_half(slot_rows, gate_half, up_half, down_half):
@@ -135,7 +201,10 @@
     head_count = head_width // DH
     score_scale = 1.0 / math.sqrt(DH)
     cells_flat = table_cells.reshape(cell_count * tables, model_width)
-    flat_rows = lax.all_gather(cells_flat, "head", axis=0, tiled=True)
+    head_size = lax.axis_size("head")
+    flat_rows = head_gather(cells_flat, head_size).reshape(
+        head_size * cells_flat.shape[0], model_width
+    )
     row_cells = flat_rows.shape[0] // tables
     q_all = (
         jnp.dot(flat_rows, w_query, preferred_element_type=jnp.float32)

time: 324 us -> 318 us (0.981)
  waiting for transfers between devices: 129 us -> 91.3 us
  Pallas kernels: 36.7 us -> 66.4 us
    all_gather x1 -> x0, waiting for transfers between devices: 36.3 us -> none  [shards(): flat_rows = lax.all_gather(cells_flat, 'head', axis=0, tiled=True)]
    pallas_call x0 -> x1, Pallas kernels: none -> 29.7 us  [head_gather(): pl.pallas_call(functools.partial(head_gather_body, size=size), out_shape=...]
    ppermute x7, waiting for transfers between devices: 78.7 us -> 72.9 us  [shards(): lax.ppermute(w_out, 'head', [(index, (index + shift) % head_size) for ind...]
    all_gather x1, waiting for transfers between devices: 5.49 us -> 10.1 us  [shards(): kv_all = lax.all_gather(kv_rows, 'expert', axis=0, tiled=True)]
    unnamed x31 -> x27, local copies, waits for them, and re-layouts: 20.1 us -> 20.1 us
  transfers between devices with their start and end apart: 12 -> 11, of which waited for: 7 -> 7; matrix products, arithmetic and copies ran while one was open for 8% -> 9% of each run, Pallas kernels for 11% -> 12%
where the time goes in v11:
time: 318 us; the launch traced here: 317 us
  waiting for transfers between devices  91.3 us (29%)
  Pallas kernels  66.4 us (21%)
  blocking collectives  49.8 us (16%)
  local copies, waits for them, and re-layouts  47.3 us (15%)
  matrix products  28.6 us (9%)
  starting transfers between devices  15.3 us (5%)
  between operations  13.6 us (4%)
  other arithmetic  4.41 us (1%)
    ppermute x7, waiting for transfers between devices, shards(): lax.ppermute(w_out, 'head', [(index, (index + shift) % head_size) for ind...  72.9 us
    pallas_call x1, Pallas kernels, flash_attention(): pl.pallas_call(functools.partial(flash_body, scale=scale, key_block=key_b...  36.7 us
    pallas_call x1, Pallas kernels, head_gather(): pl.pallas_call(functools.partial(head_gather_body, size=size), out_shape=...  29.7 us
    all_to_all x1, blocking collectives, shards(): received = lax.all_to_all(send_rows, ('expert', 'head'), 0, 0, tiled=True)  25.6 us
    all_to_all x1, blocking collectives, shards(): lax.all_to_all(summed_halves, ('expert', 'head'), 0, 0, tiled=True)  24.1 us
    unnamed x27, local copies, waits for them, and re-layouts  20.1 us
    all_gather x1, waiting for transfers between devices, shards(): kv_all = lax.all_gather(kv_rows, 'expert', axis=0, tiled=True)  10.1 us
    ppermute x7, starting transfers between devices, shards(): lax.ppermute(w_out, 'head', [(index, (index + shift) % head_size) for ind...  8.52 us
  transfers between devices with their start and end apart: 11, of which 7 were waited for; matrix products, arithmetic and copies ran while one was open for 9% of the time, Pallas kernels for 12%

profile of v11, /device:TPU:1, one launch (start us, length us, event | category | flops | bytes accessed | tf_op | source)
XLA Modules:
  0.0 316.6 jit_solution(2295598584301929583)
XLA Ops:
  6.5 2.2 reshape.106.x_ref
  8.7 29.7 %shard_map.118 = bf16[8,128,2048]{2,1,0:T(8,128)(2,1)} custom-call(bf16[128,2048]{1,0:T(8,128)(2,1)} %reshape.106.x_ref), custom_call_target="tpu_custom_call" | custom-call | tf_op jit(solution)/shard_map/pallas_call | solution.py:158
  38.4 6.2 %fusion.19 = bf16[1024,512]{0,1:T(8,128)(2,1)} fusion(bf16[1024,2048]{1,0:T(8,128)(2,1)} %bitcast.44, bf16[2048,256]{1,0:T(8,128)(2,1)} %param.15, bf16[2048,256]{1,0:T(8,128)(2,1)} %param.14), kind=kOutput, calls=%fused_computation.20 | convolution fusion | flops 2152202240 | bytes 7340032 | tf_op jit(solution)/shard_map/dot_general | solution.py:216
  44.7 2.3 copy.17
  46.9 2.3 reshape.110
  51.5 2.1 collective-permute-start.3
  53.6 2.2 collective-permute-start.4
  55.8 3.7 %convolution_convert_fusion.2 = bf16[1024,256]{1,0:T(8,128)(2,1)S(1)} fusion(bf16[1024,2048]{1,0:T(8,128)(2,1)} %bitcast.45, bf16[2048,256]{1,0:T(8,128)(2,1)} %param.13), kind=kOutput, calls=%fused_computation.21 | convolution fusion | flops 1074003968 | bytes 5767168 | tf_op jit(solution)/shard_map/dot_general | solution.py:210
  59.6 2.4 constant_dynamic-update-slice_fusion.7
  62.7 1.0 reshape.109.q_ref
  63.9 8.4 %collective-permute-done = bf16[256,2048]{1,0:T(8,128)(2,1)} collective-permute-done((bf16[256,2048]{1,0:T(8,128)(2,1)}, bf16[256,2048]{1,0:T(8,128)(2,1)}, u32[]{:S(2)}, u32[]{:S(2)}) %collective-permute-start) | collective-permute-done | bytes 1048608 | tf_op jit(solution)/shard_map/ppermute | solution.py:231
  72.3 2.0 collective-permute-start.5
  74.3 2.3 constant_dynamic-update-slice_fusion.6
  76.6 21.4 %collective-permute-done.1 = bf16[256,2048]{1,0:T(8,128)(2,1)} collective-permute-done((bf16[256,2048]{1,0:T(8,128)(2,1)}, bf16[256,2048]{1,0:T(8,128)(2,1)}, u32[]{:S(2)}, u32[]{:S(2)}) %collective-permute-start.1) | collective-permute-done | bytes 1048608 | tf_op jit(solution)/shard_map/ppermute | solution.py:231
  98.1 2.3 constant_dynamic-update-slice_fusion.5
  100.4 43.0 %collective-permute-done.2 = bf16[256,2048]{1,0:T(8,128)(2,1)} collective-permute-done((bf16[256,2048]{1,0:T(8,128)(2,1)}, bf16[256,2048]{1,0:T(8,128)(2,1)}, u32[]{:S(2)}, u32[]{:S(2)}) %collective-permute-start.2) | collective-permute-done | bytes 1048608 | tf_op jit(solution)/shard_map/ppermute | solution.py:231
  143.4 2.3 constant_dynamic-update-slice_fusion.4
  145.7 2.3 constant_dynamic-update-slice_fusion.3
  148.0 2.3 constant_dynamic-update-slice_fusion.2
  150.4 10.1 %all-gather.2.cloned.1.call-done.k_ref.v_ref = bf16[8192,1024]{1,0:T(8,128)(2,1)} async-done(((bf16[512,1024]{1,0:T(8,128)(2,1)}), bf16[8192,1024]{1,0:T(8,128)(2,1)}) %all-gather.2.cloned.1.call-update) | async-done | bytes 16777232 | tf_op jit(solution)/shard_map/all_gather | solution.py:220
  160.4 36.7 %shard_map.119 = bf16[512,512]{1,0:T(8,128)(2,1)} custom-call(s32[3]{0:T(128)} %pad_add_fusion.scalars, bf16[512,512]{1,0:T(8,128)(2,1)} %reshape.109.q_ref, bf16[8192,1024]{1,0:T(8,128)(2,1)} %all-gather.2.cloned.1.call-done.k_ref.v_ref, bf16[8192,1024]{1,0:T(8,128)(2,1)} %all-gather.2.cloned.1.call-done.k_ref.v_ref), custom_call_target="tpu_custom_call" | custom-call | flops 8589934592 | bytes 17825792 | tf_op jit(solution)/shard_map/pallas_call | solution.py:91
  197.1 1.2 reshape.111
  199.2 5.1 %all-to-all-start = ((bf16[8,64,2,256]{3,1,2,0:T(8,128)(2,1)}), bf16[8,64,2,256]{3,1,2,0:T(8,128)(2,1)}, u32[]{:S(2)}, u32[]{:S(2)}) async-start(bf16[8,64,2,256]{3,1,2,0:T(8,128)(2,1)} %copy.18), calls=%async_computation | async-start | bytes 1048576 | tf_op jit(solution)/shard_map/all_to_all | solution.py:236
  204.3 2.3 constant_dynamic-update-slice_fusion.1
  206.7 2.4 constant_dynamic-update-slice_fusion
  209.1 4.8 %all-to-all-done = bf16[8,64,2,256]{3,1,2,0:T(8,128)(2,1)} async-done(((bf16[8,64,2,256]{3,1,2,0:T(8,128)(2,1)}), bf16[8,64,2,256]{3,1,2,0:T(8,128)(2,1)}, u32[]{:S(2)}, u32[]{:S(2)}) %all-to-all-start) | async-done | bytes 524320 | tf_op jit(solution)/shard_map/all_to_all | solution.py:236
  213.9 2.4 gather_fusion
  216.4 1.2 select_bitcast_fusion
  217.9 4.8 %multiply_reduce_fusion = (f32[128]{0:T(128)S(1)}, f32[128,2048]{1,0:T(8,128)S(1)}) fusion(bf16[128,2048]{1,0:T(8,128)(2,1)S(1)} %bitcast.46, bf16[2048,2048]{1,0:T(8,128)(2,1)} %constant_dynamic-update-slice_fusion, bf16[128,2048]{1,0:T(8,128)(2,1)S(1)} %copy-done.2), kind=kOutput, calls=%fused_computation.23 | convolution fusion | flops 1074790272 | bytes 10486272 | tf_op jit(solution)/shard_map/dot_general | solution.py:241
  222.8 1.0 copy-done.1
  223.7 1.5 convolution_convert_fusion.1
  225.2 2.5 all_to_all.20
  227.8 25.6 %all_to_all.29 = bf16[128,2,2048]{2,1,0:T(2,128)(2,1)} all-to-all(bf16[128,2,2048]{2,1,0:T(2,128)(2,1)} %all_to_all.20), channel_id=1, replica_groups=mesh['expert'=16,'head'=8] {'expert','head'}, dimensions={0} | all-to-all | bytes 2097152 | tf_op jit(solution)/shard_map/all_to_all | solution.py:266
  253.4 2.2 all_to_all.22
  255.6 1.2 collective-permute-start.7
  256.8 1.3 constant_dynamic-update-slice_fusion.9
  258.1 1.2 collective-permute-done.7
  259.4 1.3 copy-done.3
  260.7 2.8 fusion.13
  263.5 7.6 %convolution_convert_fusion = bf16[512,2048]{1,0:T(8,128)(2,1)} fusion(bf16[1,704,2048]{2,1,0:T(8,128)(2,1)S(1)} %copy-done, f32[704,512]{1,0:T(8,128)} %fusion.13, bf16[512,2048]{1,0:T(8,128)(2,1)} %copy-done.3, bf16[1,704,2048]{2,1,0:T(8,128)(2,1)} %param.19), kind=kOutput, calls=%fused_computation.1 | convolution fusion | flops 2956001280 | bytes 11403264 | tf_op jit(solution)/shard_map/dot_general | solution.py:179
  271.2 1.3 slice.11
  272.9 2.3 collective-permute-done.8
  275.2 2.6 add_convert_fusion
  277.8 2.5 all_to_all.23
  280.3 24.1 %all_to_all.30 = bf16[128,2,2048]{2,1,0:T(2,128)(2,1)} all-to-all(bf16[128,2,2048]{2,1,0:T(2,128)(2,1)} %all_to_all.23), channel_id=1, replica_groups=mesh['expert'=16,'head'=8] {'expert','head'}, dimensions={0} | all-to-all | bytes 2097152 | tf_op jit(solution)/shard_map/all_to_all | solution.py:274
  304.5 2.2 all_to_all.25
  306.7 1.9 fusion.5
  308.6 1.1 reshape.113
  (40 shorter events, 5.0 us)
Async XLA Ops:
  6.5 257.0 %copy-start = (bf16[1,704,2048]{2,1,0:T(8,128)(2,1)S(1)}, bf16[1,704,2048]{2,1,0:T(8,128)(2,1)}, u32[]{:S(2)}) copy-start(bf16[1,704,2048]{2,1,0:T(8,128)(2,1)} %param.20) | copy-start | bytes 8650756
  6.5 153.9 %all-gather.2.cloned.1.call-start = ((), (), s32[]{:S(2)}) async-start(), calls=%async_computation.3 | async-start | bytes 17825792 | tf_op jit(solution)/shard_map/all_gather | solution.py:220
  49.2 12.8 %copy-start.5 = (s32[64,2]{0,1:T(2,128)S(1)}, s32[64,2]{0,1:T(2,128)}, u32[]{:S(2)}) copy-start(s32[64,2]{0,1:T(2,128)} %param.23) | copy-start | bytes 1540
  49.2 12.8 %copy-start.6 = (s32[64,2]{0,1:T(2,128)S(1)}, s32[64,2]{0,1:T(2,128)}, u32[]{:S(2)}) copy-start(s32[64,2]{0,1:T(2,128)} %param.22) | copy-start | bytes 1540
  49.2 12.8 %copy-start.8 = (s32[2]{0:T(128)S(1)}, s32[2]{0:T(128)}, u32[]{:S(2)}) copy-start(s32[2]{0:T(128)} %param.21) | copy-start | bytes 28
  49.3 23.0 %collective-permute-start = (bf16[256,2048]{1,0:T(8,128)(2,1)}, bf16[256,2048]{1,0:T(8,128)(2,1)}, u32[]{:S(2)}, u32[]{:S(2)}) collective-permute-start(bf16[256,2048]{1,0:T(8,128)(2,1)} %param.16), channel_id=1, source_target_pairs={{0,1},{1,2},{2,3},{3,4},{4,5},{5,6},{6,7},{7,0},{8,9},{9,10},{10,1... | collective-permute-start | bytes 3145736 | tf_op jit(solution)/shard_map/ppermute | solution.py:231
  50.0 48.1 %collective-permute-start.1 = (bf16[256,2048]{1,0:T(8,128)(2,1)}, bf16[256,2048]{1,0:T(8,128)(2,1)}, u32[]{:S(2)}, u32[]{:S(2)}) collective-permute-start(bf16[256,2048]{1,0:T(8,128)(2,1)} %param.16), channel_id=1, source_target_pairs={{0,2},{1,3},{2,4},{3,5},{4,6},{5,7},{6,0},{7,1},{8,10},{9,11},{10,... | collective-permute-start | bytes 3145736 | tf_op jit(solution)/shard_map/ppermute | solution.py:231
  50.7 92.7 %collective-permute-start.2 = (bf16[256,2048]{1,0:T(8,128)(2,1)}, bf16[256,2048]{1,0:T(8,128)(2,1)}, u32[]{:S(2)}, u32[]{:S(2)}) collective-permute-start(bf16[256,2048]{1,0:T(8,128)(2,1)} %param.16), channel_id=1, source_target_pairs={{0,3},{1,4},{2,5},{3,6},{4,7},{5,0},{6,1},{7,2},{8,11},{9,12},{10,... | collective-permute-start | bytes 3145736 | tf_op jit(solution)/shard_map/ppermute | solution.py:231
  51.5 94.3 %collective-permute-start.3 = (bf16[256,2048]{1,0:T(8,128)(2,1)}, bf16[256,2048]{1,0:T(8,128)(2,1)}, u32[]{:S(2)}, u32[]{:S(2)}) collective-permute-start(bf16[256,2048]{1,0:T(8,128)(2,1)} %param.16), channel_id=1, source_target_pairs={{0,4},{1,5},{2,6},{3,7},{4,0},{5,1},{6,2},{7,3},{8,12},{9,13},{10,... | collective-permute-start | bytes 3145736 | tf_op jit(solution)/shard_map/ppermute | solution.py:231
  53.6 94.4 %collective-permute-start.4 = (bf16[256,2048]{1,0:T(8,128)(2,1)}, bf16[256,2048]{1,0:T(8,128)(2,1)}, u32[]{:S(2)}, u32[]{:S(2)}) collective-permute-start(bf16[256,2048]{1,0:T(8,128)(2,1)} %param.16), channel_id=1, source_target_pairs={{0,5},{1,6},{2,7},{3,0},{4,1},{5,2},{6,3},{7,4},{8,13},{9,14},{10,... | collective-permute-start | bytes 3145736 | tf_op jit(solution)/shard_map/ppermute | solution.py:231
  59.5 4.1 %copy-start.4 = (bf16[2048]{0:T(1024)(128)(2,1)S(1)}, bf16[2048]{0:T(1024)(128)(2,1)}, u32[]{:S(2)}) copy-start(bf16[2048]{0:T(1024)(128)(2,1)} %param.17) | copy-start | bytes 12292
  72.3 132.0 %collective-permute-start.5 = (bf16[256,2048]{1,0:T(8,128)(2,1)}, bf16[256,2048]{1,0:T(8,128)(2,1)}, u32[]{:S(2)}, u32[]{:S(2)}) collective-permute-start(bf16[256,2048]{1,0:T(8,128)(2,1)} %param.16), channel_id=1, source_target_pairs={{0,6},{1,7},{2,0},{3,1},{4,2},{5,3},{6,4},{7,5},{8,14},{9,15},{10,... | collective-permute-start | bytes 3145736 | tf_op jit(solution)/shard_map/ppermute | solution.py:231
  98.1 108.6 %collective-permute-start.6 = (bf16[256,2048]{1,0:T(8,128)(2,1)}, bf16[256,2048]{1,0:T(8,128)(2,1)}, u32[]{:S(2)}, u32[]{:S(2)}) collective-permute-start(bf16[256,2048]{1,0:T(8,128)(2,1)} %param.16), channel_id=1, source_target_pairs={{0,7},{1,0},{2,1},{3,2},{4,3},{5,4},{6,5},{7,6},{8,15},{9,8},{10,9... | collective-permute-start | bytes 3145736 | tf_op jit(solution)/shard_map/ppermute | solution.py:231
  199.2 14.7 %all-to-all-start = ((bf16[8,64,2,256]{3,1,2,0:T(8,128)(2,1)}), bf16[8,64,2,256]{3,1,2,0:T(8,128)(2,1)}, u32[]{:S(2)}, u32[]{:S(2)}) async-start(bf16[8,64,2,256]{3,1,2,0:T(8,128)(2,1)} %copy.18), calls=%async_computation | async-start | bytes 1048576 | tf_op jit(solution)/shard_map/all_to_all | solution.py:236
  206.7 11.3 %copy-start.2 = (bf16[128,2048]{1,0:T(8,128)(2,1)S(1)}, bf16[128,2048]{1,0:T(8,128)(2,1)}, u32[]{:S(2)}) copy-start(bf16[128,2048]{1,0:T(8,128)(2,1)} %reshape.106.x_ref) | copy-start | bytes 1572868
  222.8 1.0 copy-start.1
  255.6 5.1 %copy-start.7 = (bf16[1,704,2048]{2,1,0:T(8,128)(2,1)S(1)}, bf16[1,704,2048]{2,1,0:T(8,128)(2,1)}, u32[]{:S(2)}) copy-start(bf16[1,704,2048]{2,1,0:T(8,128)(2,1)} %param.18) | copy-start | bytes 8650756
  255.6 3.7 %collective-permute-start.7 = (bf16[256,2048]{1,0:T(8,128)(2,1)}, bf16[256,2048]{1,0:T(8,128)(2,1)S(1)}, u32[]{:S(2)}, u32[]{:S(2)}) collective-permute-start(bf16[256,2048]{1,0:T(8,128)(2,1)} %all_to_all.22), channel_id=1, source_target_pairs={{0,1},{1,0},{2,3},{3,2},{4,5},{5,4},{6,7},{7,6},{8,9},{9,8},{10,11... | collective-permute-start | bytes 3145736 | tf_op jit(solution)/shard_map/ppermute | solution.py:268
  259.4 1.3 copy-start.3
  272.5 2.7 collective-permute-start.8
Sparse Core Ops, SparseCore 0:
  49.3 111.0 all-gather.1

commit v12 on v11

--- a/solution.py
+++ b/solution.py
@@ -232,17 +232,14 @@
                 w_out, "head", [(index, (index + shift) % head_size) for index in range(head_size)]
             )
         )
-    w_rel = jnp.concatenate(w_parts, axis=0)
     by_owner = lax.all_to_all(
         attended.reshape(head_size, cell_count, tables, head_width), "head", 0, 0, tiled=True
     )
     groups_rel = (me_head - jnp.arange(head_size)) % head_size
-    rel = jnp.take(by_owner, groups_rel, axis=0).transpose(1, 2, 0, 3)
-    summed = jnp.dot(
-        rel.reshape(cell_count * tables, head_size * head_width),
-        w_rel,
-        preferred_element_type=jnp.float32,
-    )
+    rel = jnp.take(by_owner, groups_rel, axis=0).reshape(head_size, cell_count * tables, head_width)
+    summed = jnp.dot(rel[0], w_parts[0], preferred_element_type=jnp.float32)
+    for shift in range(1, head_size):
+        summed = summed + jnp.dot(rel[shift], w_parts[shift], preferred_element_type=jnp.float32)
     residual = cells_flat.astype(jnp.float32) + summed
     mean_square = jnp.mean(residual * residual, axis=-1, keepdims=True)
     normed = (residual * lax.rsqrt(mean_square + 1e-06) * norm_gain.astype(jnp.float32)).astype(

time: 318 us -> 351 us (1.10)
  waiting for transfers between devices: 91.3 us -> 141 us
  local copies, waits for them, and re-layouts: 47.3 us -> 28.8 us
  matrix products: 28.6 us -> 34.1 us
    all_gather x1, waiting for transfers between devices: 10.1 us -> 99.7 us  [shards(): kv_all = lax.all_gather(kv_rows, 'expert', axis=0, tiled=True)]
    ppermute x7, waiting for transfers between devices: 72.9 us -> 28.9 us  [shards(): lax.ppermute(w_out, 'head', [(index, (index + shift) % head_size) for ind...]
    unnamed x27 -> x23, local copies, waits for them, and re-layouts: 20.1 us -> 3.62 us
    dot_general x1 -> x8, matrix products: 4.81 us -> 10.3 us  [the longest x7 8.65 us: shards(): jnp.dot(rel[shift], w_parts[shift], preferred_element_type=jnp.float32)]
    all_to_all x1, waiting for transfers between devices: 4.82 us -> 9.15 us  [shards(): lax.all_to_all(attended.reshape(head_size, cell_count, tables, head_width...]
  transfers between devices with their start and end apart: 11 -> 11, of which waited for: 7 -> 6; matrix products, arithmetic and copies ran while one was open for 9% -> 7% of each run, Pallas kernels for 12% -> 10%
where the time goes in v12:
time: 351 us; the launch traced here: 350 us
  waiting for transfers between devices  141 us (40%)
  Pallas kernels  66.4 us (19%)
  blocking collectives  48.4 us (14%)
  matrix products  34.1 us (10%)
  local copies, waits for them, and re-layouts  28.8 us (8%)
  starting transfers between devices  14 us (4%)
  between operations  13.7 us (4%)
  other arithmetic  3.6 us (1%)
    all_gather x1, waiting for transfers between devices, shards(): kv_all = lax.all_gather(kv_rows, 'expert', axis=0, tiled=True)  99.7 us
    pallas_call x1, Pallas kernels, flash_attention(): pl.pallas_call(functools.partial(flash_body, scale=scale, key_block=key_b...  36.7 us
    pallas_call x1, Pallas kernels, head_gather(): pl.pallas_call(functools.partial(head_gather_body, size=size), out_shape=...  29.7 us
    ppermute x7, waiting for transfers between devices, shards(): lax.ppermute(w_out, 'head', [(index, (index + shift) % head_size) for ind...  28.9 us
    all_to_all x1, blocking collectives, shards(): received = lax.all_to_all(send_rows, ('expert', 'head'), 0, 0, tiled=True)  24.2 us
    all_to_all x1, blocking collectives, shards(): lax.all_to_all(summed_halves, ('expert', 'head'), 0, 0, tiled=True)  24.1 us
    all_to_all x1, waiting for transfers between devices, shards(): lax.all_to_all(attended.reshape(head_size, cell_count, tables, head_width...  9.15 us
    dot_general x7, matrix products, shards(): jnp.dot(rel[shift], w_parts[shift], preferred_element_type=jnp.float32)  8.65 us
  transfers between devices with their start and end apart: 11, of which 6 were waited for; matrix products, arithmetic and copies ran while one was open for 7% of the time, Pallas kernels for 10%

profile of v12, /device:TPU:1, one launch (start us, length us, event | category | flops | bytes accessed | tf_op | source)
XLA Modules:
  0.0 350.3 jit_solution(5389539022197113488)
XLA Ops:
  6.5 2.2 reshape.120.x_ref
  8.7 29.7 %shard_map.118 = bf16[8,128,2048]{2,1,0:T(8,128)(2,1)} custom-call(bf16[128,2048]{1,0:T(8,128)(2,1)} %reshape.120.x_ref), custom_call_target="tpu_custom_call" | custom-call | tf_op jit(solution)/shard_map/pallas_call | solution.py:158
  38.4 6.2 %fusion.25 = bf16[1024,512]{0,1:T(8,128)(2,1)} fusion(bf16[1024,2048]{1,0:T(8,128)(2,1)} %bitcast.53, bf16[2048,256]{1,0:T(8,128)(2,1)} %param.15, bf16[2048,256]{1,0:T(8,128)(2,1)} %param.14), kind=kOutput, calls=%fused_computation.27 | convolution fusion | flops 2152202240 | bytes 7340032 | tf_op jit(solution)/shard_map/dot_general | solution.py:216
  44.7 2.3 copy.15
  47.0 2.2 reshape.124
  49.5 3.1 collective-permute-start.4
  52.5 0.6 collective-permute-start.3
  53.2 2.2 collective-permute-start.2
  55.3 3.7 %convolution_convert_fusion.2 = bf16[1024,256]{1,0:T(8,128)(2,1)S(1)} fusion(bf16[1024,2048]{1,0:T(8,128)(2,1)} %bitcast.54, bf16[2048,256]{1,0:T(8,128)(2,1)} %param.13), kind=kOutput, calls=%fused_computation.28 | convolution fusion | flops 1074003968 | bytes 5767168 | tf_op jit(solution)/shard_map/dot_general | solution.py:210
  59.1 1.0 reshape.123.q_ref
  60.1 0.6 pad_add_fusion.scalars
  60.7 99.7 %all-gather.2.cloned.1.call-done.k_ref.v_ref = bf16[8192,1024]{1,0:T(8,128)(2,1)} async-done(((bf16[512,1024]{1,0:T(8,128)(2,1)}), bf16[8192,1024]{1,0:T(8,128)(2,1)}) %all-gather.2.cloned.1.call-update) | async-done | bytes 16777232 | tf_op jit(solution)/shard_map/all_gather | solution.py:220
  160.4 36.7 %shard_map.119 = bf16[512,512]{1,0:T(8,128)(2,1)} custom-call(s32[3]{0:T(128)} %pad_add_fusion.scalars, bf16[512,512]{1,0:T(8,128)(2,1)} %reshape.123.q_ref, bf16[8192,1024]{1,0:T(8,128)(2,1)} %all-gather.2.cloned.1.call-done.k_ref.v_ref, bf16[8192,1024]{1,0:T(8,128)(2,1)} %all-gather.2.cloned.1.call-done.k_ref.v_ref), custom_call_target="tpu_custom_call" | custom-call | flops 8589934592 | bytes 17825792 | tf_op jit(solution)/shard_map/pallas_call | solution.py:91
  197.1 2.0 reshape.125
  199.1 5.1 %all-to-all-start = ((bf16[8,64,2,256]{3,2,1,0:T(2,128)(2,1)}), bf16[8,64,2,256]{3,2,1,0:T(2,128)(2,1)S(1)}, u32[]{:S(2)}, u32[]{:S(2)}) async-start(bf16[8,64,2,256]{3,2,1,0:T(2,128)(2,1)} %reshape.125), calls=%async_computation | async-start | bytes 1048576 | tf_op jit(solution)/shard_map/all_to_all | solution.py:235
  204.6 9.1 %all-to-all-done = bf16[8,64,2,256]{3,2,1,0:T(2,128)(2,1)S(1)} async-done(((bf16[8,64,2,256]{3,2,1,0:T(2,128)(2,1)}), bf16[8,64,2,256]{3,2,1,0:T(2,128)(2,1)S(1)}, u32[]{:S(2)}, u32[]{:S(2)}) %all-to-all-start) | async-done | bytes 524320 | tf_op jit(solution)/shard_map/all_to_all | solution.py:235
  213.8 2.4 gather_fusion
  216.1 1.6 broadcast_select_fusion
  218.4 1.6 fusion.43
  220.0 1.1 collective-permute-start
  221.1 1.5 fusion.48
  222.7 1.5 fusion.47
  224.3 1.5 fusion.46
  225.8 1.5 fusion.45
  227.4 1.5 fusion.44
  228.9 12.9 %collective-permute-done = bf16[256,2048]{1,0:T(8,128)(2,1)S(1)} collective-permute-done((bf16[256,2048]{1,0:T(8,128)(2,1)S(1)}, bf16[256,2048]{1,0:T(8,128)(2,1)S(1)}, u32[]{:S(2)}, u32[]{:S(2)}) %collective-permute-start) | collective-permute-done | bytes 1048608 | tf_op jit(solution)/shard_map/ppermute | solution.py:231
  242.1 16.0 %collective-permute-done.1 = bf16[256,2048]{1,0:T(8,128)(2,1)S(1)} collective-permute-done((bf16[256,2048]{1,0:T(8,128)(2,1)S(1)}, bf16[256,2048]{1,0:T(8,128)(2,1)S(1)}, u32[]{:S(2)}, u32[]{:S(2)}) %collective-permute-start.1) | collective-permute-done | bytes 1048608 | tf_op jit(solution)/shard_map/ppermute | solution.py:231
  258.1 0.7 multiply_reduce_fusion
  258.8 1.0 copy-done.1
  259.8 1.5 convolution_convert_fusion.1
  261.3 2.5 all_to_all.20
  263.8 24.2 %all_to_all.29 = bf16[128,2,2048]{2,1,0:T(2,128)(2,1)} all-to-all(bf16[128,2,2048]{2,1,0:T(2,128)(2,1)} %all_to_all.20), channel_id=1, replica_groups=mesh['expert'=16,'head'=8] {'expert','head'}, dimensions={0} | all-to-all | bytes 2097152 | tf_op jit(solution)/shard_map/all_to_all | solution.py:263
  288.1 2.3 all_to_all.22
  290.3 1.2 collective-permute-start.7
  291.5 1.3 constant_dynamic-update-slice_fusion.1
  292.8 1.2 collective-permute-done.7
  294.1 1.3 copy-done.5
  295.4 2.8 fusion.19
  298.3 7.6 %convolution_convert_fusion = bf16[512,2048]{1,0:T(8,128)(2,1)} fusion(bf16[1,704,2048]{2,1,0:T(8,128)(2,1)S(1)} %copy-done, f32[704,512]{1,0:T(8,128)} %fusion.19, bf16[512,2048]{1,0:T(8,128)(2,1)} %copy-done.5, bf16[1,704,2048]{2,1,0:T(8,128)(2,1)} %param.19), kind=kOutput, calls=%fused_computation.1 | convolution fusion | flops 2956001280 | bytes 11403264 | tf_op jit(solution)/shard_map/dot_general | solution.py:179
  305.9 1.4 slice.59
  307.3 0.5 collective-permute-start.8
  307.8 2.3 collective-permute-done.8
  310.1 1.4 add_convert_fusion
  311.5 2.5 all_to_all.23
  314.0 24.1 %all_to_all.30 = bf16[128,2,2048]{2,1,0:T(2,128)(2,1)} all-to-all(bf16[128,2,2048]{2,1,0:T(2,128)(2,1)} %all_to_all.23), channel_id=1, replica_groups=mesh['expert'=16,'head'=8] {'expert','head'}, dimensions={0} | all-to-all | bytes 2097152 | tf_op jit(solution)/shard_map/all_to_all | solution.py:271
  338.1 2.3 all_to_all.25
  340.4 1.9 fusion.11
  342.3 1.1 reshape.126
  (49 shorter events, 1.7 us)
Async XLA Ops:
  6.5 291.7 %copy-start = (bf16[1,704,2048]{2,1,0:T(8,128)(2,1)S(1)}, bf16[1,704,2048]{2,1,0:T(8,128)(2,1)}, u32[]{:S(2)}) copy-start(bf16[1,704,2048]{2,1,0:T(8,128)(2,1)} %param.20) | copy-start | bytes 8650756
  6.5 153.9 %all-gather.2.cloned.1.call-start = ((), (), s32[]{:S(2)}) async-start(), calls=%async_computation.3 | async-start | bytes 17825792 | tf_op jit(solution)/shard_map/all_gather | solution.py:220
  49.2 170.8 %collective-permute-start.6 = (bf16[256,2048]{1,0:T(8,128)(2,1)}, bf16[256,2048]{1,0:T(8,128)(2,1)}, u32[]{:S(2)}, u32[]{:S(2)}) collective-permute-start(bf16[256,2048]{1,0:T(8,128)(2,1)} %param.16), channel_id=1, source_target_pairs={{0,7},{1,0},{2,1},{3,2},{4,3},{5,4},{6,5},{7,6},{8,15},{9,8},{10,9... | collective-permute-start | bytes 3145736 | tf_op jit(solution)/shard_map/ppermute | solution.py:231
  49.3 173.3 %collective-permute-start.5 = (bf16[256,2048]{1,0:T(8,128)(2,1)}, bf16[256,2048]{1,0:T(8,128)(2,1)}, u32[]{:S(2)}, u32[]{:S(2)}) collective-permute-start(bf16[256,2048]{1,0:T(8,128)(2,1)} %param.16), channel_id=1, source_target_pairs={{0,6},{1,7},{2,0},{3,1},{4,2},{5,3},{6,4},{7,5},{8,14},{9,15},{10,... | collective-permute-start | bytes 3145736 | tf_op jit(solution)/shard_map/ppermute | solution.py:231
  49.5 174.8 %collective-permute-start.4 = (bf16[256,2048]{1,0:T(8,128)(2,1)}, bf16[256,2048]{1,0:T(8,128)(2,1)}, u32[]{:S(2)}, u32[]{:S(2)}) collective-permute-start(bf16[256,2048]{1,0:T(8,128)(2,1)} %param.16), channel_id=1, source_target_pairs={{0,5},{1,6},{2,7},{3,0},{4,1},{5,2},{6,3},{7,4},{8,13},{9,14},{10,... | collective-permute-start | bytes 3145736 | tf_op jit(solution)/shard_map/ppermute | solution.py:231
  52.5 173.3 %collective-permute-start.3 = (bf16[256,2048]{1,0:T(8,128)(2,1)}, bf16[256,2048]{1,0:T(8,128)(2,1)}, u32[]{:S(2)}, u32[]{:S(2)}) collective-permute-start(bf16[256,2048]{1,0:T(8,128)(2,1)} %param.16), channel_id=1, source_target_pairs={{0,4},{1,5},{2,6},{3,7},{4,0},{5,1},{6,2},{7,3},{8,12},{9,13},{10,... | collective-permute-start | bytes 3145736 | tf_op jit(solution)/shard_map/ppermute | solution.py:231
  53.2 174.2 %collective-permute-start.2 = (bf16[256,2048]{1,0:T(8,128)(2,1)}, bf16[256,2048]{1,0:T(8,128)(2,1)}, u32[]{:S(2)}, u32[]{:S(2)}) collective-permute-start(bf16[256,2048]{1,0:T(8,128)(2,1)} %param.16), channel_id=1, source_target_pairs={{0,3},{1,4},{2,5},{3,6},{4,7},{5,0},{6,1},{7,2},{8,11},{9,12},{10,... | collective-permute-start | bytes 3145736 | tf_op jit(solution)/shard_map/ppermute | solution.py:231
  55.3 4.7 %copy-start.10 = (s32[2]{0:T(128)S(1)}, s32[2]{0:T(128)}, u32[]{:S(2)}) copy-start(s32[2]{0:T(128)} %param.21) | copy-start | bytes 28
  197.1 7.1 %copy-start.7 = (s32[64,2]{0,1:T(2,128)S(1)}, s32[64,2]{0,1:T(2,128)}, u32[]{:S(2)}) copy-start(s32[64,2]{0,1:T(2,128)} %param.23) | copy-start | bytes 1540
  197.1 7.1 %copy-start.8 = (s32[64,2]{0,1:T(2,128)S(1)}, s32[64,2]{0,1:T(2,128)}, u32[]{:S(2)}) copy-start(s32[64,2]{0,1:T(2,128)} %param.22) | copy-start | bytes 1540
  197.1 7.2 %copy-start.6 = (bf16[2048]{0:T(1024)(128)(2,1)S(1)}, bf16[2048]{0:T(1024)(128)(2,1)}, u32[]{:S(2)}) copy-start(bf16[2048]{0:T(1024)(128)(2,1)} %param.17) | copy-start | bytes 12292
  199.1 14.6 %all-to-all-start = ((bf16[8,64,2,256]{3,2,1,0:T(2,128)(2,1)}), bf16[8,64,2,256]{3,2,1,0:T(2,128)(2,1)S(1)}, u32[]{:S(2)}, u32[]{:S(2)}) async-start(bf16[8,64,2,256]{3,2,1,0:T(2,128)(2,1)} %reshape.125), calls=%async_computation | async-start | bytes 1048576 | tf_op jit(solution)/shard_map/all_to_all | solution.py:235
  218.4 1.6 copy-start.4
  220.0 21.8 %collective-permute-start = (bf16[256,2048]{1,0:T(8,128)(2,1)S(1)}, bf16[256,2048]{1,0:T(8,128)(2,1)S(1)}, u32[]{:S(2)}, u32[]{:S(2)}) collective-permute-start(bf16[256,2048]{1,0:T(8,128)(2,1)S(1)} %copy-done.4), channel_id=1, source_target_pairs={{0,1},{1,2},{2,3},{3,4},{4,5},{5,6},{6,7},{7,0},{8,9},{9,10},{10,1... | collective-permute-start | bytes 3145736 | tf_op jit(solution)/shard_map/ppermute | solution.py:231
  222.6 35.5 %collective-permute-start.1 = (bf16[256,2048]{1,0:T(8,128)(2,1)S(1)}, bf16[256,2048]{1,0:T(8,128)(2,1)S(1)}, u32[]{:S(2)}, u32[]{:S(2)}) collective-permute-start(bf16[256,2048]{1,0:T(8,128)(2,1)S(1)} %copy-done.4), channel_id=1, source_target_pairs={{0,2},{1,3},{2,4},{3,5},{4,6},{5,7},{6,0},{7,1},{8,10},{9,11},{10,... | collective-permute-start | bytes 3145736 | tf_op jit(solution)/shard_map/ppermute | solution.py:231
  228.9 29.2 %copy-start.2 = (bf16[128,2048]{1,0:T(8,128)(2,1)S(1)}, bf16[128,2048]{1,0:T(8,128)(2,1)}, u32[]{:S(2)}) copy-start(bf16[128,2048]{1,0:T(8,128)(2,1)} %reshape.120.x_ref) | copy-start | bytes 1572868
  258.8 1.0 copy-start.1
  290.3 5.1 %copy-start.9 = (bf16[1,704,2048]{2,1,0:T(8,128)(2,1)S(1)}, bf16[1,704,2048]{2,1,0:T(8,128)(2,1)}, u32[]{:S(2)}) copy-start(bf16[1,704,2048]{2,1,0:T(8,128)(2,1)} %param.18) | copy-start | bytes 8650756
  290.3 3.7 %collective-permute-start.7 = (bf16[256,2048]{1,0:T(8,128)(2,1)}, bf16[256,2048]{1,0:T(8,128)(2,1)S(1)}, u32[]{:S(2)}, u32[]{:S(2)}) collective-permute-start(bf16[256,2048]{1,0:T(8,128)(2,1)} %all_to_all.22), channel_id=1, source_target_pairs={{0,1},{1,0},{2,3},{3,2},{4,5},{5,4},{6,7},{7,6},{8,9},{9,8},{10,11... | collective-permute-start | bytes 3145736 | tf_op jit(solution)/shard_map/ppermute | solution.py:265
  294.1 1.3 copy-start.5
  305.9 4.2 %copy-start.3 = (bf16[512,2048]{1,0:T(8,128)(2,1)S(1)}, bf16[512,2048]{1,0:T(8,128)(2,1)}, u32[]{:S(2)}) copy-start(bf16[512,2048]{1,0:T(8,128)(2,1)} %convolution_convert_fusion) | copy-start | bytes 6291460
  307.3 2.7 collective-permute-start.8
Sparse Core Ops, SparseCore 0:
  49.3 111.0 all-gather.1

commit v13 on v11

--- a/solution.py
+++ b/solution.py
@@ -104,9 +104,10 @@
 
 
 MESH_ID = pl.DeviceIdType.MESH
-
-
-def head_gather_body(x_ref, out_ref, send_sem, recv_sem, local_sem, *, size):
+GATHER_PARTS = 2
+
+
+def head_gather_body(x_ref, out_ref, send_sem, recv_sem, local_sem, *, size, parts):
     chips = size // 2
     me = lax.axis_index("head")
     core = me % 2
@@ -116,11 +117,13 @@
     ahead = ((z + chips + step) % chips) * 2 + core
     behind = ((z + chips - step) % chips) * 2 + core
     far = ((z + 2) % chips) * 2 + core
-
-    def remote(src, slot, sem, device):
+    rows = x_ref.shape[0] // parts
+
+    def remote(src, slot, part, sem, device):
+        piece = pl.ds(part * rows, rows)
         return pltpu.make_async_remote_copy(
-            src, out_ref.at[slot], send_sem.at[sem], recv_sem.at[slot],
-            device_id={"head": device}, device_id_type=MESH_ID,
+            src.at[piece], out_ref.at[slot, piece], send_sem.at[sem * parts + part],
+            recv_sem.at[slot * parts + part], device_id={"head": device}, device_id_type=MESH_ID,
         )
 
     barrier = pltpu.get_barrier_semaphore()
@@ -130,25 +133,31 @@
 
     local = pltpu.make_async_copy(x_ref, out_ref.at[me], local_sem)
     local.start()
-    sent = [remote(x_ref, me, 0, ahead), remote(x_ref, me, 1, behind), remote(x_ref, me, 2, partner)]
-    for copy in sent:
+    sent = []
+    for part in range(parts):
+        for sem, device in ((0, ahead), (1, behind), (2, partner)):
+            copy = remote(x_ref, me, part, sem, device)
+            copy.start()
+            sent.append(copy)
+    for part in range(parts):
+        remote(x_ref, behind, part, 0, behind).wait_recv()
+        for sem, device in ((3, ahead), (4, partner)):
+            copy = remote(out_ref.at[behind], behind, part, sem, device)
+            copy.start()
+            sent.append(copy)
+    for part in range(parts):
+        remote(x_ref, ahead, part, 0, ahead).wait_recv()
+        copy = remote(out_ref.at[ahead], ahead, part, 5, partner)
         copy.start()
-    remote(x_ref, behind, 0, behind).wait_recv()
-    relay = remote(out_ref.at[behind], behind, 3, ahead)
-    relay.start()
-    to_partner = remote(out_ref.at[behind], behind, 4, partner)
-    to_partner.start()
-    sent += [relay, to_partner]
-    remote(x_ref, ahead, 0, ahead).wait_recv()
-    to_partner = remote(out_ref.at[ahead], ahead, 5, partner)
-    to_partner.start()
-    sent.append(to_partner)
-    remote(x_ref, far, 0, behind).wait_recv()
-    to_partner = remote(out_ref.at[far], far, 6, partner)
-    to_partner.start()
-    sent.append(to_partner)
+        sent.append(copy)
+    for part in range(parts):
+        remote(x_ref, far, part, 0, behind).wait_recv()
+        copy = remote(out_ref.at[far], far, part, 6, partner)
+        copy.start()
+        sent.append(copy)
     for j in range(chips):
-        remote(x_ref, j * 2 + 1 - core, 0, partner).wait_recv()
+        for part in range(parts):
+            remote(x_ref, j * 2 + 1 - core, part, 0, partner).wait_recv()
     local.wait()
     for copy in sent:
         copy.wait_send()
@@ -156,13 +165,13 @@
 
 def head_gather(x, size):
     return pl.pallas_call(
-        functools.partial(head_gather_body, size=size),
+        functools.partial(head_gather_body, size=size, parts=GATHER_PARTS),
         out_shape=jax.ShapeDtypeStruct((size,) + x.shape, x.dtype),
         in_specs=[pl.BlockSpec(memory_space=pltpu.VMEM)],
         out_specs=pl.BlockSpec(memory_space=pl.ANY),
         scratch_shapes=[
-            pltpu.SemaphoreType.DMA((size - 1,)),
-            pltpu.SemaphoreType.DMA((size,)),
+            pltpu.SemaphoreType.DMA(((size - 1) * GATHER_PARTS,)),
+            pltpu.SemaphoreType.DMA((size * GATHER_PARTS,)),
             pltpu.SemaphoreType.DMA,
         ],
         compiler_params=pltpu.CompilerParams(collective_id=0, has_side_effects=True),

time: 318 us -> 315 us (level)
    ppermute x7, waiting for transfers between devices: 72.9 us -> 69.7 us  [shards(): lax.ppermute(w_out, 'head', [(index, (index + shift) % head_size) for ind...]
  transfers between devices with their start and end apart: 11 -> 11, of which waited for: 7 -> 8; matrix products, arithmetic and copies ran while one was open for 9% -> 9% of each run, Pallas kernels for 12% -> 12%
where the time goes in v13:
time: 315 us; the launch traced here: 314 us
  waiting for transfers between devices  91.2 us (29%)
  Pallas kernels  63.4 us (20%)
  blocking collectives  49.7 us (16%)
  local copies, waits for them, and re-layouts  47.3 us (15%)
  matrix products  28.6 us (9%)
  starting transfers between devices  15.3 us (5%)
  between operations  13.6 us (4%)
  other arithmetic  4.41 us (1%)
    ppermute x7, waiting for transfers between devices, shards(): lax.ppermute(w_out, 'head', [(index, (index + shift) % head_size) for ind...  69.7 us
    pallas_call x1, Pallas kernels, flash_attention(): pl.pallas_call(functools.partial(flash_body, scale=scale, key_block=key_b...  36.7 us
    pallas_call x1, Pallas kernels, head_gather(): pl.pallas_call(functools.partial(head_gather_body, size=size, parts=GATHE...  26.7 us
    all_to_all x1, blocking collectives, shards(): received = lax.all_to_all(send_rows, ('expert', 'head'), 0, 0, tiled=True)  25.6 us
    all_to_all x1, blocking collectives, shards(): lax.all_to_all(summed_halves, ('expert', 'head'), 0, 0, tiled=True)  24.1 us
    unnamed x27, local copies, waits for them, and re-layouts  20.1 us
    all_gather x1, waiting for transfers between devices, shards(): kv_all = lax.all_gather(kv_rows, 'expert', axis=0, tiled=True)  13.2 us
    ppermute x7, starting transfers between devices, shards(): lax.ppermute(w_out, 'head', [(index, (index + shift) % head_size) for ind...  8.51 us
  transfers between devices with their start and end apart: 11, of which 8 were waited for; matrix products, arithmetic and copies ran while one was open for 9% of the time, Pallas kernels for 12%

profile of v13, /device:TPU:1, one launch (start us, length us, event | category | flops | bytes accessed | tf_op | source)
XLA Modules:
  0.0 313.5 jit_solution(5658477566422038066)
XLA Ops:
  6.5 2.2 reshape.106.x_ref
  8.7 26.7 %shard_map.118 = bf16[8,128,2048]{2,1,0:T(8,128)(2,1)} custom-call(bf16[128,2048]{1,0:T(8,128)(2,1)} %reshape.106.x_ref), custom_call_target="tpu_custom_call" | custom-call | tf_op jit(solution)/shard_map/pallas_call | solution.py:167
  35.4 6.2 %fusion.19 = bf16[1024,512]{0,1:T(8,128)(2,1)} fusion(bf16[1024,2048]{1,0:T(8,128)(2,1)} %bitcast.44, bf16[2048,256]{1,0:T(8,128)(2,1)} %param.15, bf16[2048,256]{1,0:T(8,128)(2,1)} %param.14), kind=kOutput, calls=%fused_computation.20 | convolution fusion | flops 2152202240 | bytes 7340032 | tf_op jit(solution)/shard_map/dot_general | solution.py:225
  41.6 2.3 copy.17
  43.9 2.3 reshape.110
  47.7 1.7 collective-permute-start.2
  49.4 1.2 collective-permute-start.3
  50.6 2.2 collective-permute-start.4
  52.7 3.7 %convolution_convert_fusion.2 = bf16[1024,256]{1,0:T(8,128)(2,1)S(1)} fusion(bf16[1024,2048]{1,0:T(8,128)(2,1)} %bitcast.45, bf16[2048,256]{1,0:T(8,128)(2,1)} %param.13), kind=kOutput, calls=%fused_computation.21 | convolution fusion | flops 1074003968 | bytes 5767168 | tf_op jit(solution)/shard_map/dot_general | solution.py:219
  56.5 2.4 constant_dynamic-update-slice_fusion.7
  60.8 8.4 %collective-permute-done = bf16[256,2048]{1,0:T(8,128)(2,1)} collective-permute-done((bf16[256,2048]{1,0:T(8,128)(2,1)}, bf16[256,2048]{1,0:T(8,128)(2,1)}, u32[]{:S(2)}, u32[]{:S(2)}) %collective-permute-start) | collective-permute-done | bytes 1048608 | tf_op jit(solution)/shard_map/ppermute | solution.py:240
  69.2 2.0 collective-permute-start.5
  71.2 2.3 constant_dynamic-update-slice_fusion.6
  73.6 20.9 %collective-permute-done.1 = bf16[256,2048]{1,0:T(8,128)(2,1)} collective-permute-done((bf16[256,2048]{1,0:T(8,128)(2,1)}, bf16[256,2048]{1,0:T(8,128)(2,1)}, u32[]{:S(2)}, u32[]{:S(2)}) %collective-permute-start.1) | collective-permute-done | bytes 1048608 | tf_op jit(solution)/shard_map/ppermute | solution.py:240
  94.4 2.3 constant_dynamic-update-slice_fusion.5
  96.8 17.4 %collective-permute-done.2 = bf16[256,2048]{1,0:T(8,128)(2,1)} collective-permute-done((bf16[256,2048]{1,0:T(8,128)(2,1)}, bf16[256,2048]{1,0:T(8,128)(2,1)}, u32[]{:S(2)}, u32[]{:S(2)}) %collective-permute-start.2) | collective-permute-done | bytes 1048608 | tf_op jit(solution)/shard_map/ppermute | solution.py:240
  114.2 2.4 constant_dynamic-update-slice_fusion.4
  116.5 23.0 %collective-permute-done.3 = bf16[256,2048]{1,0:T(8,128)(2,1)} collective-permute-done((bf16[256,2048]{1,0:T(8,128)(2,1)}, bf16[256,2048]{1,0:T(8,128)(2,1)}, u32[]{:S(2)}, u32[]{:S(2)}) %collective-permute-start.3) | collective-permute-done | bytes 1048608 | tf_op jit(solution)/shard_map/ppermute | solution.py:240
  139.5 2.3 constant_dynamic-update-slice_fusion.3
  141.8 2.3 constant_dynamic-update-slice_fusion.2
  144.2 13.2 %all-gather.2.cloned.1.call-done.k_ref.v_ref = bf16[8192,1024]{1,0:T(8,128)(2,1)} async-done(((bf16[512,1024]{1,0:T(8,128)(2,1)}), bf16[8192,1024]{1,0:T(8,128)(2,1)}) %all-gather.2.cloned.1.call-update) | async-done | bytes 16777232 | tf_op jit(solution)/shard_map/all_gather | solution.py:229
  157.4 36.7 %shard_map.119 = bf16[512,512]{1,0:T(8,128)(2,1)} custom-call(s32[3]{0:T(128)} %pad_add_fusion.scalars, bf16[512,512]{1,0:T(8,128)(2,1)} %reshape.109.q_ref, bf16[8192,1024]{1,0:T(8,128)(2,1)} %all-gather.2.cloned.1.call-done.k_ref.v_ref, bf16[8192,1024]{1,0:T(8,128)(2,1)} %all-gather.2.cloned.1.call-done.k_ref.v_ref), custom_call_target="tpu_custom_call" | custom-call | flops 8589934592 | bytes 17825792 | tf_op jit(solution)/shard_map/pallas_call | solution.py:91
  194.1 1.2 reshape.111
  196.2 5.1 %all-to-all-start = ((bf16[8,64,2,256]{3,1,2,0:T(8,128)(2,1)}), bf16[8,64,2,256]{3,1,2,0:T(8,128)(2,1)}, u32[]{:S(2)}, u32[]{:S(2)}) async-start(bf16[8,64,2,256]{3,1,2,0:T(8,128)(2,1)} %copy.18), calls=%async_computation | async-start | bytes 1048576 | tf_op jit(solution)/shard_map/all_to_all | solution.py:245
  201.3 2.3 constant_dynamic-update-slice_fusion.1
  203.6 2.4 constant_dynamic-update-slice_fusion
  206.1 4.8 %all-to-all-done = bf16[8,64,2,256]{3,1,2,0:T(8,128)(2,1)} async-done(((bf16[8,64,2,256]{3,1,2,0:T(8,128)(2,1)}), bf16[8,64,2,256]{3,1,2,0:T(8,128)(2,1)}, u32[]{:S(2)}, u32[]{:S(2)}) %all-to-all-start) | async-done | bytes 524320 | tf_op jit(solution)/shard_map/all_to_all | solution.py:245
  210.9 2.4 gather_fusion
  213.3 1.2 select_bitcast_fusion
  214.9 4.8 %multiply_reduce_fusion = (f32[128]{0:T(128)S(1)}, f32[128,2048]{1,0:T(8,128)S(1)}) fusion(bf16[128,2048]{1,0:T(8,128)(2,1)S(1)} %bitcast.46, bf16[2048,2048]{1,0:T(8,128)(2,1)} %constant_dynamic-update-slice_fusion, bf16[128,2048]{1,0:T(8,128)(2,1)S(1)} %copy-done.2), kind=kOutput, calls=%fused_computation.23 | convolution fusion | flops 1074790272 | bytes 10486272 | tf_op jit(solution)/shard_map/dot_general | solution.py:250
  220.7 1.5 convolution_convert_fusion.1
  222.2 2.5 all_to_all.20
  224.7 25.6 %all_to_all.29 = bf16[128,2,2048]{2,1,0:T(2,128)(2,1)} all-to-all(bf16[128,2,2048]{2,1,0:T(2,128)(2,1)} %all_to_all.20), channel_id=1, replica_groups=mesh['expert'=16,'head'=8] {'expert','head'}, dimensions={0} | all-to-all | bytes 2097152 | tf_op jit(solution)/shard_map/all_to_all | solution.py:275
  250.3 2.2 all_to_all.22
  252.5 1.2 collective-permute-start.7
  253.7 1.3 constant_dynamic-update-slice_fusion.9
  255.0 1.2 collective-permute-done.7
  256.3 1.3 copy-done.3
  257.6 2.8 fusion.13
  260.5 7.6 %convolution_convert_fusion = bf16[512,2048]{1,0:T(8,128)(2,1)} fusion(bf16[1,704,2048]{2,1,0:T(8,128)(2,1)S(1)} %copy-done, f32[704,512]{1,0:T(8,128)} %fusion.13, bf16[512,2048]{1,0:T(8,128)(2,1)} %copy-done.3, bf16[1,704,2048]{2,1,0:T(8,128)(2,1)} %param.19), kind=kOutput, calls=%fused_computation.1 | convolution fusion | flops 2956001280 | bytes 11403264 | tf_op jit(solution)/shard_map/dot_general | solution.py:188
  268.1 1.3 slice.11
  269.9 2.3 collective-permute-done.8
  272.1 2.6 add_convert_fusion
  274.7 2.5 all_to_all.23
  277.3 24.1 %all_to_all.30 = bf16[128,2,2048]{2,1,0:T(2,128)(2,1)} all-to-all(bf16[128,2,2048]{2,1,0:T(2,128)(2,1)} %all_to_all.23), channel_id=1, replica_groups=mesh['expert'=16,'head'=8] {'expert','head'}, dimensions={0} | all-to-all | bytes 2097152 | tf_op jit(solution)/shard_map/all_to_all | solution.py:283
  301.4 2.2 all_to_all.25
  303.6 1.9 fusion.5
  305.5 1.1 reshape.113
  (40 shorter events, 6.2 us)
Async XLA Ops:
  6.5 253.9 %copy-start = (bf16[1,704,2048]{2,1,0:T(8,128)(2,1)S(1)}, bf16[1,704,2048]{2,1,0:T(8,128)(2,1)}, u32[]{:S(2)}) copy-start(bf16[1,704,2048]{2,1,0:T(8,128)(2,1)} %param.20) | copy-start | bytes 8650756
  6.5 150.9 %all-gather.2.cloned.1.call-start = ((), (), s32[]{:S(2)}) async-start(), calls=%async_computation.3 | async-start | bytes 17825792 | tf_op jit(solution)/shard_map/all_gather | solution.py:229
  46.2 12.8 %copy-start.5 = (s32[64,2]{0,1:T(2,128)S(1)}, s32[64,2]{0,1:T(2,128)}, u32[]{:S(2)}) copy-start(s32[64,2]{0,1:T(2,128)} %param.23) | copy-start | bytes 1540
  46.2 12.8 %copy-start.6 = (s32[64,2]{0,1:T(2,128)S(1)}, s32[64,2]{0,1:T(2,128)}, u32[]{:S(2)}) copy-start(s32[64,2]{0,1:T(2,128)} %param.22) | copy-start | bytes 1540
  46.2 12.8 %copy-start.8 = (s32[2]{0:T(128)S(1)}, s32[2]{0:T(128)}, u32[]{:S(2)}) copy-start(s32[2]{0:T(128)} %param.21) | copy-start | bytes 28
  46.2 23.0 %collective-permute-start = (bf16[256,2048]{1,0:T(8,128)(2,1)}, bf16[256,2048]{1,0:T(8,128)(2,1)}, u32[]{:S(2)}, u32[]{:S(2)}) collective-permute-start(bf16[256,2048]{1,0:T(8,128)(2,1)} %param.16), channel_id=1, source_target_pairs={{0,1},{1,2},{2,3},{3,4},{4,5},{5,6},{6,7},{7,0},{8,9},{9,10},{10,1... | collective-permute-start | bytes 3145736 | tf_op jit(solution)/shard_map/ppermute | solution.py:240
  46.9 47.5 %collective-permute-start.1 = (bf16[256,2048]{1,0:T(8,128)(2,1)}, bf16[256,2048]{1,0:T(8,128)(2,1)}, u32[]{:S(2)}, u32[]{:S(2)}) collective-permute-start(bf16[256,2048]{1,0:T(8,128)(2,1)} %param.16), channel_id=1, source_target_pairs={{0,2},{1,3},{2,4},{3,5},{4,6},{5,7},{6,0},{7,1},{8,10},{9,11},{10,... | collective-permute-start | bytes 3145736 | tf_op jit(solution)/shard_map/ppermute | solution.py:240
  47.7 66.5 %collective-permute-start.2 = (bf16[256,2048]{1,0:T(8,128)(2,1)}, bf16[256,2048]{1,0:T(8,128)(2,1)}, u32[]{:S(2)}, u32[]{:S(2)}) collective-permute-start(bf16[256,2048]{1,0:T(8,128)(2,1)} %param.16), channel_id=1, source_target_pairs={{0,3},{1,4},{2,5},{3,6},{4,7},{5,0},{6,1},{7,2},{8,11},{9,12},{10,... | collective-permute-start | bytes 3145736 | tf_op jit(solution)/shard_map/ppermute | solution.py:240
  49.4 90.1 %collective-permute-start.3 = (bf16[256,2048]{1,0:T(8,128)(2,1)}, bf16[256,2048]{1,0:T(8,128)(2,1)}, u32[]{:S(2)}, u32[]{:S(2)}) collective-permute-start(bf16[256,2048]{1,0:T(8,128)(2,1)} %param.16), channel_id=1, source_target_pairs={{0,4},{1,5},{2,6},{3,7},{4,0},{5,1},{6,2},{7,3},{8,12},{9,13},{10,... | collective-permute-start | bytes 3145736 | tf_op jit(solution)/shard_map/ppermute | solution.py:240
  50.6 91.3 %collective-permute-start.4 = (bf16[256,2048]{1,0:T(8,128)(2,1)}, bf16[256,2048]{1,0:T(8,128)(2,1)}, u32[]{:S(2)}, u32[]{:S(2)}) collective-permute-start(bf16[256,2048]{1,0:T(8,128)(2,1)} %param.16), channel_id=1, source_target_pairs={{0,5},{1,6},{2,7},{3,0},{4,1},{5,2},{6,3},{7,4},{8,13},{9,14},{10,... | collective-permute-start | bytes 3145736 | tf_op jit(solution)/shard_map/ppermute | solution.py:240
  56.5 4.1 %copy-start.4 = (bf16[2048]{0:T(1024)(128)(2,1)S(1)}, bf16[2048]{0:T(1024)(128)(2,1)}, u32[]{:S(2)}) copy-start(bf16[2048]{0:T(1024)(128)(2,1)} %param.17) | copy-start | bytes 12292
  69.2 132.1 %collective-permute-start.5 = (bf16[256,2048]{1,0:T(8,128)(2,1)}, bf16[256,2048]{1,0:T(8,128)(2,1)}, u32[]{:S(2)}, u32[]{:S(2)}) collective-permute-start(bf16[256,2048]{1,0:T(8,128)(2,1)} %param.16), channel_id=1, source_target_pairs={{0,6},{1,7},{2,0},{3,1},{4,2},{5,3},{6,4},{7,5},{8,14},{9,15},{10,... | collective-permute-start | bytes 3145736 | tf_op jit(solution)/shard_map/ppermute | solution.py:240
  94.4 109.2 %collective-permute-start.6 = (bf16[256,2048]{1,0:T(8,128)(2,1)}, bf16[256,2048]{1,0:T(8,128)(2,1)}, u32[]{:S(2)}, u32[]{:S(2)}) collective-permute-start(bf16[256,2048]{1,0:T(8,128)(2,1)} %param.16), channel_id=1, source_target_pairs={{0,7},{1,0},{2,1},{3,2},{4,3},{5,4},{6,5},{7,6},{8,15},{9,8},{10,9... | collective-permute-start | bytes 3145736 | tf_op jit(solution)/shard_map/ppermute | solution.py:240
  196.2 14.7 %all-to-all-start = ((bf16[8,64,2,256]{3,1,2,0:T(8,128)(2,1)}), bf16[8,64,2,256]{3,1,2,0:T(8,128)(2,1)}, u32[]{:S(2)}, u32[]{:S(2)}) async-start(bf16[8,64,2,256]{3,1,2,0:T(8,128)(2,1)} %copy.18), calls=%async_computation | async-start | bytes 1048576 | tf_op jit(solution)/shard_map/all_to_all | solution.py:245
  203.6 11.3 %copy-start.2 = (bf16[128,2048]{1,0:T(8,128)(2,1)S(1)}, bf16[128,2048]{1,0:T(8,128)(2,1)}, u32[]{:S(2)}) copy-start(bf16[128,2048]{1,0:T(8,128)(2,1)} %reshape.106.x_ref) | copy-start | bytes 1572868
  219.7 1.0 copy-start.1
  252.5 5.1 %copy-start.7 = (bf16[1,704,2048]{2,1,0:T(8,128)(2,1)S(1)}, bf16[1,704,2048]{2,1,0:T(8,128)(2,1)}, u32[]{:S(2)}) copy-start(bf16[1,704,2048]{2,1,0:T(8,128)(2,1)} %param.18) | copy-start | bytes 8650756
  252.5 3.7 %collective-permute-start.7 = (bf16[256,2048]{1,0:T(8,128)(2,1)}, bf16[256,2048]{1,0:T(8,128)(2,1)S(1)}, u32[]{:S(2)}, u32[]{:S(2)}) collective-permute-start(bf16[256,2048]{1,0:T(8,128)(2,1)} %all_to_all.22), channel_id=1, source_target_pairs={{0,1},{1,0},{2,3},{3,2},{4,5},{5,4},{6,7},{7,6},{8,9},{9,8},{10,11... | collective-permute-start | bytes 3145736 | tf_op jit(solution)/shard_map/ppermute | solution.py:277
  256.3 1.3 copy-start.3
  269.4 2.7 collective-permute-start.8
Sparse Core Ops, SparseCore 0:
  46.3 111.0 all-gather.1

commit v14 on v13

--- a/solution.py
+++ b/solution.py
@@ -104,7 +104,7 @@
 
 
 MESH_ID = pl.DeviceIdType.MESH
-GATHER_PARTS = 2
+GATHER_PARTS = 4
 
 
 def head_gather_body(x_ref, out_ref, send_sem, recv_sem, local_sem, *, size, parts):

time: 315 us -> 308 us (0.978)
  Pallas kernels: 63.4 us -> 56.7 us
    pallas_call x1, Pallas kernels: 36.7 us -> 30 us  [flash_attention(): pl.pallas_call(functools.partial(flash_body, scale=scale, key_block=key_b...]
  transfers between devices with their start and end apart: 11 -> 11, of which waited for: 8 -> 8; matrix products, arithmetic and copies ran while one was open for 9% -> 9% of each run, Pallas kernels for 12% -> 10%
where the time goes in v14:
time: 308 us; the launch traced here: 307 us
  waiting for transfers between devices  91.3 us (30%)
  Pallas kernels  56.7 us (18%)
  blocking collectives  49.7 us (16%)
  local copies, waits for them, and re-layouts  47.3 us (15%)
  matrix products  28.6 us (9%)
  starting transfers between devices  15.1 us (5%)
  between operations  13.6 us (4%)
  other arithmetic  4.41 us (1%)
    ppermute x7, waiting for transfers between devices, shards(): lax.ppermute(w_out, 'head', [(index, (index + shift) % head_size) for ind...  70 us
    pallas_call x1, Pallas kernels, flash_attention(): pl.pallas_call(functools.partial(flash_body, scale=scale, key_block=key_b...  30 us
    pallas_call x1, Pallas kernels, head_gather(): pl.pallas_call(functools.partial(head_gather_body, size=size, parts=GATHE...  26.7 us
    all_to_all x1, blocking collectives, shards(): received = lax.all_to_all(send_rows, ('expert', 'head'), 0, 0, tiled=True)  25.6 us
    all_to_all x1, blocking collectives, shards(): lax.all_to_all(summed_halves, ('expert', 'head'), 0, 0, tiled=True)  24.1 us
    unnamed x27, local copies, waits for them, and re-layouts  20.1 us
    all_gather x1, waiting for transfers between devices, shards(): kv_all = lax.all_gather(kv_rows, 'expert', axis=0, tiled=True)  13 us
    ppermute x7, starting transfers between devices, shards(): lax.ppermute(w_out, 'head', [(index, (index + shift) % head_size) for ind...  8.36 us
  transfers between devices with their start and end apart: 11, of which 8 were waited for; matrix products, arithmetic and copies ran while one was open for 9% of the time, Pallas kernels for 10%

profile of v14, /device:TPU:1, one launch (start us, length us, event | category | flops | bytes accessed | tf_op | source)
XLA Modules:
  0.0 306.7 jit_solution(1885626996299503855)
XLA Ops:
  6.5 2.2 reshape.106.x_ref
  8.7 26.7 %shard_map.118 = bf16[8,128,2048]{2,1,0:T(8,128)(2,1)} custom-call(bf16[128,2048]{1,0:T(8,128)(2,1)} %reshape.106.x_ref), custom_call_target="tpu_custom_call" | custom-call | tf_op jit(solution)/shard_map/pallas_call | solution.py:167
  35.4 6.2 %fusion.19 = bf16[1024,512]{0,1:T(8,128)(2,1)} fusion(bf16[1024,2048]{1,0:T(8,128)(2,1)} %bitcast.44, bf16[2048,256]{1,0:T(8,128)(2,1)} %param.15, bf16[2048,256]{1,0:T(8,128)(2,1)} %param.14), kind=kOutput, calls=%fused_computation.20 | convolution fusion | flops 2152202240 | bytes 7340032 | tf_op jit(solution)/shard_map/dot_general | solution.py:225
  41.6 2.3 copy.17
  43.9 2.3 reshape.110
  47.1 2.4 collective-permute-start.2
  49.5 1.2 collective-permute-start.3
  50.7 2.0 collective-permute-start.4
  52.7 3.7 %convolution_convert_fusion.2 = bf16[1024,256]{1,0:T(8,128)(2,1)S(1)} fusion(bf16[1024,2048]{1,0:T(8,128)(2,1)} %bitcast.45, bf16[2048,256]{1,0:T(8,128)(2,1)} %param.13), kind=kOutput, calls=%fused_computation.21 | convolution fusion | flops 1074003968 | bytes 5767168 | tf_op jit(solution)/shard_map/dot_general | solution.py:219
  56.5 2.4 constant_dynamic-update-slice_fusion.7
  60.8 8.5 %collective-permute-done = bf16[256,2048]{1,0:T(8,128)(2,1)} collective-permute-done((bf16[256,2048]{1,0:T(8,128)(2,1)}, bf16[256,2048]{1,0:T(8,128)(2,1)}, u32[]{:S(2)}, u32[]{:S(2)}) %collective-permute-start) | collective-permute-done | bytes 1048608 | tf_op jit(solution)/shard_map/ppermute | solution.py:240
  69.3 1.9 collective-permute-start.5
  71.2 2.3 constant_dynamic-update-slice_fusion.6
  73.5 20.9 %collective-permute-done.1 = bf16[256,2048]{1,0:T(8,128)(2,1)} collective-permute-done((bf16[256,2048]{1,0:T(8,128)(2,1)}, bf16[256,2048]{1,0:T(8,128)(2,1)}, u32[]{:S(2)}, u32[]{:S(2)}) %collective-permute-start.1) | collective-permute-done | bytes 1048608 | tf_op jit(solution)/shard_map/ppermute | solution.py:240
  94.4 2.3 constant_dynamic-update-slice_fusion.5
  96.7 17.5 %collective-permute-done.2 = bf16[256,2048]{1,0:T(8,128)(2,1)} collective-permute-done((bf16[256,2048]{1,0:T(8,128)(2,1)}, bf16[256,2048]{1,0:T(8,128)(2,1)}, u32[]{:S(2)}, u32[]{:S(2)}) %collective-permute-start.2) | collective-permute-done | bytes 1048608 | tf_op jit(solution)/shard_map/ppermute | solution.py:240
  114.3 2.4 constant_dynamic-update-slice_fusion.4
  116.6 23.0 %collective-permute-done.3 = bf16[256,2048]{1,0:T(8,128)(2,1)} collective-permute-done((bf16[256,2048]{1,0:T(8,128)(2,1)}, bf16[256,2048]{1,0:T(8,128)(2,1)}, u32[]{:S(2)}, u32[]{:S(2)}) %collective-permute-start.3) | collective-permute-done | bytes 1048608 | tf_op jit(solution)/shard_map/ppermute | solution.py:240
  139.7 2.3 constant_dynamic-update-slice_fusion.3
  142.0 2.3 constant_dynamic-update-slice_fusion.2
  144.3 13.0 %all-gather.2.cloned.1.call-done.k_ref.v_ref = bf16[8192,1024]{1,0:T(8,128)(2,1)} async-done(((bf16[512,1024]{1,0:T(8,128)(2,1)}), bf16[8192,1024]{1,0:T(8,128)(2,1)}) %all-gather.2.cloned.1.call-update) | async-done | bytes 16777232 | tf_op jit(solution)/shard_map/all_gather | solution.py:229
  157.3 30.0 %shard_map.119 = bf16[512,512]{1,0:T(8,128)(2,1)} custom-call(s32[3]{0:T(128)} %pad_add_fusion.scalars, bf16[512,512]{1,0:T(8,128)(2,1)} %reshape.109.q_ref, bf16[8192,1024]{1,0:T(8,128)(2,1)} %all-gather.2.cloned.1.call-done.k_ref.v_ref, bf16[8192,1024]{1,0:T(8,128)(2,1)} %all-gather.2.cloned.1.call-done.k_ref.v_ref), custom_call_target="tpu_custom_call" | custom-call | flops 8589934592 | bytes 17825792 | tf_op jit(solution)/shard_map/pallas_call | solution.py:91
  187.3 1.2 reshape.111
  189.3 5.1 %all-to-all-start = ((bf16[8,64,2,256]{3,1,2,0:T(8,128)(2,1)}), bf16[8,64,2,256]{3,1,2,0:T(8,128)(2,1)}, u32[]{:S(2)}, u32[]{:S(2)}) async-start(bf16[8,64,2,256]{3,1,2,0:T(8,128)(2,1)} %copy.18), calls=%async_computation | async-start | bytes 1048576 | tf_op jit(solution)/shard_map/all_to_all | solution.py:245
  194.5 2.3 constant_dynamic-update-slice_fusion.1
  196.8 2.4 constant_dynamic-update-slice_fusion
  199.2 4.8 %all-to-all-done = bf16[8,64,2,256]{3,1,2,0:T(8,128)(2,1)} async-done(((bf16[8,64,2,256]{3,1,2,0:T(8,128)(2,1)}), bf16[8,64,2,256]{3,1,2,0:T(8,128)(2,1)}, u32[]{:S(2)}, u32[]{:S(2)}) %all-to-all-start) | async-done | bytes 524320 | tf_op jit(solution)/shard_map/all_to_all | solution.py:245
  204.1 2.4 gather_fusion
  206.5 1.2 select_bitcast_fusion
  208.1 4.8 %multiply_reduce_fusion = (f32[128]{0:T(128)S(1)}, f32[128,2048]{1,0:T(8,128)S(1)}) fusion(bf16[128,2048]{1,0:T(8,128)(2,1)S(1)} %bitcast.46, bf16[2048,2048]{1,0:T(8,128)(2,1)} %constant_dynamic-update-slice_fusion, bf16[128,2048]{1,0:T(8,128)(2,1)S(1)} %copy-done.2), kind=kOutput, calls=%fused_computation.23 | convolution fusion | flops 1074790272 | bytes 10486272 | tf_op jit(solution)/shard_map/dot_general | solution.py:250
  213.9 1.5 convolution_convert_fusion.1
  215.4 2.5 all_to_all.20
  217.9 25.6 %all_to_all.29 = bf16[128,2,2048]{2,1,0:T(2,128)(2,1)} all-to-all(bf16[128,2,2048]{2,1,0:T(2,128)(2,1)} %all_to_all.20), channel_id=1, replica_groups=mesh['expert'=16,'head'=8] {'expert','head'}, dimensions={0} | all-to-all | bytes 2097152 | tf_op jit(solution)/shard_map/all_to_all | solution.py:275
  243.5 2.2 all_to_all.22
  245.7 1.2 collective-permute-start.7
  246.9 1.3 constant_dynamic-update-slice_fusion.9
  248.2 1.2 collective-permute-done.7
  249.5 1.3 copy-done.3
  250.8 2.8 fusion.13
  253.6 7.6 %convolution_convert_fusion = bf16[512,2048]{1,0:T(8,128)(2,1)} fusion(bf16[1,704,2048]{2,1,0:T(8,128)(2,1)S(1)} %copy-done, f32[704,512]{1,0:T(8,128)} %fusion.13, bf16[512,2048]{1,0:T(8,128)(2,1)} %copy-done.3, bf16[1,704,2048]{2,1,0:T(8,128)(2,1)} %param.19), kind=kOutput, calls=%fused_computation.1 | convolution fusion | flops 2956001280 | bytes 11403264 | tf_op jit(solution)/shard_map/dot_general | solution.py:188
  261.3 1.3 slice.11
  263.0 2.3 collective-permute-done.8
  265.3 2.6 add_convert_fusion
  267.9 2.5 all_to_all.23
  270.4 24.1 %all_to_all.30 = bf16[128,2,2048]{2,1,0:T(2,128)(2,1)} all-to-all(bf16[128,2,2048]{2,1,0:T(2,128)(2,1)} %all_to_all.23), channel_id=1, replica_groups=mesh['expert'=16,'head'=8] {'expert','head'}, dimensions={0} | all-to-all | bytes 2097152 | tf_op jit(solution)/shard_map/all_to_all | solution.py:283
  294.6 2.2 all_to_all.25
  296.8 1.9 fusion.5
  298.7 1.1 reshape.113
  (40 shorter events, 5.7 us)
Async XLA Ops:
  6.5 247.1 %copy-start = (bf16[1,704,2048]{2,1,0:T(8,128)(2,1)S(1)}, bf16[1,704,2048]{2,1,0:T(8,128)(2,1)}, u32[]{:S(2)}) copy-start(bf16[1,704,2048]{2,1,0:T(8,128)(2,1)} %param.20) | copy-start | bytes 8650756
  6.5 150.7 %all-gather.2.cloned.1.call-start = ((), (), s32[]{:S(2)}) async-start(), calls=%async_computation.3 | async-start | bytes 17825792 | tf_op jit(solution)/shard_map/all_gather | solution.py:229
  46.2 12.8 %copy-start.5 = (s32[64,2]{0,1:T(2,128)S(1)}, s32[64,2]{0,1:T(2,128)}, u32[]{:S(2)}) copy-start(s32[64,2]{0,1:T(2,128)} %param.23) | copy-start | bytes 1540
  46.2 12.7 %copy-start.6 = (s32[64,2]{0,1:T(2,128)S(1)}, s32[64,2]{0,1:T(2,128)}, u32[]{:S(2)}) copy-start(s32[64,2]{0,1:T(2,128)} %param.22) | copy-start | bytes 1540
  46.2 12.7 %copy-start.8 = (s32[2]{0:T(128)S(1)}, s32[2]{0:T(128)}, u32[]{:S(2)}) copy-start(s32[2]{0:T(128)} %param.21) | copy-start | bytes 28
  46.2 23.1 %collective-permute-start = (bf16[256,2048]{1,0:T(8,128)(2,1)}, bf16[256,2048]{1,0:T(8,128)(2,1)}, u32[]{:S(2)}, u32[]{:S(2)}) collective-permute-start(bf16[256,2048]{1,0:T(8,128)(2,1)} %param.16), channel_id=1, source_target_pairs={{0,1},{1,2},{2,3},{3,4},{4,5},{5,6},{6,7},{7,0},{8,9},{9,10},{10,1... | collective-permute-start | bytes 3145736 | tf_op jit(solution)/shard_map/ppermute | solution.py:240
  47.0 47.4 %collective-permute-start.1 = (bf16[256,2048]{1,0:T(8,128)(2,1)}, bf16[256,2048]{1,0:T(8,128)(2,1)}, u32[]{:S(2)}, u32[]{:S(2)}) collective-permute-start(bf16[256,2048]{1,0:T(8,128)(2,1)} %param.16), channel_id=1, source_target_pairs={{0,2},{1,3},{2,4},{3,5},{4,6},{5,7},{6,0},{7,1},{8,10},{9,11},{10,... | collective-permute-start | bytes 3145736 | tf_op jit(solution)/shard_map/ppermute | solution.py:240
  47.1 67.2 %collective-permute-start.2 = (bf16[256,2048]{1,0:T(8,128)(2,1)}, bf16[256,2048]{1,0:T(8,128)(2,1)}, u32[]{:S(2)}, u32[]{:S(2)}) collective-permute-start(bf16[256,2048]{1,0:T(8,128)(2,1)} %param.16), channel_id=1, source_target_pairs={{0,3},{1,4},{2,5},{3,6},{4,7},{5,0},{6,1},{7,2},{8,11},{9,12},{10,... | collective-permute-start | bytes 3145736 | tf_op jit(solution)/shard_map/ppermute | solution.py:240
  49.5 90.2 %collective-permute-start.3 = (bf16[256,2048]{1,0:T(8,128)(2,1)}, bf16[256,2048]{1,0:T(8,128)(2,1)}, u32[]{:S(2)}, u32[]{:S(2)}) collective-permute-start(bf16[256,2048]{1,0:T(8,128)(2,1)} %param.16), channel_id=1, source_target_pairs={{0,4},{1,5},{2,6},{3,7},{4,0},{5,1},{6,2},{7,3},{8,12},{9,13},{10,... | collective-permute-start | bytes 3145736 | tf_op jit(solution)/shard_map/ppermute | solution.py:240
  50.7 91.3 %collective-permute-start.4 = (bf16[256,2048]{1,0:T(8,128)(2,1)}, bf16[256,2048]{1,0:T(8,128)(2,1)}, u32[]{:S(2)}, u32[]{:S(2)}) collective-permute-start(bf16[256,2048]{1,0:T(8,128)(2,1)} %param.16), channel_id=1, source_target_pairs={{0,5},{1,6},{2,7},{3,0},{4,1},{5,2},{6,3},{7,4},{8,13},{9,14},{10,... | collective-permute-start | bytes 3145736 | tf_op jit(solution)/shard_map/ppermute | solution.py:240
  56.4 4.1 %copy-start.4 = (bf16[2048]{0:T(1024)(128)(2,1)S(1)}, bf16[2048]{0:T(1024)(128)(2,1)}, u32[]{:S(2)}) copy-start(bf16[2048]{0:T(1024)(128)(2,1)} %param.17) | copy-start | bytes 12292
  69.3 125.2 %collective-permute-start.5 = (bf16[256,2048]{1,0:T(8,128)(2,1)}, bf16[256,2048]{1,0:T(8,128)(2,1)}, u32[]{:S(2)}, u32[]{:S(2)}) collective-permute-start(bf16[256,2048]{1,0:T(8,128)(2,1)} %param.16), channel_id=1, source_target_pairs={{0,6},{1,7},{2,0},{3,1},{4,2},{5,3},{6,4},{7,5},{8,14},{9,15},{10,... | collective-permute-start | bytes 3145736 | tf_op jit(solution)/shard_map/ppermute | solution.py:240
  94.4 102.4 %collective-permute-start.6 = (bf16[256,2048]{1,0:T(8,128)(2,1)}, bf16[256,2048]{1,0:T(8,128)(2,1)}, u32[]{:S(2)}, u32[]{:S(2)}) collective-permute-start(bf16[256,2048]{1,0:T(8,128)(2,1)} %param.16), channel_id=1, source_target_pairs={{0,7},{1,0},{2,1},{3,2},{4,3},{5,4},{6,5},{7,6},{8,15},{9,8},{10,9... | collective-permute-start | bytes 3145736 | tf_op jit(solution)/shard_map/ppermute | solution.py:240
  189.3 14.7 %all-to-all-start = ((bf16[8,64,2,256]{3,1,2,0:T(8,128)(2,1)}), bf16[8,64,2,256]{3,1,2,0:T(8,128)(2,1)}, u32[]{:S(2)}, u32[]{:S(2)}) async-start(bf16[8,64,2,256]{3,1,2,0:T(8,128)(2,1)} %copy.18), calls=%async_computation | async-start | bytes 1048576 | tf_op jit(solution)/shard_map/all_to_all | solution.py:245
  196.8 11.3 %copy-start.2 = (bf16[128,2048]{1,0:T(8,128)(2,1)S(1)}, bf16[128,2048]{1,0:T(8,128)(2,1)}, u32[]{:S(2)}) copy-start(bf16[128,2048]{1,0:T(8,128)(2,1)} %reshape.106.x_ref) | copy-start | bytes 1572868
  212.9 1.0 copy-start.1
  245.7 5.1 %copy-start.7 = (bf16[1,704,2048]{2,1,0:T(8,128)(2,1)S(1)}, bf16[1,704,2048]{2,1,0:T(8,128)(2,1)}, u32[]{:S(2)}) copy-start(bf16[1,704,2048]{2,1,0:T(8,128)(2,1)} %param.18) | copy-start | bytes 8650756
  245.7 3.7 %collective-permute-start.7 = (bf16[256,2048]{1,0:T(8,128)(2,1)}, bf16[256,2048]{1,0:T(8,128)(2,1)S(1)}, u32[]{:S(2)}, u32[]{:S(2)}) collective-permute-start(bf16[256,2048]{1,0:T(8,128)(2,1)} %all_to_all.22), channel_id=1, source_target_pairs={{0,1},{1,0},{2,3},{3,2},{4,5},{5,4},{6,7},{7,6},{8,9},{9,8},{10,11... | collective-permute-start | bytes 3145736 | tf_op jit(solution)/shard_map/ppermute | solution.py:277
  249.5 1.3 copy-start.3
  262.6 2.7 collective-permute-start.8
Sparse Core Ops, SparseCore 0:
  46.3 110.9 all-gather.1

commit v15 on v13

--- a/solution.py
+++ b/solution.py
@@ -28,7 +28,7 @@
 
     def update(masked):
         q = q_ref[...]
-        k = k_ref[...]
+        k = k_ref[...].reshape(-1, DH)
         scores = lax.dot_general(
             q, k, (((1,), (1,)), ((), ())), preferred_element_type=jnp.float32
         ) * scale
@@ -41,7 +41,7 @@
         p = jnp.exp(scores - m_new[:, :1])
         l_ref[...] = alpha * l_ref[...] + jnp.sum(p, axis=1, keepdims=True)
         acc_ref[...] = acc_ref[...] * alpha + jnp.dot(
-            p.astype(jnp.bfloat16), v_ref[...], preferred_element_type=jnp.float32
+            p.astype(jnp.bfloat16), v_ref[...].reshape(-1, DH), preferred_element_type=jnp.float32
         )
         m_ref[...] = m_new
 
@@ -61,9 +61,10 @@
 
 
 def flash_attention(scalars, q_all, kv_all, heads, scale):
-    rows = q_all.shape[0]
-    keys = kv_all.shape[0]
+    rows = q_all.shape[1]
+    keys = kv_all.shape[0] * kv_all.shape[2]
     tables = scalars.shape[0] - 1
+    per_block = KEY_BLOCK // kv_all.shape[2]
     key_block = KEY_BLOCK
     nk = keys // key_block
 
@@ -74,10 +75,14 @@
         num_scalar_prefetch=1,
         grid=(tables, heads, nk),
         in_specs=[
-            pl.BlockSpec((rows, DH), lambda s, h, j, sc: (0, s * heads + h)),
-            pl.BlockSpec((key_block, DH), lambda s, h, j, sc: (clamp(j, sc, s), s * 2 * heads + h)),
+            pl.BlockSpec((pl.squeezed, rows, DH), lambda s, h, j, sc: (s, 0, h)),
             pl.BlockSpec(
-                (key_block, DH), lambda s, h, j, sc: (clamp(j, sc, s), s * 2 * heads + heads + h)
+                (per_block, pl.squeezed, kv_all.shape[2], DH),
+                lambda s, h, j, sc: (clamp(j, sc, s), s, 0, h),
+            ),
+            pl.BlockSpec(
+                (per_block, pl.squeezed, kv_all.shape[2], DH),
+                lambda s, h, j, sc: (clamp(j, sc, s), s, 0, heads + h),
             ),
         ],
         out_specs=pl.BlockSpec((rows, DH), lambda s, h, j, sc: (0, s * heads + h)),
@@ -117,12 +122,12 @@
     ahead = ((z + chips + step) % chips) * 2 + core
     behind = ((z + chips - step) % chips) * 2 + core
     far = ((z + 2) % chips) * 2 + core
-    rows = x_ref.shape[0] // parts
+    rows = x_ref.shape[1] // parts
 
     def remote(src, slot, part, sem, device):
         piece = pl.ds(part * rows, rows)
         return pltpu.make_async_remote_copy(
-            src.at[piece], out_ref.at[slot, piece], send_sem.at[sem * parts + part],
+            src.at[:, piece], out_ref.at[:, slot, piece], send_sem.at[sem * parts + part],
             recv_sem.at[slot * parts + part], device_id={"head": device}, device_id_type=MESH_ID,
         )
 
@@ -131,7 +136,7 @@
         pl.semaphore_signal(barrier, 1, device_id={"head": device}, device_id_type=MESH_ID)
     pl.semaphore_wait(barrier, 3)
 
-    local = pltpu.make_async_copy(x_ref, out_ref.at[me], local_sem)
+    local = pltpu.make_async_copy(x_ref, out_ref.at[:, me], local_sem)
     local.start()
     sent = []
     for part in range(parts):
@@ -142,17 +147,17 @@
     for part in range(parts):
         remote(x_ref, behind, part, 0, behind).wait_recv()
         for sem, device in ((3, ahead), (4, partner)):
-            copy = remote(out_ref.at[behind], behind, part, sem, device)
+            copy = remote(out_ref.at[:, behind], behind, part, sem, device)
             copy.start()
             sent.append(copy)
     for part in range(parts):
         remote(x_ref, ahead, part, 0, ahead).wait_recv()
-        copy = remote(out_ref.at[ahead], ahead, part, 5, partner)
+        copy = remote(out_ref.at[:, ahead], ahead, part, 5, partner)
         copy.start()
         sent.append(copy)
     for part in range(parts):
         remote(x_ref, far, part, 0, behind).wait_recv()
-        copy = remote(out_ref.at[far], far, part, 6, partner)
+        copy = remote(out_ref.at[:, far], far, part, 6, partner)
         copy.start()
         sent.append(copy)
     for j in range(chips):
@@ -166,7 +171,7 @@
 def head_gather(x, size):
     return pl.pallas_call(
         functools.partial(head_gather_body, size=size, parts=GATHER_PARTS),
-        out_shape=jax.ShapeDtypeStruct((size,) + x.shape, x.dtype),
+        out_shape=jax.ShapeDtypeStruct((x.shape[0], size) + x.shape[1:], x.dtype),
         in_specs=[pl.BlockSpec(memory_space=pltpu.VMEM)],
         out_specs=pl.BlockSpec(memory_space=pl.ANY),
         scratch_shapes=[
@@ -211,22 +216,17 @@
     score_scale = 1.0 / math.sqrt(DH)
     cells_flat = table_cells.reshape(cell_count * tables, model_width)
     head_size = lax.axis_size("head")
-    flat_rows = head_gather(cells_flat, head_size).reshape(
-        head_size * cells_flat.shape[0], model_width
-    )
-    row_cells = flat_rows.shape[0] // tables
-    q_all = (
-        jnp.dot(flat_rows, w_query, preferred_element_type=jnp.float32)
-        .astype(jnp.bfloat16)
-        .reshape(row_cells, tables * head_width)
-    )
+    by_table = head_gather(table_cells.transpose(1, 0, 2), head_size)
+    row_cells = head_size * cell_count
+    by_table = by_table.reshape(tables, row_cells, model_width)
+    q_all = jnp.einsum(
+        "tcd,dk->tck", by_table, w_query, preferred_element_type=jnp.float32
+    ).astype(jnp.bfloat16)
     kv_weight = jnp.concatenate([w_key, w_value], axis=1)
-    kv_rows = (
-        jnp.dot(flat_rows, kv_weight, preferred_element_type=jnp.float32)
-        .astype(jnp.bfloat16)
-        .reshape(row_cells, tables * 2 * head_width)
-    )
-    kv_all = lax.all_gather(kv_rows, "expert", axis=0, tiled=True)
+    kv_rows = jnp.einsum(
+        "tcd,dk->tck", by_table, kv_weight, preferred_element_type=jnp.float32
+    ).astype(jnp.bfloat16)
+    kv_all = lax.all_gather(kv_rows, "expert", axis=0, tiled=False)
     offset = lax.axis_index("expert") * row_cells
     scalars = jnp.concatenate(
         [lengths.astype(jnp.int32), jnp.reshape(offset, (1,)).astype(jnp.int32)]

time: 315 us -> 309 us (0.981)
  Pallas kernels: 63.4 us -> 56.8 us
    unnamed x27 -> x32, local copies, waits for them, and re-layouts: 20.1 us -> 26.8 us
    pallas_call x1, Pallas kernels: 36.7 us -> 30.1 us  [flash_attention(): pl.pallas_call(functools.partial(flash_body, scale=scale, key_block=key_b...]
    reshape x3 -> x0, local copies, waits for them, and re-layouts: 5.43 us -> none  [the longest x1 2.28 us: shards(): kv_rows = jnp.dot(flat_rows, kv_weight, preferred_element_type=jnp.float3...]
  transfers between devices with their start and end apart: 11 -> 11, of which waited for: 8 -> 8; matrix products, arithmetic and copies ran while one was open for 9% -> 9% of each run, Pallas kernels for 12% -> 10%
where the time goes in v15:
time: 309 us; the launch traced here: 308 us
  waiting for transfers between devices  90.4 us (29%)
  Pallas kernels  56.8 us (18%)
  blocking collectives  49.7 us (16%)
  local copies, waits for them, and re-layouts  48.6 us (16%)
  matrix products  29.4 us (10%)
  starting transfers between devices  15.3 us (5%)
  between operations  13.6 us (4%)
  other arithmetic  4.45 us (1%)
    ppermute x7, waiting for transfers between devices, shards(): lax.ppermute(w_out, 'head', [(index, (index + shift) % head_size) for ind...  68.9 us
    pallas_call x1, Pallas kernels, flash_attention(): pl.pallas_call(functools.partial(flash_body, scale=scale, key_block=key_b...  30.1 us
    unnamed x32, local copies, waits for them, and re-layouts  26.8 us
    pallas_call x1, Pallas kernels, head_gather(): pl.pallas_call(functools.partial(head_gather_body, size=size, parts=GATHE...  26.7 us
    all_to_all x1, blocking collectives, shards(): received = lax.all_to_all(send_rows, ('expert', 'head'), 0, 0, tiled=True)  25.6 us
    all_to_all x1, blocking collectives, shards(): lax.all_to_all(summed_halves, ('expert', 'head'), 0, 0, tiled=True)  24.1 us
    all_gather x1, waiting for transfers between devices, shards(): kv_all = lax.all_gather(kv_rows, 'expert', axis=0, tiled=False)  13.2 us
    ppermute x7, starting transfers between devices, shards(): lax.ppermute(w_out, 'head', [(index, (index + shift) % head_size) for ind...  8.51 us
  transfers between devices with their start and end apart: 11, of which 8 were waited for; matrix products, arithmetic and copies ran while one was open for 9% of the time, Pallas kernels for 10%

profile of v15, /device:TPU:1, one launch (start us, length us, event | category | flops | bytes accessed | tf_op | source)
XLA Modules:
  0.0 308.2 jit_solution(2712076370746520319)
XLA Ops:
  6.5 2.1 copy.39
  8.7 26.7 %shard_map.118 = bf16[2,8,64,2048]{3,2,1,0:T(8,128)(2,1)} custom-call(bf16[2,64,2048]{2,1,0:T(8,128)(2,1)} %bitcast.62), custom_call_target="tpu_custom_call" | custom-call | tf_op jit(solution)/shard_map/pallas_call | solution.py:172
  35.4 2.3 copy.32
  37.7 2.3 copy.31
  39.9 6.2 %fusion.16 = bf16[2,512,512]{1,2,0:T(8,128)(2,1)} fusion(bf16[2,512,2048]{2,1,0:T(8,128)(2,1)} %bitcast.59, bf16[2048,256]{0,1:T(8,128)(2,1)} %copy.32, bf16[2048,256]{0,1:T(8,128)(2,1)} %copy.31), kind=kOutput, calls=%fused_computation.20 | convolution fusion | flops 2152202240 | bytes 7340032 | tf_op jit(solution)/shard_map/tcd,dk->tck/dot_general | solution.py:226
  46.1 2.3 copy.33
  50.0 1.7 collective-permute-start.2
  51.7 1.1 collective-permute-start.3
  52.8 2.2 collective-permute-start.4
  55.0 4.5 %convolution_convert_fusion.2.q_ref = bf16[2,512,256]{2,1,0:T(8,128)(2,1)} fusion(bf16[2,512,2048]{2,1,0:T(8,128)(2,1)} %bitcast.60, bf16[2048,256]{1,0:T(8,128)(2,1)} %param.13), kind=kOutput, calls=%fused_computation.21 | convolution fusion | flops 1074003968 | bytes 5767168 | tf_op jit(solution)/shard_map/tcd,dk->tck/dot_general | solution.py:222
  59.6 2.4 constant_dynamic-update-slice_fusion.7
  63.9 7.6 %collective-permute-done = bf16[256,2048]{1,0:T(8,128)(2,1)} collective-permute-done((bf16[256,2048]{1,0:T(8,128)(2,1)}, bf16[256,2048]{1,0:T(8,128)(2,1)}, u32[]{:S(2)}, u32[]{:S(2)}) %collective-permute-start) | collective-permute-done | bytes 1048608 | tf_op jit(solution)/shard_map/ppermute | solution.py:240
  71.5 2.0 collective-permute-start.5
  73.5 2.3 constant_dynamic-update-slice_fusion.6
  75.8 20.9 %collective-permute-done.1 = bf16[256,2048]{1,0:T(8,128)(2,1)} collective-permute-done((bf16[256,2048]{1,0:T(8,128)(2,1)}, bf16[256,2048]{1,0:T(8,128)(2,1)}, u32[]{:S(2)}, u32[]{:S(2)}) %collective-permute-start.1) | collective-permute-done | bytes 1048608 | tf_op jit(solution)/shard_map/ppermute | solution.py:240
  96.7 2.3 constant_dynamic-update-slice_fusion.5
  99.1 17.4 %collective-permute-done.2 = bf16[256,2048]{1,0:T(8,128)(2,1)} collective-permute-done((bf16[256,2048]{1,0:T(8,128)(2,1)}, bf16[256,2048]{1,0:T(8,128)(2,1)}, u32[]{:S(2)}, u32[]{:S(2)}) %collective-permute-start.2) | collective-permute-done | bytes 1048608 | tf_op jit(solution)/shard_map/ppermute | solution.py:240
  116.5 2.4 constant_dynamic-update-slice_fusion.4
  118.8 23.0 %collective-permute-done.3 = bf16[256,2048]{1,0:T(8,128)(2,1)} collective-permute-done((bf16[256,2048]{1,0:T(8,128)(2,1)}, bf16[256,2048]{1,0:T(8,128)(2,1)}, u32[]{:S(2)}, u32[]{:S(2)}) %collective-permute-start.3) | collective-permute-done | bytes 1048608 | tf_op jit(solution)/shard_map/ppermute | solution.py:240
  141.8 2.3 constant_dynamic-update-slice_fusion.3
  144.1 2.3 constant_dynamic-update-slice_fusion.2
  146.5 13.2 %all-gather.3.cloned.1.call-done = bf16[32,512,512]{2,1,0:T(8,128)(2,1)} async-done(((bf16[2,512,512]{2,1,0:T(8,128)(2,1)}), bf16[32,512,512]{2,1,0:T(8,128)(2,1)}) %all-gather.3.cloned.1.call-update) | async-done | bytes 16777232 | tf_op jit(solution)/shard_map/all_gather | solution.py:229
  159.7 30.1 %shard_map.119 = bf16[512,512]{1,0:T(8,128)(2,1)} custom-call(s32[3]{0:T(128)} %pad_add_fusion.scalars, bf16[2,512,256]{2,1,0:T(8,128)(2,1)} %convolution_convert_fusion.2.q_ref, bf16[16,2,512,512]{3,2,1,0:T(8,128)(2,1)} %bitcast.57, bf16[16,2,512,512]{3,2,1,0:T(8,128)(2,1)} %bitcast.58), custom_call_target="tpu_custom_call" | custom-call | flops 8589934592 | bytes 17825792 | tf_op jit(solution)/shard_map/pallas_call | solution.py:96
  189.8 1.2 reshape.102
  191.9 5.1 %all-to-all-start = ((bf16[8,64,2,256]{3,1,2,0:T(8,128)(2,1)}), bf16[8,64,2,256]{3,1,2,0:T(8,128)(2,1)S(1)}, u32[]{:S(2)}, u32[]{:S(2)}) async-start(bf16[8,64,2,256]{3,1,2,0:T(8,128)(2,1)} %copy.34), calls=%async_computation | async-start | bytes 1048576 | tf_op jit(solution)/shard_map/all_to_all | solution.py:245
  197.0 2.3 constant_dynamic-update-slice_fusion.1
  199.3 2.4 constant_dynamic-update-slice_fusion
  201.7 4.8 %all-to-all-done = bf16[8,64,2,256]{3,1,2,0:T(8,128)(2,1)S(1)} async-done(((bf16[8,64,2,256]{3,1,2,0:T(8,128)(2,1)}), bf16[8,64,2,256]{3,1,2,0:T(8,128)(2,1)S(1)}, u32[]{:S(2)}, u32[]{:S(2)}) %all-to-all-start) | async-done | bytes 524320 | tf_op jit(solution)/shard_map/all_to_all | solution.py:245
  206.5 1.4 gather_fusion
  207.8 1.2 select_bitcast_fusion
  209.5 4.8 %multiply_reduce_fusion = (f32[128]{0:T(128)S(1)}, f32[128,2048]{1,0:T(8,128)S(1)}) fusion(f32[128,2048]{1,0:T(8,128)S(1)} %copy-done.2, bf16[128,2048]{1,0:T(8,128)(2,1)S(1)} %bitcast.61, bf16[2048,2048]{1,0:T(8,128)(2,1)} %constant_dynamic-update-slice_fusion), kind=kOutput, calls=%fused_computation.24 | convolution fusion | flops 1074528128 | bytes 11010560 | tf_op jit(solution)/shard_map/dot_general | solution.py:250
  215.3 1.5 convolution_convert_fusion.1
  216.8 2.5 all_to_all.20
  219.4 25.6 %all_to_all.29 = bf16[128,2,2048]{2,1,0:T(2,128)(2,1)} all-to-all(bf16[128,2,2048]{2,1,0:T(2,128)(2,1)} %all_to_all.20), channel_id=1, replica_groups=mesh['expert'=16,'head'=8] {'expert','head'}, dimensions={0} | all-to-all | bytes 2097152 | tf_op jit(solution)/shard_map/all_to_all | solution.py:275
  245.0 2.2 all_to_all.22
  247.2 1.2 collective-permute-start.7
  248.4 1.3 constant_dynamic-update-slice_fusion.9
  249.7 1.2 collective-permute-done.7
  251.0 1.3 copy-done.4
  252.3 2.8 fusion.10
  255.1 7.6 %convolution_convert_fusion = bf16[512,2048]{1,0:T(8,128)(2,1)} fusion(bf16[1,704,2048]{2,1,0:T(8,128)(2,1)S(1)} %copy-done, f32[704,512]{1,0:T(8,128)} %fusion.10, bf16[512,2048]{1,0:T(8,128)(2,1)} %copy-done.4, bf16[1,704,2048]{2,1,0:T(8,128)(2,1)} %param.19), kind=kOutput, calls=%fused_computation.1 | convolution fusion | flops 2956001280 | bytes 11403264 | tf_op jit(solution)/shard_map/dot_general | solution.py:193
  262.8 1.3 slice.11
  264.5 2.3 collective-permute-done.8
  266.8 2.6 add_convert_fusion
  269.4 2.5 all_to_all.23
  271.9 24.1 %all_to_all.30 = bf16[128,2,2048]{2,1,0:T(2,128)(2,1)} all-to-all(bf16[128,2,2048]{2,1,0:T(2,128)(2,1)} %all_to_all.23), channel_id=1, replica_groups=mesh['expert'=16,'head'=8] {'expert','head'}, dimensions={0} | all-to-all | bytes 2097152 | tf_op jit(solution)/shard_map/all_to_all | solution.py:283
  296.1 2.2 all_to_all.25
  298.3 1.9 fusion.5
  (43 shorter events, 7.5 us)
Async XLA Ops:
  6.5 248.6 %copy-start = (bf16[1,704,2048]{2,1,0:T(8,128)(2,1)S(1)}, bf16[1,704,2048]{2,1,0:T(8,128)(2,1)}, u32[]{:S(2)}) copy-start(bf16[1,704,2048]{2,1,0:T(8,128)(2,1)} %param.20) | copy-start | bytes 8650756
  6.5 153.1 %all-gather.3.cloned.1.call-start = ((), (), s32[]{:S(2)}) async-start(), calls=%async_computation.3 | async-start | bytes 17825792 | tf_op jit(solution)/shard_map/all_gather | solution.py:229
  48.5 13.5 %copy-start.6 = (s32[64,2]{0,1:T(2,128)S(1)}, s32[64,2]{0,1:T(2,128)}, u32[]{:S(2)}) copy-start(s32[64,2]{0,1:T(2,128)} %param.23) | copy-start | bytes 1540
  48.5 13.5 %copy-start.7 = (s32[64,2]{0,1:T(2,128)S(1)}, s32[64,2]{0,1:T(2,128)}, u32[]{:S(2)}) copy-start(s32[64,2]{0,1:T(2,128)} %param.22) | copy-start | bytes 1540
  48.5 13.5 %copy-start.9 = (s32[2]{0:T(128)S(1)}, s32[2]{0:T(128)}, u32[]{:S(2)}) copy-start(s32[2]{0:T(128)} %param.21) | copy-start | bytes 28
  48.5 14.0 %copy-start.3 = (bf16[64,2,2048]{2,1,0:T(2,128)(2,1)S(1)}, bf16[64,2,2048]{2,1,0:T(2,128)(2,1)}, u32[]{:S(2)}) copy-start(bf16[64,2,2048]{2,1,0:T(2,128)(2,1)} %param.12) | copy-start | bytes 1572868
  48.5 23.0 %collective-permute-start = (bf16[256,2048]{1,0:T(8,128)(2,1)}, bf16[256,2048]{1,0:T(8,128)(2,1)}, u32[]{:S(2)}, u32[]{:S(2)}) collective-permute-start(bf16[256,2048]{1,0:T(8,128)(2,1)} %param.16), channel_id=1, source_target_pairs={{0,1},{1,2},{2,3},{3,4},{4,5},{5,6},{6,7},{7,0},{8,9},{9,10},{10,1... | collective-permute-start | bytes 3145736 | tf_op jit(solution)/shard_map/ppermute | solution.py:240
  49.2 47.5 %collective-permute-start.1 = (bf16[256,2048]{1,0:T(8,128)(2,1)}, bf16[256,2048]{1,0:T(8,128)(2,1)}, u32[]{:S(2)}, u32[]{:S(2)}) collective-permute-start(bf16[256,2048]{1,0:T(8,128)(2,1)} %param.16), channel_id=1, source_target_pairs={{0,2},{1,3},{2,4},{3,5},{4,6},{5,7},{6,0},{7,1},{8,10},{9,11},{10,... | collective-permute-start | bytes 3145736 | tf_op jit(solution)/shard_map/ppermute | solution.py:240
  50.0 66.5 %collective-permute-start.2 = (bf16[256,2048]{1,0:T(8,128)(2,1)}, bf16[256,2048]{1,0:T(8,128)(2,1)}, u32[]{:S(2)}, u32[]{:S(2)}) collective-permute-start(bf16[256,2048]{1,0:T(8,128)(2,1)} %param.16), channel_id=1, source_target_pairs={{0,3},{1,4},{2,5},{3,6},{4,7},{5,0},{6,1},{7,2},{8,11},{9,12},{10,... | collective-permute-start | bytes 3145736 | tf_op jit(solution)/shard_map/ppermute | solution.py:240
  51.7 90.1 %collective-permute-start.3 = (bf16[256,2048]{1,0:T(8,128)(2,1)}, bf16[256,2048]{1,0:T(8,128)(2,1)}, u32[]{:S(2)}, u32[]{:S(2)}) collective-permute-start(bf16[256,2048]{1,0:T(8,128)(2,1)} %param.16), channel_id=1, source_target_pairs={{0,4},{1,5},{2,6},{3,7},{4,0},{5,1},{6,2},{7,3},{8,12},{9,13},{10,... | collective-permute-start | bytes 3145736 | tf_op jit(solution)/shard_map/ppermute | solution.py:240
  52.8 91.3 %collective-permute-start.4 = (bf16[256,2048]{1,0:T(8,128)(2,1)}, bf16[256,2048]{1,0:T(8,128)(2,1)}, u32[]{:S(2)}, u32[]{:S(2)}) collective-permute-start(bf16[256,2048]{1,0:T(8,128)(2,1)} %param.16), channel_id=1, source_target_pairs={{0,5},{1,6},{2,7},{3,0},{4,1},{5,2},{6,3},{7,4},{8,13},{9,14},{10,... | collective-permute-start | bytes 3145736 | tf_op jit(solution)/shard_map/ppermute | solution.py:240
  59.5 4.1 %copy-start.5 = (bf16[2048]{0:T(1024)(128)(2,1)S(1)}, bf16[2048]{0:T(1024)(128)(2,1)}, u32[]{:S(2)}) copy-start(bf16[2048]{0:T(1024)(128)(2,1)} %param.17) | copy-start | bytes 12292
  71.5 125.5 %collective-permute-start.5 = (bf16[256,2048]{1,0:T(8,128)(2,1)}, bf16[256,2048]{1,0:T(8,128)(2,1)}, u32[]{:S(2)}, u32[]{:S(2)}) collective-permute-start(bf16[256,2048]{1,0:T(8,128)(2,1)} %param.16), channel_id=1, source_target_pairs={{0,6},{1,7},{2,0},{3,1},{4,2},{5,3},{6,4},{7,5},{8,14},{9,15},{10,... | collective-permute-start | bytes 3145736 | tf_op jit(solution)/shard_map/ppermute | solution.py:240
  96.7 102.6 %collective-permute-start.6 = (bf16[256,2048]{1,0:T(8,128)(2,1)}, bf16[256,2048]{1,0:T(8,128)(2,1)}, u32[]{:S(2)}, u32[]{:S(2)}) collective-permute-start(bf16[256,2048]{1,0:T(8,128)(2,1)} %param.16), channel_id=1, source_target_pairs={{0,7},{1,0},{2,1},{3,2},{4,3},{5,4},{6,5},{7,6},{8,15},{9,8},{10,9... | collective-permute-start | bytes 3145736 | tf_op jit(solution)/shard_map/ppermute | solution.py:240
  191.9 14.6 %all-to-all-start = ((bf16[8,64,2,256]{3,1,2,0:T(8,128)(2,1)}), bf16[8,64,2,256]{3,1,2,0:T(8,128)(2,1)S(1)}, u32[]{:S(2)}, u32[]{:S(2)}) async-start(bf16[8,64,2,256]{3,1,2,0:T(8,128)(2,1)} %copy.34), calls=%async_computation | async-start | bytes 1048576 | tf_op jit(solution)/shard_map/all_to_all | solution.py:245
  207.8 1.7 copy-start.2
  214.4 1.0 copy-start.1
  247.2 5.1 %copy-start.8 = (bf16[1,704,2048]{2,1,0:T(8,128)(2,1)S(1)}, bf16[1,704,2048]{2,1,0:T(8,128)(2,1)}, u32[]{:S(2)}) copy-start(bf16[1,704,2048]{2,1,0:T(8,128)(2,1)} %param.18) | copy-start | bytes 8650756
  247.2 3.7 %collective-permute-start.7 = (bf16[256,2048]{1,0:T(8,128)(2,1)}, bf16[256,2048]{1,0:T(8,128)(2,1)S(1)}, u32[]{:S(2)}, u32[]{:S(2)}) collective-permute-start(bf16[256,2048]{1,0:T(8,128)(2,1)} %all_to_all.22), channel_id=1, source_target_pairs={{0,1},{1,0},{2,3},{3,2},{4,5},{5,4},{6,7},{7,6},{8,9},{9,8},{10,11... | collective-permute-start | bytes 3145736 | tf_op jit(solution)/shard_map/ppermute | solution.py:277
  251.0 1.3 copy-start.4
  264.1 2.7 collective-permute-start.8
Sparse Core Ops, SparseCore 0:
  48.6 111.0 all-gather.2

commit v16 on v13

--- a/solution.py
+++ b/solution.py
@@ -131,14 +131,14 @@
         pl.semaphore_signal(barrier, 1, device_id={"head": device}, device_id_type=MESH_ID)
     pl.semaphore_wait(barrier, 3)
 
-    local = pltpu.make_async_copy(x_ref, out_ref.at[me], local_sem)
-    local.start()
     sent = []
     for part in range(parts):
         for sem, device in ((0, ahead), (1, behind), (2, partner)):
             copy = remote(x_ref, me, part, sem, device)
             copy.start()
             sent.append(copy)
+    local = pltpu.make_async_copy(x_ref, out_ref.at[me], local_sem)
+    local.start()
     for part in range(parts):
         remote(x_ref, behind, part, 0, behind).wait_recv()
         for sem, device in ((3, ahead), (4, partner)):

time: 315 us -> 315 us (level)
  no operation moved by 1% of the time
where the time goes in v16:
time: 315 us; the launch traced here: 314 us
  waiting for transfers between devices  91.2 us (29%)
  Pallas kernels  63.4 us (20%)
  blocking collectives  49.7 us (16%)
  local copies, waits for them, and re-layouts  47.3 us (15%)
  matrix products  28.6 us (9%)
  starting transfers between devices  15.3 us (5%)
  between operations  13.6 us (4%)
  other arithmetic  4.41 us (1%)
    ppermute x7, waiting for transfers between devices, shards(): lax.ppermute(w_out, 'head', [(index, (index + shift) % head_size) for ind...  69.7 us
    pallas_call x1, Pallas kernels, flash_attention(): pl.pallas_call(functools.partial(flash_body, scale=scale, key_block=key_b...  36.7 us
    pallas_call x1, Pallas kernels, head_gather(): pl.pallas_call(functools.partial(head_gather_body, size=size, parts=GATHE...  26.7 us
    all_to_all x1, blocking collectives, shards(): received = lax.all_to_all(send_rows, ('expert', 'head'), 0, 0, tiled=True)  25.6 us
    all_to_all x1, blocking collectives, shards(): lax.all_to_all(summed_halves, ('expert', 'head'), 0, 0, tiled=True)  24.1 us
    unnamed x27, local copies, waits for them, and re-layouts  20.1 us
    all_gather x1, waiting for transfers between devices, shards(): kv_all = lax.all_gather(kv_rows, 'expert', axis=0, tiled=True)  13.2 us
    ppermute x7, starting transfers between devices, shards(): lax.ppermute(w_out, 'head', [(index, (index + shift) % head_size) for ind...  8.51 us
  transfers between devices with their start and end apart: 11, of which 8 were waited for; matrix products, arithmetic and copies ran while one was open for 9% of the time, Pallas kernels for 12%

profile of v16, /device:TPU:1, one launch (start us, length us, event | category | flops | bytes accessed | tf_op | source)
XLA Modules:
  0.0 313.5 jit_solution(7451405109151904950)
XLA Ops:
  6.5 2.2 reshape.106.x_ref
  8.7 26.7 %shard_map.118 = bf16[8,128,2048]{2,1,0:T(8,128)(2,1)} custom-call(bf16[128,2048]{1,0:T(8,128)(2,1)} %reshape.106.x_ref), custom_call_target="tpu_custom_call" | custom-call | tf_op jit(solution)/shard_map/pallas_call | solution.py:167
  35.4 6.2 %fusion.19 = bf16[1024,512]{0,1:T(8,128)(2,1)} fusion(bf16[1024,2048]{1,0:T(8,128)(2,1)} %bitcast.44, bf16[2048,256]{1,0:T(8,128)(2,1)} %param.15, bf16[2048,256]{1,0:T(8,128)(2,1)} %param.14), kind=kOutput, calls=%fused_computation.20 | convolution fusion | flops 2152202240 | bytes 7340032 | tf_op jit(solution)/shard_map/dot_general | solution.py:225
  41.6 2.3 copy.17
  43.9 2.3 reshape.110
  47.7 1.7 collective-permute-start.2
  49.4 1.2 collective-permute-start.3
  50.6 2.2 collective-permute-start.4
  52.7 3.7 %convolution_convert_fusion.2 = bf16[1024,256]{1,0:T(8,128)(2,1)S(1)} fusion(bf16[1024,2048]{1,0:T(8,128)(2,1)} %bitcast.45, bf16[2048,256]{1,0:T(8,128)(2,1)} %param.13), kind=kOutput, calls=%fused_computation.21 | convolution fusion | flops 1074003968 | bytes 5767168 | tf_op jit(solution)/shard_map/dot_general | solution.py:219
  56.5 2.4 constant_dynamic-update-slice_fusion.7
  60.8 8.4 %collective-permute-done = bf16[256,2048]{1,0:T(8,128)(2,1)} collective-permute-done((bf16[256,2048]{1,0:T(8,128)(2,1)}, bf16[256,2048]{1,0:T(8,128)(2,1)}, u32[]{:S(2)}, u32[]{:S(2)}) %collective-permute-start) | collective-permute-done | bytes 1048608 | tf_op jit(solution)/shard_map/ppermute | solution.py:240
  69.2 2.0 collective-permute-start.5
  71.2 2.3 constant_dynamic-update-slice_fusion.6
  73.6 20.9 %collective-permute-done.1 = bf16[256,2048]{1,0:T(8,128)(2,1)} collective-permute-done((bf16[256,2048]{1,0:T(8,128)(2,1)}, bf16[256,2048]{1,0:T(8,128)(2,1)}, u32[]{:S(2)}, u32[]{:S(2)}) %collective-permute-start.1) | collective-permute-done | bytes 1048608 | tf_op jit(solution)/shard_map/ppermute | solution.py:240
  94.4 2.3 constant_dynamic-update-slice_fusion.5
  96.8 17.4 %collective-permute-done.2 = bf16[256,2048]{1,0:T(8,128)(2,1)} collective-permute-done((bf16[256,2048]{1,0:T(8,128)(2,1)}, bf16[256,2048]{1,0:T(8,128)(2,1)}, u32[]{:S(2)}, u32[]{:S(2)}) %collective-permute-start.2) | collective-permute-done | bytes 1048608 | tf_op jit(solution)/shard_map/ppermute | solution.py:240
  114.2 2.4 constant_dynamic-update-slice_fusion.4
  116.5 23.0 %collective-permute-done.3 = bf16[256,2048]{1,0:T(8,128)(2,1)} collective-permute-done((bf16[256,2048]{1,0:T(8,128)(2,1)}, bf16[256,2048]{1,0:T(8,128)(2,1)}, u32[]{:S(2)}, u32[]{:S(2)}) %collective-permute-start.3) | collective-permute-done | bytes 1048608 | tf_op jit(solution)/shard_map/ppermute | solution.py:240
  139.5 2.3 constant_dynamic-update-slice_fusion.3
  141.8 2.3 constant_dynamic-update-slice_fusion.2
  144.2 13.2 %all-gather.2.cloned.1.call-done.k_ref.v_ref = bf16[8192,1024]{1,0:T(8,128)(2,1)} async-done(((bf16[512,1024]{1,0:T(8,128)(2,1)}), bf16[8192,1024]{1,0:T(8,128)(2,1)}) %all-gather.2.cloned.1.call-update) | async-done | bytes 16777232 | tf_op jit(solution)/shard_map/all_gather | solution.py:229
  157.4 36.7 %shard_map.119 = bf16[512,512]{1,0:T(8,128)(2,1)} custom-call(s32[3]{0:T(128)} %pad_add_fusion.scalars, bf16[512,512]{1,0:T(8,128)(2,1)} %reshape.109.q_ref, bf16[8192,1024]{1,0:T(8,128)(2,1)} %all-gather.2.cloned.1.call-done.k_ref.v_ref, bf16[8192,1024]{1,0:T(8,128)(2,1)} %all-gather.2.cloned.1.call-done.k_ref.v_ref), custom_call_target="tpu_custom_call" | custom-call | flops 8589934592 | bytes 17825792 | tf_op jit(solution)/shard_map/pallas_call | solution.py:91
  194.1 1.2 reshape.111
  196.2 5.1 %all-to-all-start = ((bf16[8,64,2,256]{3,1,2,0:T(8,128)(2,1)}), bf16[8,64,2,256]{3,1,2,0:T(8,128)(2,1)}, u32[]{:S(2)}, u32[]{:S(2)}) async-start(bf16[8,64,2,256]{3,1,2,0:T(8,128)(2,1)} %copy.18), calls=%async_computation | async-start | bytes 1048576 | tf_op jit(solution)/shard_map/all_to_all | solution.py:245
  201.3 2.3 constant_dynamic-update-slice_fusion.1
  203.6 2.4 constant_dynamic-update-slice_fusion
  206.1 4.8 %all-to-all-done = bf16[8,64,2,256]{3,1,2,0:T(8,128)(2,1)} async-done(((bf16[8,64,2,256]{3,1,2,0:T(8,128)(2,1)}), bf16[8,64,2,256]{3,1,2,0:T(8,128)(2,1)}, u32[]{:S(2)}, u32[]{:S(2)}) %all-to-all-start) | async-done | bytes 524320 | tf_op jit(solution)/shard_map/all_to_all | solution.py:245
  210.9 2.4 gather_fusion
  213.3 1.2 select_bitcast_fusion
  214.9 4.8 %multiply_reduce_fusion = (f32[128]{0:T(128)S(1)}, f32[128,2048]{1,0:T(8,128)S(1)}) fusion(bf16[128,2048]{1,0:T(8,128)(2,1)S(1)} %bitcast.46, bf16[2048,2048]{1,0:T(8,128)(2,1)} %constant_dynamic-update-slice_fusion, bf16[128,2048]{1,0:T(8,128)(2,1)S(1)} %copy-done.2), kind=kOutput, calls=%fused_computation.23 | convolution fusion | flops 1074790272 | bytes 10486272 | tf_op jit(solution)/shard_map/dot_general | solution.py:250
  220.7 1.5 convolution_convert_fusion.1
  222.2 2.5 all_to_all.20
  224.7 25.6 %all_to_all.29 = bf16[128,2,2048]{2,1,0:T(2,128)(2,1)} all-to-all(bf16[128,2,2048]{2,1,0:T(2,128)(2,1)} %all_to_all.20), channel_id=1, replica_groups=mesh['expert'=16,'head'=8] {'expert','head'}, dimensions={0} | all-to-all | bytes 2097152 | tf_op jit(solution)/shard_map/all_to_all | solution.py:275
  250.3 2.2 all_to_all.22
  252.5 1.2 collective-permute-start.7
  253.7 1.3 constant_dynamic-update-slice_fusion.9
  255.0 1.2 collective-permute-done.7
  256.3 1.3 copy-done.3
  257.6 2.8 fusion.13
  260.5 7.6 %convolution_convert_fusion = bf16[512,2048]{1,0:T(8,128)(2,1)} fusion(bf16[1,704,2048]{2,1,0:T(8,128)(2,1)S(1)} %copy-done, f32[704,512]{1,0:T(8,128)} %fusion.13, bf16[512,2048]{1,0:T(8,128)(2,1)} %copy-done.3, bf16[1,704,2048]{2,1,0:T(8,128)(2,1)} %param.19), kind=kOutput, calls=%fused_computation.1 | convolution fusion | flops 2956001280 | bytes 11403264 | tf_op jit(solution)/shard_map/dot_general | solution.py:188
  268.1 1.3 slice.11
  269.8 2.3 collective-permute-done.8
  272.1 2.6 add_convert_fusion
  274.7 2.5 all_to_all.23
  277.2 24.1 %all_to_all.30 = bf16[128,2,2048]{2,1,0:T(2,128)(2,1)} all-to-all(bf16[128,2,2048]{2,1,0:T(2,128)(2,1)} %all_to_all.23), channel_id=1, replica_groups=mesh['expert'=16,'head'=8] {'expert','head'}, dimensions={0} | all-to-all | bytes 2097152 | tf_op jit(solution)/shard_map/all_to_all | solution.py:283
  301.4 2.2 all_to_all.25
  303.6 1.9 fusion.5
  305.5 1.1 reshape.113
  (40 shorter events, 6.2 us)
Async XLA Ops:
  6.5 253.9 %copy-start = (bf16[1,704,2048]{2,1,0:T(8,128)(2,1)S(1)}, bf16[1,704,2048]{2,1,0:T(8,128)(2,1)}, u32[]{:S(2)}) copy-start(bf16[1,704,2048]{2,1,0:T(8,128)(2,1)} %param.20) | copy-start | bytes 8650756
  6.5 150.9 %all-gather.2.cloned.1.call-start = ((), (), s32[]{:S(2)}) async-start(), calls=%async_computation.3 | async-start | bytes 17825792 | tf_op jit(solution)/shard_map/all_gather | solution.py:229
  46.2 12.8 %copy-start.5 = (s32[64,2]{0,1:T(2,128)S(1)}, s32[64,2]{0,1:T(2,128)}, u32[]{:S(2)}) copy-start(s32[64,2]{0,1:T(2,128)} %param.23) | copy-start | bytes 1540
  46.2 12.8 %copy-start.6 = (s32[64,2]{0,1:T(2,128)S(1)}, s32[64,2]{0,1:T(2,128)}, u32[]{:S(2)}) copy-start(s32[64,2]{0,1:T(2,128)} %param.22) | copy-start | bytes 1540
  46.2 12.8 %copy-start.8 = (s32[2]{0:T(128)S(1)}, s32[2]{0:T(128)}, u32[]{:S(2)}) copy-start(s32[2]{0:T(128)} %param.21) | copy-start | bytes 28
  46.2 23.0 %collective-permute-start = (bf16[256,2048]{1,0:T(8,128)(2,1)}, bf16[256,2048]{1,0:T(8,128)(2,1)}, u32[]{:S(2)}, u32[]{:S(2)}) collective-permute-start(bf16[256,2048]{1,0:T(8,128)(2,1)} %param.16), channel_id=1, source_target_pairs={{0,1},{1,2},{2,3},{3,4},{4,5},{5,6},{6,7},{7,0},{8,9},{9,10},{10,1... | collective-permute-start | bytes 3145736 | tf_op jit(solution)/shard_map/ppermute | solution.py:240
  46.9 47.5 %collective-permute-start.1 = (bf16[256,2048]{1,0:T(8,128)(2,1)}, bf16[256,2048]{1,0:T(8,128)(2,1)}, u32[]{:S(2)}, u32[]{:S(2)}) collective-permute-start(bf16[256,2048]{1,0:T(8,128)(2,1)} %param.16), channel_id=1, source_target_pairs={{0,2},{1,3},{2,4},{3,5},{4,6},{5,7},{6,0},{7,1},{8,10},{9,11},{10,... | collective-permute-start | bytes 3145736 | tf_op jit(solution)/shard_map/ppermute | solution.py:240
  47.7 66.5 %collective-permute-start.2 = (bf16[256,2048]{1,0:T(8,128)(2,1)}, bf16[256,2048]{1,0:T(8,128)(2,1)}, u32[]{:S(2)}, u32[]{:S(2)}) collective-permute-start(bf16[256,2048]{1,0:T(8,128)(2,1)} %param.16), channel_id=1, source_target_pairs={{0,3},{1,4},{2,5},{3,6},{4,7},{5,0},{6,1},{7,2},{8,11},{9,12},{10,... | collective-permute-start | bytes 3145736 | tf_op jit(solution)/shard_map/ppermute | solution.py:240
  49.4 90.1 %collective-permute-start.3 = (bf16[256,2048]{1,0:T(8,128)(2,1)}, bf16[256,2048]{1,0:T(8,128)(2,1)}, u32[]{:S(2)}, u32[]{:S(2)}) collective-permute-start(bf16[256,2048]{1,0:T(8,128)(2,1)} %param.16), channel_id=1, source_target_pairs={{0,4},{1,5},{2,6},{3,7},{4,0},{5,1},{6,2},{7,3},{8,12},{9,13},{10,... | collective-permute-start | bytes 3145736 | tf_op jit(solution)/shard_map/ppermute | solution.py:240
  50.6 91.3 %collective-permute-start.4 = (bf16[256,2048]{1,0:T(8,128)(2,1)}, bf16[256,2048]{1,0:T(8,128)(2,1)}, u32[]{:S(2)}, u32[]{:S(2)}) collective-permute-start(bf16[256,2048]{1,0:T(8,128)(2,1)} %param.16), channel_id=1, source_target_pairs={{0,5},{1,6},{2,7},{3,0},{4,1},{5,2},{6,3},{7,4},{8,13},{9,14},{10,... | collective-permute-start | bytes 3145736 | tf_op jit(solution)/shard_map/ppermute | solution.py:240
  56.5 4.1 %copy-start.4 = (bf16[2048]{0:T(1024)(128)(2,1)S(1)}, bf16[2048]{0:T(1024)(128)(2,1)}, u32[]{:S(2)}) copy-start(bf16[2048]{0:T(1024)(128)(2,1)} %param.17) | copy-start | bytes 12292
  69.2 132.1 %collective-permute-start.5 = (bf16[256,2048]{1,0:T(8,128)(2,1)}, bf16[256,2048]{1,0:T(8,128)(2,1)}, u32[]{:S(2)}, u32[]{:S(2)}) collective-permute-start(bf16[256,2048]{1,0:T(8,128)(2,1)} %param.16), channel_id=1, source_target_pairs={{0,6},{1,7},{2,0},{3,1},{4,2},{5,3},{6,4},{7,5},{8,14},{9,15},{10,... | collective-permute-start | bytes 3145736 | tf_op jit(solution)/shard_map/ppermute | solution.py:240
  94.4 109.2 %collective-permute-start.6 = (bf16[256,2048]{1,0:T(8,128)(2,1)}, bf16[256,2048]{1,0:T(8,128)(2,1)}, u32[]{:S(2)}, u32[]{:S(2)}) collective-permute-start(bf16[256,2048]{1,0:T(8,128)(2,1)} %param.16), channel_id=1, source_target_pairs={{0,7},{1,0},{2,1},{3,2},{4,3},{5,4},{6,5},{7,6},{8,15},{9,8},{10,9... | collective-permute-start | bytes 3145736 | tf_op jit(solution)/shard_map/ppermute | solution.py:240
  196.2 14.7 %all-to-all-start = ((bf16[8,64,2,256]{3,1,2,0:T(8,128)(2,1)}), bf16[8,64,2,256]{3,1,2,0:T(8,128)(2,1)}, u32[]{:S(2)}, u32[]{:S(2)}) async-start(bf16[8,64,2,256]{3,1,2,0:T(8,128)(2,1)} %copy.18), calls=%async_computation | async-start | bytes 1048576 | tf_op jit(solution)/shard_map/all_to_all | solution.py:245
  203.6 11.3 %copy-start.2 = (bf16[128,2048]{1,0:T(8,128)(2,1)S(1)}, bf16[128,2048]{1,0:T(8,128)(2,1)}, u32[]{:S(2)}) copy-start(bf16[128,2048]{1,0:T(8,128)(2,1)} %reshape.106.x_ref) | copy-start | bytes 1572868
  219.7 1.0 copy-start.1
  252.5 5.1 %copy-start.7 = (bf16[1,704,2048]{2,1,0:T(8,128)(2,1)S(1)}, bf16[1,704,2048]{2,1,0:T(8,128)(2,1)}, u32[]{:S(2)}) copy-start(bf16[1,704,2048]{2,1,0:T(8,128)(2,1)} %param.18) | copy-start | bytes 8650756
  252.5 3.7 %collective-permute-start.7 = (bf16[256,2048]{1,0:T(8,128)(2,1)}, bf16[256,2048]{1,0:T(8,128)(2,1)S(1)}, u32[]{:S(2)}, u32[]{:S(2)}) collective-permute-start(bf16[256,2048]{1,0:T(8,128)(2,1)} %all_to_all.22), channel_id=1, source_target_pairs={{0,1},{1,0},{2,3},{3,2},{4,5},{5,4},{6,7},{7,6},{8,9},{9,8},{10,11... | collective-permute-start | bytes 3145736 | tf_op jit(solution)/shard_map/ppermute | solution.py:277
  256.3 1.3 copy-start.3
  269.4 2.7 collective-permute-start.8
Sparse Core Ops, SparseCore 0:
  46.3 111.0 all-gather.1

commit v17 on v13

--- a/solution.py
+++ b/solution.py
@@ -134,8 +134,8 @@
     local = pltpu.make_async_copy(x_ref, out_ref.at[me], local_sem)
     local.start()
     sent = []
-    for part in range(parts):
-        for sem, device in ((0, ahead), (1, behind), (2, partner)):
+    for sem, device in ((0, ahead), (1, behind), (2, partner)):
+        for part in range(parts):
             copy = remote(x_ref, me, part, sem, device)
             copy.start()
             sent.append(copy)

time: 315 us -> 312 us (level)
  Pallas kernels: 63.4 us -> 58.1 us
    pallas_call x1, Pallas kernels: 36.7 us -> 31.4 us  [flash_attention(): pl.pallas_call(functools.partial(flash_body, scale=scale, key_block=key_b...]
  transfers between devices with their start and end apart: 11 -> 11, of which waited for: 8 -> 8; matrix products, arithmetic and copies ran while one was open for 9% -> 9% of each run, Pallas kernels for 12% -> 10%
where the time goes in v17:
time: 312 us; the launch traced here: 308 us
  waiting for transfers between devices  91.2 us (29%)
  Pallas kernels  58.1 us (19%)
  blocking collectives  49.7 us (16%)
  local copies, waits for them, and re-layouts  47.3 us (15%)
  matrix products  28.6 us (9%)
  starting transfers between devices  15.3 us (5%)
  between operations  13.6 us (4%)
  other arithmetic  4.41 us (1%)
    ppermute x7, waiting for transfers between devices, shards(): lax.ppermute(w_out, 'head', [(index, (index + shift) % head_size) for ind...  69.7 us
    pallas_call x1, Pallas kernels, flash_attention(): pl.pallas_call(functools.partial(flash_body, scale=scale, key_block=key_b...  31.4 us
    pallas_call x1, Pallas kernels, head_gather(): pl.pallas_call(functools.partial(head_gather_body, size=size, parts=GATHE...  26.7 us
    all_to_all x1, blocking collectives, shards(): received = lax.all_to_all(send_rows, ('expert', 'head'), 0, 0, tiled=True)  25.6 us
    all_to_all x1, blocking collectives, shards(): lax.all_to_all(summed_halves, ('expert', 'head'), 0, 0, tiled=True)  24.1 us
    unnamed x27, local copies, waits for them, and re-layouts  20.1 us
    all_gather x1, waiting for transfers between devices, shards(): kv_all = lax.all_gather(kv_rows, 'expert', axis=0, tiled=True)  13.2 us
    ppermute x7, starting transfers between devices, shards(): lax.ppermute(w_out, 'head', [(index, (index + shift) % head_size) for ind...  8.5 us
  transfers between devices with their start and end apart: 11, of which 8 were waited for; matrix products, arithmetic and copies ran while one was open for 9% of the time, Pallas kernels for 10%

profile of v17, /device:TPU:1, one launch (start us, length us, event | category | flops | bytes accessed | tf_op | source)
XLA Modules:
  0.0 308.2 jit_solution(7680962051394545692)
XLA Ops:
  6.5 2.2 reshape.106.x_ref
  8.7 26.7 %shard_map.118 = bf16[8,128,2048]{2,1,0:T(8,128)(2,1)} custom-call(bf16[128,2048]{1,0:T(8,128)(2,1)} %reshape.106.x_ref), custom_call_target="tpu_custom_call" | custom-call | tf_op jit(solution)/shard_map/pallas_call | solution.py:167
  35.4 6.2 %fusion.19 = bf16[1024,512]{0,1:T(8,128)(2,1)} fusion(bf16[1024,2048]{1,0:T(8,128)(2,1)} %bitcast.44, bf16[2048,256]{1,0:T(8,128)(2,1)} %param.15, bf16[2048,256]{1,0:T(8,128)(2,1)} %param.14), kind=kOutput, calls=%fused_computation.20 | convolution fusion | flops 2152202240 | bytes 7340032 | tf_op jit(solution)/shard_map/dot_general | solution.py:225
  41.6 2.3 copy.17
  43.9 2.3 reshape.110
  47.7 1.7 collective-permute-start.2
  49.4 1.2 collective-permute-start.3
  50.6 2.2 collective-permute-start.4
  52.7 3.7 %convolution_convert_fusion.2 = bf16[1024,256]{1,0:T(8,128)(2,1)S(1)} fusion(bf16[1024,2048]{1,0:T(8,128)(2,1)} %bitcast.45, bf16[2048,256]{1,0:T(8,128)(2,1)} %param.13), kind=kOutput, calls=%fused_computation.21 | convolution fusion | flops 1074003968 | bytes 5767168 | tf_op jit(solution)/shard_map/dot_general | solution.py:219
  56.5 2.4 constant_dynamic-update-slice_fusion.7
  60.8 8.4 %collective-permute-done = bf16[256,2048]{1,0:T(8,128)(2,1)} collective-permute-done((bf16[256,2048]{1,0:T(8,128)(2,1)}, bf16[256,2048]{1,0:T(8,128)(2,1)}, u32[]{:S(2)}, u32[]{:S(2)}) %collective-permute-start) | collective-permute-done | bytes 1048608 | tf_op jit(solution)/shard_map/ppermute | solution.py:240
  69.2 2.0 collective-permute-start.5
  71.2 2.3 constant_dynamic-update-slice_fusion.6
  73.6 20.9 %collective-permute-done.1 = bf16[256,2048]{1,0:T(8,128)(2,1)} collective-permute-done((bf16[256,2048]{1,0:T(8,128)(2,1)}, bf16[256,2048]{1,0:T(8,128)(2,1)}, u32[]{:S(2)}, u32[]{:S(2)}) %collective-permute-start.1) | collective-permute-done | bytes 1048608 | tf_op jit(solution)/shard_map/ppermute | solution.py:240
  94.4 2.3 constant_dynamic-update-slice_fusion.5
  96.8 17.4 %collective-permute-done.2 = bf16[256,2048]{1,0:T(8,128)(2,1)} collective-permute-done((bf16[256,2048]{1,0:T(8,128)(2,1)}, bf16[256,2048]{1,0:T(8,128)(2,1)}, u32[]{:S(2)}, u32[]{:S(2)}) %collective-permute-start.2) | collective-permute-done | bytes 1048608 | tf_op jit(solution)/shard_map/ppermute | solution.py:240
  114.2 2.4 constant_dynamic-update-slice_fusion.4
  116.5 23.0 %collective-permute-done.3 = bf16[256,2048]{1,0:T(8,128)(2,1)} collective-permute-done((bf16[256,2048]{1,0:T(8,128)(2,1)}, bf16[256,2048]{1,0:T(8,128)(2,1)}, u32[]{:S(2)}, u32[]{:S(2)}) %collective-permute-start.3) | collective-permute-done | bytes 1048608 | tf_op jit(solution)/shard_map/ppermute | solution.py:240
  139.5 2.3 constant_dynamic-update-slice_fusion.3
  141.8 2.3 constant_dynamic-update-slice_fusion.2
  144.2 13.2 %all-gather.2.cloned.1.call-done.k_ref.v_ref = bf16[8192,1024]{1,0:T(8,128)(2,1)} async-done(((bf16[512,1024]{1,0:T(8,128)(2,1)}), bf16[8192,1024]{1,0:T(8,128)(2,1)}) %all-gather.2.cloned.1.call-update) | async-done | bytes 16777232 | tf_op jit(solution)/shard_map/all_gather | solution.py:229
  157.4 31.4 %shard_map.119 = bf16[512,512]{1,0:T(8,128)(2,1)} custom-call(s32[3]{0:T(128)} %pad_add_fusion.scalars, bf16[512,512]{1,0:T(8,128)(2,1)} %reshape.109.q_ref, bf16[8192,1024]{1,0:T(8,128)(2,1)} %all-gather.2.cloned.1.call-done.k_ref.v_ref, bf16[8192,1024]{1,0:T(8,128)(2,1)} %all-gather.2.cloned.1.call-done.k_ref.v_ref), custom_call_target="tpu_custom_call" | custom-call | flops 8589934592 | bytes 17825792 | tf_op jit(solution)/shard_map/pallas_call | solution.py:91
  188.8 1.2 reshape.111
  190.9 5.1 %all-to-all-start = ((bf16[8,64,2,256]{3,1,2,0:T(8,128)(2,1)}), bf16[8,64,2,256]{3,1,2,0:T(8,128)(2,1)}, u32[]{:S(2)}, u32[]{:S(2)}) async-start(bf16[8,64,2,256]{3,1,2,0:T(8,128)(2,1)} %copy.18), calls=%async_computation | async-start | bytes 1048576 | tf_op jit(solution)/shard_map/all_to_all | solution.py:245
  196.0 2.3 constant_dynamic-update-slice_fusion.1
  198.3 2.4 constant_dynamic-update-slice_fusion
  200.8 4.8 %all-to-all-done = bf16[8,64,2,256]{3,1,2,0:T(8,128)(2,1)} async-done(((bf16[8,64,2,256]{3,1,2,0:T(8,128)(2,1)}), bf16[8,64,2,256]{3,1,2,0:T(8,128)(2,1)}, u32[]{:S(2)}, u32[]{:S(2)}) %all-to-all-start) | async-done | bytes 524320 | tf_op jit(solution)/shard_map/all_to_all | solution.py:245
  205.6 2.4 gather_fusion
  208.0 1.2 select_bitcast_fusion
  209.6 4.8 %multiply_reduce_fusion = (f32[128]{0:T(128)S(1)}, f32[128,2048]{1,0:T(8,128)S(1)}) fusion(bf16[128,2048]{1,0:T(8,128)(2,1)S(1)} %bitcast.46, bf16[2048,2048]{1,0:T(8,128)(2,1)} %constant_dynamic-update-slice_fusion, bf16[128,2048]{1,0:T(8,128)(2,1)S(1)} %copy-done.2), kind=kOutput, calls=%fused_computation.23 | convolution fusion | flops 1074790272 | bytes 10486272 | tf_op jit(solution)/shard_map/dot_general | solution.py:250
  215.4 1.5 convolution_convert_fusion.1
  216.9 2.5 all_to_all.20
  219.4 25.6 %all_to_all.29 = bf16[128,2,2048]{2,1,0:T(2,128)(2,1)} all-to-all(bf16[128,2,2048]{2,1,0:T(2,128)(2,1)} %all_to_all.20), channel_id=1, replica_groups=mesh['expert'=16,'head'=8] {'expert','head'}, dimensions={0} | all-to-all | bytes 2097152 | tf_op jit(solution)/shard_map/all_to_all | solution.py:275
  245.0 2.2 all_to_all.22
  247.3 1.2 collective-permute-start.7
  248.4 1.3 constant_dynamic-update-slice_fusion.9
  249.7 1.2 collective-permute-done.7
  251.0 1.3 copy-done.3
  252.3 2.8 fusion.13
  255.2 7.6 %convolution_convert_fusion = bf16[512,2048]{1,0:T(8,128)(2,1)} fusion(bf16[1,704,2048]{2,1,0:T(8,128)(2,1)S(1)} %copy-done, f32[704,512]{1,0:T(8,128)} %fusion.13, bf16[512,2048]{1,0:T(8,128)(2,1)} %copy-done.3, bf16[1,704,2048]{2,1,0:T(8,128)(2,1)} %param.19), kind=kOutput, calls=%fused_computation.1 | convolution fusion | flops 2956001280 | bytes 11403264 | tf_op jit(solution)/shard_map/dot_general | solution.py:188
  262.8 1.3 slice.11
  264.6 2.3 collective-permute-done.8
  266.9 2.6 add_convert_fusion
  269.4 2.5 all_to_all.23
  272.0 24.1 %all_to_all.30 = bf16[128,2,2048]{2,1,0:T(2,128)(2,1)} all-to-all(bf16[128,2,2048]{2,1,0:T(2,128)(2,1)} %all_to_all.23), channel_id=1, replica_groups=mesh['expert'=16,'head'=8] {'expert','head'}, dimensions={0} | all-to-all | bytes 2097152 | tf_op jit(solution)/shard_map/all_to_all | solution.py:283
  296.1 2.2 all_to_all.25
  298.3 1.9 fusion.5
  300.2 1.1 reshape.113
  (40 shorter events, 6.2 us)
Async XLA Ops:
  6.5 248.6 %copy-start = (bf16[1,704,2048]{2,1,0:T(8,128)(2,1)S(1)}, bf16[1,704,2048]{2,1,0:T(8,128)(2,1)}, u32[]{:S(2)}) copy-start(bf16[1,704,2048]{2,1,0:T(8,128)(2,1)} %param.20) | copy-start | bytes 8650756
  6.5 150.9 %all-gather.2.cloned.1.call-start = ((), (), s32[]{:S(2)}) async-start(), calls=%async_computation.3 | async-start | bytes 17825792 | tf_op jit(solution)/shard_map/all_gather | solution.py:229
  46.2 12.8 %copy-start.5 = (s32[64,2]{0,1:T(2,128)S(1)}, s32[64,2]{0,1:T(2,128)}, u32[]{:S(2)}) copy-start(s32[64,2]{0,1:T(2,128)} %param.23) | copy-start | bytes 1540
  46.2 12.8 %copy-start.6 = (s32[64,2]{0,1:T(2,128)S(1)}, s32[64,2]{0,1:T(2,128)}, u32[]{:S(2)}) copy-start(s32[64,2]{0,1:T(2,128)} %param.22) | copy-start | bytes 1540
  46.2 12.8 %copy-start.8 = (s32[2]{0:T(128)S(1)}, s32[2]{0:T(128)}, u32[]{:S(2)}) copy-start(s32[2]{0:T(128)} %param.21) | copy-start | bytes 28
  46.2 23.0 %collective-permute-start = (bf16[256,2048]{1,0:T(8,128)(2,1)}, bf16[256,2048]{1,0:T(8,128)(2,1)}, u32[]{:S(2)}, u32[]{:S(2)}) collective-permute-start(bf16[256,2048]{1,0:T(8,128)(2,1)} %param.16), channel_id=1, source_target_pairs={{0,1},{1,2},{2,3},{3,4},{4,5},{5,6},{6,7},{7,0},{8,9},{9,10},{10,1... | collective-permute-start | bytes 3145736 | tf_op jit(solution)/shard_map/ppermute | solution.py:240
  46.9 47.5 %collective-permute-start.1 = (bf16[256,2048]{1,0:T(8,128)(2,1)}, bf16[256,2048]{1,0:T(8,128)(2,1)}, u32[]{:S(2)}, u32[]{:S(2)}) collective-permute-start(bf16[256,2048]{1,0:T(8,128)(2,1)} %param.16), channel_id=1, source_target_pairs={{0,2},{1,3},{2,4},{3,5},{4,6},{5,7},{6,0},{7,1},{8,10},{9,11},{10,... | collective-permute-start | bytes 3145736 | tf_op jit(solution)/shard_map/ppermute | solution.py:240
  47.7 66.5 %collective-permute-start.2 = (bf16[256,2048]{1,0:T(8,128)(2,1)}, bf16[256,2048]{1,0:T(8,128)(2,1)}, u32[]{:S(2)}, u32[]{:S(2)}) collective-permute-start(bf16[256,2048]{1,0:T(8,128)(2,1)} %param.16), channel_id=1, source_target_pairs={{0,3},{1,4},{2,5},{3,6},{4,7},{5,0},{6,1},{7,2},{8,11},{9,12},{10,... | collective-permute-start | bytes 3145736 | tf_op jit(solution)/shard_map/ppermute | solution.py:240
  49.4 90.1 %collective-permute-start.3 = (bf16[256,2048]{1,0:T(8,128)(2,1)}, bf16[256,2048]{1,0:T(8,128)(2,1)}, u32[]{:S(2)}, u32[]{:S(2)}) collective-permute-start(bf16[256,2048]{1,0:T(8,128)(2,1)} %param.16), channel_id=1, source_target_pairs={{0,4},{1,5},{2,6},{3,7},{4,0},{5,1},{6,2},{7,3},{8,12},{9,13},{10,... | collective-permute-start | bytes 3145736 | tf_op jit(solution)/shard_map/ppermute | solution.py:240
  50.6 91.3 %collective-permute-start.4 = (bf16[256,2048]{1,0:T(8,128)(2,1)}, bf16[256,2048]{1,0:T(8,128)(2,1)}, u32[]{:S(2)}, u32[]{:S(2)}) collective-permute-start(bf16[256,2048]{1,0:T(8,128)(2,1)} %param.16), channel_id=1, source_target_pairs={{0,5},{1,6},{2,7},{3,0},{4,1},{5,2},{6,3},{7,4},{8,13},{9,14},{10,... | collective-permute-start | bytes 3145736 | tf_op jit(solution)/shard_map/ppermute | solution.py:240
  56.5 4.1 %copy-start.4 = (bf16[2048]{0:T(1024)(128)(2,1)S(1)}, bf16[2048]{0:T(1024)(128)(2,1)}, u32[]{:S(2)}) copy-start(bf16[2048]{0:T(1024)(128)(2,1)} %param.17) | copy-start | bytes 12292
  69.2 126.8 %collective-permute-start.5 = (bf16[256,2048]{1,0:T(8,128)(2,1)}, bf16[256,2048]{1,0:T(8,128)(2,1)}, u32[]{:S(2)}, u32[]{:S(2)}) collective-permute-start(bf16[256,2048]{1,0:T(8,128)(2,1)} %param.16), channel_id=1, source_target_pairs={{0,6},{1,7},{2,0},{3,1},{4,2},{5,3},{6,4},{7,5},{8,14},{9,15},{10,... | collective-permute-start | bytes 3145736 | tf_op jit(solution)/shard_map/ppermute | solution.py:240
  94.4 103.9 %collective-permute-start.6 = (bf16[256,2048]{1,0:T(8,128)(2,1)}, bf16[256,2048]{1,0:T(8,128)(2,1)}, u32[]{:S(2)}, u32[]{:S(2)}) collective-permute-start(bf16[256,2048]{1,0:T(8,128)(2,1)} %param.16), channel_id=1, source_target_pairs={{0,7},{1,0},{2,1},{3,2},{4,3},{5,4},{6,5},{7,6},{8,15},{9,8},{10,9... | collective-permute-start | bytes 3145736 | tf_op jit(solution)/shard_map/ppermute | solution.py:240
  190.9 14.7 %all-to-all-start = ((bf16[8,64,2,256]{3,1,2,0:T(8,128)(2,1)}), bf16[8,64,2,256]{3,1,2,0:T(8,128)(2,1)}, u32[]{:S(2)}, u32[]{:S(2)}) async-start(bf16[8,64,2,256]{3,1,2,0:T(8,128)(2,1)} %copy.18), calls=%async_computation | async-start | bytes 1048576 | tf_op jit(solution)/shard_map/all_to_all | solution.py:245
  198.3 11.3 %copy-start.2 = (bf16[128,2048]{1,0:T(8,128)(2,1)S(1)}, bf16[128,2048]{1,0:T(8,128)(2,1)}, u32[]{:S(2)}) copy-start(bf16[128,2048]{1,0:T(8,128)(2,1)} %reshape.106.x_ref) | copy-start | bytes 1572868
  214.4 1.0 copy-start.1
  247.3 5.1 %copy-start.7 = (bf16[1,704,2048]{2,1,0:T(8,128)(2,1)S(1)}, bf16[1,704,2048]{2,1,0:T(8,128)(2,1)}, u32[]{:S(2)}) copy-start(bf16[1,704,2048]{2,1,0:T(8,128)(2,1)} %param.18) | copy-start | bytes 8650756
  247.3 3.7 %collective-permute-start.7 = (bf16[256,2048]{1,0:T(8,128)(2,1)}, bf16[256,2048]{1,0:T(8,128)(2,1)S(1)}, u32[]{:S(2)}, u32[]{:S(2)}) collective-permute-start(bf16[256,2048]{1,0:T(8,128)(2,1)} %all_to_all.22), channel_id=1, source_target_pairs={{0,1},{1,0},{2,3},{3,2},{4,5},{5,4},{6,7},{7,6},{8,9},{9,8},{10,11... | collective-permute-start | bytes 3145736 | tf_op jit(solution)/shard_map/ppermute | solution.py:277
  251.0 1.3 copy-start.3
  264.1 2.7 collective-permute-start.8
Sparse Core Ops, SparseCore 0:
  46.3 111.0 all-gather.1
